TPU v7x, 256 devices: a whole 4x4x8 slice. The times are simulated.
256 devices in a mesh: dp: 64 (over z, x, y_hi), tensor: 4 (over y_lo, core).
Axes of the slice: x: 4, y: 4 (y_hi: 2, y_lo: 2; y = y_hi * 2 + y_lo), z: 8, core: 2. Of those that a mesh axis runs over, the one named last changes fastest.
Arguments:
- inputs: float32 [64, 197, 768], P('dp')
- cotangent: float32 [64, 197, 768], P('dp'), may hold values from -6 to 6
- norm_gains: float32 [2, 768], P(None, 'dp'), may hold values from 0.5 to 1.5
- attn_mats: float32 [4, 768, 768], P(None, 'dp', 'tensor')
- router: float32 [768, 3], P('dp'), may hold values from -0.4375 to 0.4375
- expert_in: float32 [3, 768, 1536], P(None, 'dp', 'tensor'), may hold values from -0.21875 to 0.21875
- expert_out: float32 [3, 768, 1536], P(None, 'dp', 'tensor'), may hold values from -0.3125 to 0.3125
- moment_gains: float32 [2, 768], P(None, 'dp'), may hold values from -128 to 128
- moment_attn: float32 [4, 768, 768], P(None, 'dp', 'tensor'), may hold values from -32 to 32
- moment_router: float32 [768, 3], P('dp'), may hold values from -320 to 320
- moment_in: float32 [3, 768, 1536], P(None, 'dp', 'tensor'), may hold values from -32 to 32
- moment_out: float32 [3, 768, 1536], P(None, 'dp', 'tensor'), may hold values from -32 to 32
- routes: int32 [64, 197, 2], P('dp'), may hold values from 0 to 2, all different within a row; in each aligned block of 197 rows (0 to 196, 197 to 393, ..., all dimensions but the last counted through in order) at most 197 rows name the same one
Outputs:
- output: float32 [64, 197, 768], P('dp')
- grad_inputs: float32 [64, 197, 768], P('dp')
- grad_gains: float32 [2, 768], P(None, 'dp')
- grad_attn: float32 [4, 768, 768], P(None, 'dp', 'tensor')
- grad_router: float32 [768, 3], P('dp')
- grad_in: float32 [3, 768, 1536], P(None, 'dp', 'tensor')
- grad_out: float32 [3, 768, 1536], P(None, 'dp', 'tensor')
- gains_new: float32 [2, 768], P(None, 'dp')
- attn_new: float32 [4, 768, 768], P(None, 'dp', 'tensor')
- router_new: float32 [768, 3], P('dp')
- in_new: float32 [3, 768, 1536], P(None, 'dp', 'tensor')
- out_new: float32 [3, 768, 1536], P(None, 'dp', 'tensor')
- moment_gains_new: float32 [2, 768], P(None, 'dp')
- moment_attn_new: float32 [4, 768, 768], P(None, 'dp', 'tensor')
- moment_router_new: float32 [768, 3], P('dp')
- moment_in_new: float32 [3, 768, 1536], P(None, 'dp', 'tensor')
- moment_out_new: float32 [3, 768, 1536], P(None, 'dp', 'tensor')
Inputs may be any that keep to these rules, and one draw needn't show every extreme that they name: `routes`: in the rows of one index of dp no expert is named by more than 197 of them, a bound that some block reaches; a row's two experts differ.
All inputs are finite; a program needn't handle non-finite values.
Results may differ from a plain program's by a relative error of at most 0.025.
The roundings to bfloat16 on the way count: a program that leaves them out, or rounds other values in their place, can miss the bound.
Values may be sent and summed in bfloat16 or wider, within the bound.
A program may use at most 128 MiB of HBM per device.

v0:
```python
import math

import jax
import jax.numpy as jnp
import numpy as np
from jax import lax
from jax.sharding import PartitionSpec as P

HEAD_DIM = 64
EF = 3
NS_ITERS = 3
CAP = 197


EPSILON = 1e-06
MOMENTUM = 0.9
MUON_RATE = 0.5
SMALL_RATE = 0.5
NEWTON_A = 3.4445
NEWTON_B = -4.775
NEWTON_C = 2.0315
ROOT_HALF = 0.7071067811865476
INV_ROOT_TAU = 0.3989422804014327


def for_sending(value):
    return jax.tree.map(lambda a: a.astype(jnp.bfloat16) if a.dtype == jnp.float32 else a, value)


def round_half(operand):
    return operand.astype(jnp.bfloat16)


def settle(operand):
    return lax.optimization_barrier(operand.astype(jnp.bfloat16))


def to_single(operand):
    return operand.astype(jnp.float32)


def contract_rows(left_mat, right_mat):
    return lax.dot_general(
        left_mat, right_mat, (((0,), (0,)), ((), ())), preferred_element_type=jnp.float32
    )


def contract_cols(left_mat, right_mat):
    return lax.dot_general(
        left_mat, right_mat, (((1,), (1,)), ((), ())), preferred_element_type=jnp.float32
    )


def fold_sources(received, source_count):
    return jnp.sum(
        received.reshape((source_count, received.shape[0] // source_count) + received.shape[1:]),
        axis=0,
    )


def norm_forward(row_data, gain_row):
    center = row_data - jnp.mean(row_data, axis=-1, keepdims=True)
    inv_std = lax.rsqrt(jnp.mean(center * center, axis=-1, keepdims=True) + EPSILON)
    normal = center * inv_std
    return (normal, inv_std, round_half(normal * gain_row))


def norm_backward(grad_result, normal, inv_std, gain_row):
    scaled = grad_result * gain_row
    grad_data = inv_std * (
        scaled
        - jnp.mean(scaled, axis=-1, keepdims=True)
        - normal * jnp.mean(scaled * normal, axis=-1, keepdims=True)
    )
    return (grad_data, jnp.sum(grad_result * normal, axis=0))


def gelu_value(pre_act):
    return 0.5 * pre_act * (1.0 + lax.erf(pre_act * ROOT_HALF))


def gelu_slope(pre_act):
    return 0.5 * (1.0 + lax.erf(pre_act * ROOT_HALF)) + pre_act * INV_ROOT_TAU * jnp.exp(
        -0.5 * pre_act * pre_act
    )


def slot_tables(picked, experts, capacity):
    flat_picks = picked.reshape(-1)
    assign_count = flat_picks.shape[0]
    one_hot = (flat_picks[:, None] == jnp.arange(experts, dtype=jnp.int32)[None, :]).astype(
        jnp.int32
    )
    before = jnp.cumsum(one_hot, axis=0) - one_hot
    slot_place = jnp.sum(before * one_hot, axis=1)
    target = flat_picks * capacity + slot_place
    slot_owner = (
        jnp.full((experts * capacity,), assign_count, jnp.int32)
        .at[target]
        .set(jnp.arange(assign_count, dtype=jnp.int32))
    )
    return (target, slot_owner)


def score_table(queries, key_rows):
    return jnp.einsum("bqhd,bkhd->bhqk", queries, key_rows, preferred_element_type=jnp.float32) * (
        1.0 / math.sqrt(HEAD_DIM)
    )


def attention_forward(normed, mats_half, image_count, seq_len):
    head_count = mats_half.shape[2] // HEAD_DIM

    def project(which_mat):
        return round_half(
            jnp.dot(normed, mats_half[which_mat], preferred_element_type=jnp.float32)
        ).reshape(image_count, seq_len, head_count, HEAD_DIM)

    queries = project(0)
    key_rows = project(1)
    value_rows = project(2)
    scores = score_table(queries, key_rows)
    row_peak = jnp.max(scores, axis=-1, keepdims=True)
    log_total = row_peak + jnp.log(jnp.sum(jnp.exp(scores - row_peak), axis=-1, keepdims=True))
    prob_half = round_half(jnp.exp(scores - log_total))
    attn_rows = round_half(
        jnp.einsum("bhqk,bkhd->bqhd", prob_half, value_rows, preferred_element_type=jnp.float32)
    )
    return (
        queries,
        key_rows,
        value_rows,
        log_total,
        attn_rows.reshape(image_count * seq_len, head_count * HEAD_DIM),
    )


def attention_backward(grad_attn_rows, queries, key_rows, value_rows, log_total):
    image_count, seq_len, head_count, head_size = queries.shape
    grad_heads = grad_attn_rows.reshape(image_count, seq_len, head_count, head_size)
    prob_full = jnp.exp(score_table(queries, key_rows) - log_total)
    prob_half = round_half(prob_full)
    grad_prob = jnp.einsum(
        "bqhd,bkhd->bhqk", grad_heads, value_rows, preferred_element_type=jnp.float32
    )
    grad_values = round_half(
        jnp.einsum("bhqk,bqhd->bkhd", prob_half, grad_heads, preferred_element_type=jnp.float32)
    )
    spread = jnp.sum(prob_full * grad_prob, axis=-1, keepdims=True)
    grad_scores = round_half(prob_full * (grad_prob - spread) * (1.0 / math.sqrt(HEAD_DIM)))
    grad_queries = round_half(
        jnp.einsum("bhqk,bkhd->bqhd", grad_scores, key_rows, preferred_element_type=jnp.float32)
    )
    grad_keys = round_half(
        jnp.einsum("bhqk,bqhd->bkhd", grad_scores, queries, preferred_element_type=jnp.float32)
    )
    row_total = image_count * seq_len
    full_width = head_count * head_size
    return (
        grad_queries.reshape(row_total, full_width),
        grad_keys.reshape(row_total, full_width),
        grad_values.reshape(row_total, full_width),
    )


def orthogonalize(matrix):
    current = settle(matrix * lax.rsqrt(jnp.sum(matrix * matrix) + EPSILON))
    for iteration in range(NS_ITERS):
        gram_mat = settle(contract_rows(current, current))
        square = jnp.dot(gram_mat, gram_mat, preferred_element_type=jnp.float32)
        poly_mat = round_half(NEWTON_B * to_single(gram_mat) + NEWTON_C * square)
        current = settle(
            NEWTON_A * to_single(current)
            + jnp.dot(current, poly_mat, preferred_element_type=jnp.float32)
        )
    return current


def orthogonalize_attention(block_mat):
    rows_all, slot_width = block_mat.shape
    sub_blocks = jnp.transpose(block_mat.reshape(rows_all, 2, slot_width // 2), (1, 0, 2))
    solved = jnp.stack([orthogonalize(sub_blocks[which_mat]) for which_mat in range(2)])
    return jnp.transpose(solved, (1, 0, 2)).reshape(rows_all, slot_width)


def empty_block(block_mat):
    return jnp.zeros(block_mat.shape, jnp.bfloat16)


def shards(
    inputs,
    cotangent,
    norm_gains,
    attn_mats,
    router,
    expert_in,
    expert_out,
    moment_gains,
    moment_attn,
    moment_router,
    moment_in,
    moment_out,
    routes,
):
    image_count, seq_len, model_width = inputs.shape
    dp_count = lax.axis_size("dp")
    row_count = image_count * seq_len
    gains_half, attn_half, router_half, in_half, out_half = (
        lax.all_gather(round_half(norm_gains), "dp", axis=1, tiled=True),
        lax.all_gather(round_half(attn_mats), "dp", axis=1, tiled=True),
        lax.all_gather(round_half(router), "dp", axis=0, tiled=True),
        lax.all_gather(round_half(expert_in), "dp", axis=1, tiled=True),
        lax.all_gather(round_half(expert_out), "dp", axis=1, tiled=True),
    )
    gain_one = to_single(gains_half[0])
    gain_two = to_single(gains_half[1])
    row_in = inputs.reshape(row_count, model_width)
    normal_one, inv_one, normed_one = norm_forward(row_in, gain_one)
    queries, key_rows, value_rows, log_total, attn_rows = attention_forward(
        normed_one, attn_half, image_count, seq_len
    )
    attn_part = contract_cols(attn_rows, attn_half[3])
    attn_full = lax.psum(attn_part.astype(jnp.bfloat16), "tensor").astype(jnp.float32)
    middle = row_in + attn_full
    normal_two, inv_two, normed_two = norm_forward(middle, gain_two)
    picked = routes.reshape(row_count, 2)
    target, slot_owner = slot_tables(picked, EF, CAP)
    logits = jnp.dot(normed_two, router_half, preferred_element_type=jnp.float32)
    chosen = jnp.take_along_axis(logits, picked, axis=1)
    gate_vals = jax.nn.sigmoid(chosen - chosen[:, ::-1])
    padded = jnp.concatenate([normed_two, jnp.zeros((1, model_width), jnp.bfloat16)], axis=0)
    dispatched = padded[slot_owner // 2].reshape(EF, CAP, model_width)
    pre_act = jnp.einsum("ecd,edf->ecf", dispatched, in_half, preferred_element_type=jnp.float32)
    hidden = round_half(gelu_value(pre_act))
    expert_rows = jnp.einsum("ecf,edf->ecd", hidden, out_half, preferred_element_type=jnp.float32)
    per_choice = expert_rows.reshape(EF * CAP, model_width)[target].reshape(
        row_count, 2, model_width
    )
    moe_part = jnp.sum(gate_vals[:, :, None] * per_choice, axis=1)
    moe_full = lax.psum(moe_part.astype(jnp.bfloat16), "tensor").astype(jnp.float32)
    output_rows = middle + moe_full
    grad_rows = cotangent.reshape(row_count, model_width)
    grad_choice_part = jnp.sum(grad_rows[:, None, :] * per_choice, axis=2)
    gate_flat = jnp.concatenate([gate_vals.reshape(-1), jnp.zeros((1,), jnp.float32)])
    grad_pad = jnp.concatenate([grad_rows, jnp.zeros((1, model_width), jnp.float32)], axis=0)
    grad_expert = round_half(gate_flat[slot_owner][:, None] * grad_pad[slot_owner // 2]).reshape(
        EF, CAP, model_width
    )
    grad_hidden = jnp.einsum(
        "ecd,edf->ecf", grad_expert, out_half, preferred_element_type=jnp.float32
    )
    grad_pre = round_half(grad_hidden * gelu_slope(pre_act))
    grad_dispatch = jnp.einsum(
        "ecf,edf->ecd", grad_pre, in_half, preferred_element_type=jnp.float32
    )
    grad_normed_part = jnp.sum(
        grad_dispatch.reshape(EF * CAP, model_width)[target].reshape(row_count, 2, model_width),
        axis=1,
    )
    grad_in = jnp.einsum("ecd,ecf->edf", dispatched, grad_pre, preferred_element_type=jnp.float32)
    grad_out = jnp.einsum("ecd,ecf->edf", grad_expert, hidden, preferred_element_type=jnp.float32)
    grad_choice, grad_normed_moe = (
        lax.psum(grad_choice_part.astype(jnp.bfloat16), "tensor").astype(jnp.float32),
        lax.psum(grad_normed_part.astype(jnp.bfloat16), "tensor").astype(jnp.float32),
    )
    gate_prod = gate_vals[:, 0] * gate_vals[:, 1]
    grad_first = (grad_choice[:, 0] - grad_choice[:, 1]) * gate_prod
    grad_picked = jnp.stack([grad_first, -grad_first], axis=1)
    one_hot = (picked[:, :, None] == jnp.arange(EF, dtype=jnp.int32)[None, None, :]).astype(
        jnp.float32
    )
    grad_logits = round_half(jnp.sum(grad_picked[:, :, None] * one_hot, axis=1))
    grad_router = contract_rows(normed_two, grad_logits)
    grad_normed_two = grad_normed_moe + contract_cols(grad_logits, router_half)
    grad_mid_norm, grad_gain_two = norm_backward(grad_normed_two, normal_two, inv_two, gain_two)
    grad_middle = grad_rows + grad_mid_norm
    grad_mid_half = round_half(grad_middle)
    grad_attn_rows = round_half(
        jnp.dot(grad_mid_half, attn_half[3], preferred_element_type=jnp.float32)
    )
    grad_proj_out = contract_rows(grad_mid_half, attn_rows)
    grad_queries, grad_keys, grad_values = attention_backward(
        grad_attn_rows, queries, key_rows, value_rows, log_total
    )
    grad_attn = jnp.stack(
        [
            contract_rows(normed_one, grad_queries),
            contract_rows(normed_one, grad_keys),
            contract_rows(normed_one, grad_values),
            grad_proj_out,
        ]
    )
    grad_normed_one_part = (
        contract_cols(grad_queries, attn_half[0])
        + contract_cols(grad_keys, attn_half[1])
        + contract_cols(grad_values, attn_half[2])
    )
    grad_normed_one = lax.psum(grad_normed_one_part.astype(jnp.bfloat16), "tensor").astype(
        jnp.float32
    )
    grad_in_norm, grad_gain_one = norm_backward(grad_normed_one, normal_one, inv_one, gain_one)
    grad_inputs_rows = grad_middle + grad_in_norm
    gains_cols = jnp.stack([grad_gain_one, grad_gain_two], axis=1)
    small_cols = jnp.concatenate([gains_cols, grad_router], axis=1)
    got_attn, got_in, got_out, got_small = (
        lax.all_to_all(
            grad_attn.astype(jnp.bfloat16), "dp", split_axis=1, concat_axis=0, tiled=True
        ).astype(grad_attn.dtype),
        lax.all_to_all(
            grad_in.astype(jnp.bfloat16), "dp", split_axis=1, concat_axis=0, tiled=True
        ).astype(grad_in.dtype),
        lax.all_to_all(
            grad_out.astype(jnp.bfloat16), "dp", split_axis=1, concat_axis=0, tiled=True
        ).astype(grad_out.dtype),
        lax.all_to_all(
            small_cols[None].astype(jnp.bfloat16), "dp", split_axis=1, concat_axis=0, tiled=True
        ).astype(jnp.float32),
    )
    sum_attn = fold_sources(got_attn, dp_count)
    sum_in = fold_sources(got_in, dp_count)
    sum_out = fold_sources(got_out, dp_count)
    sum_small = fold_sources(got_small, dp_count)[0]
    sum_gains = sum_small[:, :2].T
    sum_router = sum_small[:, 2:]
    small_step = SMALL_RATE / math.sqrt(image_count * dp_count * seq_len)
    moment_gains_new = MOMENTUM * moment_gains + sum_gains
    moment_attn_new = MOMENTUM * moment_attn + sum_attn
    moment_router_new = MOMENTUM * moment_router + sum_router
    moment_in_new = MOMENTUM * moment_in + sum_in
    moment_out_new = MOMENTUM * moment_out + sum_out
    gains_new = norm_gains - small_step * moment_gains_new
    router_new = router - small_step * moment_router_new
    look_attn = sum_attn + MOMENTUM * moment_attn_new
    look_in = sum_in + MOMENTUM * moment_in_new
    look_out = sum_out + MOMENTUM * moment_out_new
    shard_rows = look_in.shape[1]
    slot_width = look_in.shape[2]
    blocks = 2 * EF + 2
    per_owner = -(-blocks // dp_count)
    slot_count = dp_count * per_owner
    slot_list = list(range(blocks))
    block_list = [
        slot_list.index(slot_number) if slot_number in slot_list else blocks
        for slot_number in range(slot_count)
    ]
    slot_of_block = np.array(slot_list)
    block_of_slot = np.array(block_list)
    kind_of_slot = np.where(block_of_slot < 2, 0, np.where(block_of_slot < blocks, 1, 2))
    attn_slots = jnp.transpose(
        jnp.transpose(look_attn, (1, 0, 2)).reshape(shard_rows, 2, slot_width), (1, 0, 2)
    )
    stacked = jnp.concatenate(
        [attn_slots, look_in, look_out, jnp.zeros((1, shard_rows, slot_width), jnp.float32)], axis=0
    )
    outgoing = jnp.take(stacked, jnp.asarray(block_of_slot, dtype=jnp.int32), axis=0)
    arrived = lax.all_to_all(
        for_sending(outgoing), "dp", split_axis=0, concat_axis=1, tiled=True
    ).astype(outgoing.dtype)
    own_index = lax.axis_index("dp")
    kind_table = jnp.asarray(kind_of_slot, dtype=jnp.int32)
    kind_now = kind_table[own_index * per_owner + 0]
    results = [
        lax.switch(kind_now, [orthogonalize_attention, orthogonalize, empty_block], arrived[0])
    ]
    finished = jnp.stack(results)
    returned = lax.all_to_all(
        for_sending(finished), "dp", split_axis=1, concat_axis=0, tiled=True
    ).astype(finished.dtype)
    updates = to_single(jnp.take(returned, jnp.asarray(slot_of_block, dtype=jnp.int32), axis=0))
    update_attn = jnp.transpose(
        jnp.transpose(updates[0:2], (1, 0, 2)).reshape(shard_rows, 4, slot_width // 2), (1, 0, 2)
    )
    attn_new = attn_mats - MUON_RATE * update_attn
    in_new = expert_in - MUON_RATE * updates[2 : EF + 2]
    out_new = expert_out - MUON_RATE * updates[EF + 2 : 2 * EF + 2]
    output = output_rows.reshape(image_count, seq_len, model_width)
    grad_inputs = grad_inputs_rows.reshape(image_count, seq_len, model_width)
    return (
        output,
        grad_inputs,
        sum_gains,
        sum_attn,
        sum_router,
        sum_in,
        sum_out,
        gains_new,
        attn_new,
        router_new,
        in_new,
        out_new,
        moment_gains_new,
        moment_attn_new,
        moment_router_new,
        moment_in_new,
        moment_out_new,
    )


def solution(mesh):
    return jax.shard_map(
        shards,
        mesh=mesh,
        in_specs=(
            P("dp", None, None),
            P("dp", None, None),
            P(None, "dp"),
            P(None, "dp", "tensor"),
            P("dp", None),
            P(None, "dp", "tensor"),
            P(None, "dp", "tensor"),
            P(None, "dp"),
            P(None, "dp", "tensor"),
            P("dp", None),
            P(None, "dp", "tensor"),
            P(None, "dp", "tensor"),
            P("dp", None, None),
        ),
        out_specs=(
            P("dp", None, None),
            P("dp", None, None),
            P(None, "dp"),
            P(None, "dp", "tensor"),
            P("dp", None),
            P(None, "dp", "tensor"),
            P(None, "dp", "tensor"),
            P(None, "dp"),
            P(None, "dp", "tensor"),
            P("dp", None),
            P(None, "dp", "tensor"),
            P(None, "dp", "tensor"),
            P(None, "dp"),
            P(None, "dp", "tensor"),
            P("dp", None),
            P(None, "dp", "tensor"),
            P(None, "dp", "tensor"),
        ),
        check_vma=False,
    )
```

profile of v0, /device:TPU:94, one launch (start us, length us, event | category | flops | bytes accessed | tf_op | source)
XLA Modules:
  0.0 915.7 jit_solution(14366641946834359180)
XLA Ops:
  9.5 159.8 %all-gather = bf16[64,12,2]{1,2,0:T(2,128)(2,1)S(1)} all-gather(bf16[1,12,2]{1,2,0:T(2,128)(2,1)S(1)} %convert_bitcast_fusion.1), channel_id=1, replica_groups=mesh['dp'=64,'tensor'=4] {'dp'}, dimensions={0}, use_global_device_ids=true | all-gather | bytes 3120 | tf_op jit(solution)/shard_map/all_gather | solution.py:209
  173.9 7.0 fusion.172
  193.2 177.8 %all-gather.1 = bf16[64,12,3]{1,2,0:T(4,128)(2,1)S(1)} all-gather(bf16[1,12,3]{1,2,0:T(4,128)(2,1)S(1)} %convert_bitcast_fusion), channel_id=1, replica_groups=mesh['dp'=64,'tensor'=4] {'dp'}, dimensions={0}, use_global_device_ids=true | all-gather | bytes 4680 | tf_op jit(solution)/shard_map/all_gather | solution.py:211
  386.4 6.0 gather_fusion.7
  393.2 4.3 gather_fusion.2
  400.5 87.9 %all-gather.10.cloned.1.call-done = bf16[3,768,384]{2,0,1:T(4,128)(2,1)} async-done(((bf16[3,12,384]{2,0,1:T(4,128)(2,1)}), bf16[3,768,384]{2,0,1:T(4,128)(2,1)}) %all-gather.10.cloned.1.call-update) | async-done | bytes 1769488 | tf_op jit(solution)/shard_map/all_gather | solution.py:213
  499.5 4.7 multiply_reduce_fusion.2
  504.2 11.6 %psum.38 = bf16[197,2]{1,0:T(8,128)(2,1)S(1)} all-reduce(bf16[197,2]{1,0:T(8,128)(2,1)} %get-tuple-element.133), channel_id=1, replica_groups=mesh['dp'=64,'tensor'=4] {'tensor'}, use_global_device_ids=true, to_apply=%region_16.17 | all-reduce | flops 394 | bytes 1576 | tf_op jit(solution)/shard_map/psum | solution.py:263
  531.4 40.0 %all-reduce.10.cloned.1.call-done = bf16[197,768]{1,0:T(8,128)(2,1)} async-done(((bf16[197,768]{1,0:T(8,128)(2,1)}), bf16[197,768]{1,0:T(8,128)(2,1)}) %all-reduce.10.cloned.1.call-update) | async-done | bytes 302608 | tf_op jit(solution)/shard_map/psum | solution.py:264
  585.7 13.1 %all-to-all-start.1 = ((bf16[4,768,192]{2,0,1:T(4,128)(2,1)}), bf16[4,768,192]{2,0,1:T(4,128)(2,1)}, u32[]{:S(2)}, u32[]{:S(2)}) async-start(bf16[4,768,192]{2,0,1:T(4,128)(2,1)} %copy.201), calls=%async_computation.1 | async-start | bytes 3145728 | tf_op jit(solution)/shard_map/all_to_all | solution.py:306
  603.9 33.2 %all-to-all-done.1 = bf16[4,768,192]{2,0,1:T(4,128)(2,1)} async-done(((bf16[4,768,192]{2,0,1:T(4,128)(2,1)}), bf16[4,768,192]{2,0,1:T(4,128)(2,1)}, u32[]{:S(2)}, u32[]{:S(2)}) %all-to-all-start.1) | async-done | bytes 1179680 | tf_op jit(solution)/shard_map/all_to_all | solution.py:306
  637.1 10.8 %all-to-all-start.2 = ((bf16[3,768,384]{2,0,1:T(4,128)(2,1)}), bf16[3,768,384]{2,0,1:T(4,128)(2,1)}, u32[]{:S(2)}, u32[]{:S(2)}) async-start(bf16[3,768,384]{2,0,1:T(4,128)(2,1)} %copy.202), calls=%async_computation.2 | async-start | bytes 4718592 | tf_op jit(solution)/shard_map/all_to_all | solution.py:309
  653.5 47.8 %all-to-all-done.2 = bf16[3,768,384]{2,0,1:T(4,128)(2,1)} async-done(((bf16[3,768,384]{2,0,1:T(4,128)(2,1)}), bf16[3,768,384]{2,0,1:T(4,128)(2,1)}, u32[]{:S(2)}, u32[]{:S(2)}) %all-to-all-start.2) | async-done | bytes 1769504 | tf_op jit(solution)/shard_map/all_to_all | solution.py:309
  701.3 10.7 %all-to-all-start.3 = ((bf16[3,768,384]{2,0,1:T(4,128)(2,1)}), bf16[3,768,384]{2,0,1:T(4,128)(2,1)}, u32[]{:S(2)}, u32[]{:S(2)}) async-start(bf16[3,768,384]{2,0,1:T(4,128)(2,1)} %copy.204), calls=%async_computation.3 | async-start | bytes 4718592 | tf_op jit(solution)/shard_map/all_to_all | solution.py:312
  719.8 4.7 reshape.585
  727.1 37.7 %all-to-all-done.3 = bf16[3,768,384]{2,0,1:T(4,128)(2,1)} async-done(((bf16[3,768,384]{2,0,1:T(4,128)(2,1)}), bf16[3,768,384]{2,0,1:T(4,128)(2,1)}, u32[]{:S(2)}, u32[]{:S(2)}) %all-to-all-start.3) | async-done | bytes 1769504 | tf_op jit(solution)/shard_map/all_to_all | solution.py:312
  768.5 4.7 reshape.586
  778.8 10.3 %all-to-all-start.4 = ((bf16[64,12,384]{2,1,0:T(8,128)(2,1)}), bf16[64,12,384]{2,1,0:T(8,128)(2,1)S(1)}, u32[]{:S(2)}, u32[]{:S(2)}) async-start(bf16[64,12,384]{2,1,0:T(8,128)(2,1)} %gather_fusion.5), calls=%async_computation.4 | async-start | bytes 1572864 | tf_op jit(solution)/shard_map/all_to_all | solution.py:356
  795.1 41.7 %all-reduce.12.cloned.1.call-done = (bf16[197,768]{1,0:T(8,128)(2,1)}, bf16[197,768]{1,0:T(8,128)(2,1)}) async-done(((bf16[197,768]{1,0:T(8,128)(2,1)}, bf16[197,768]{1,0:T(8,128)(2,1)}), (bf16[197,768]{1,0:T(8,128)(2,1)}, bf16[197,768]{1,0:T(8,128)(2,1)})) %all-reduce.12.cloned.1.call-update) | async-done | bytes 605200 | tf_op jit(solution)/shard_map/psum | solution.py:240
  839.9 13.0 %all-to-all-start = ((bf16[1,768,5]{2,0,1:T(2,128)(2,1)}), bf16[1,768,5]{2,0,1:T(2,128)(2,1)}, u32[]{:S(2)}, u32[]{:S(2)}) async-start(bf16[1,768,5]{2,0,1:T(2,128)(2,1)} %copy.199), calls=%async_computation | async-start | bytes 786432 | tf_op jit(solution)/shard_map/all_to_all | solution.py:315
  853.8 4.8 conditional.1
  860.4 5.1 reduce.29
  868.1 13.3 %all-to-all-start.5 = ((bf16[64,2,2304]{2,1,0:T(2,128)(2,1)}), bf16[64,2,2304]{2,1,0:T(2,128)(2,1)}, u32[]{:S(2)}, u32[]{:S(2)}) async-start(bf16[64,2,2304]{2,1,0:T(2,128)(2,1)} %reshape.673), calls=%async_computation.5 | async-start | bytes 1179648 | tf_op jit(solution)/shard_map/all_to_all | solution.py:366
  887.4 11.1 %all-to-all-done.5 = bf16[64,2,2304]{2,1,0:T(2,128)(2,1)} async-done(((bf16[64,2,2304]{2,1,0:T(2,128)(2,1)}), bf16[64,2,2304]{2,1,0:T(2,128)(2,1)}, u32[]{:S(2)}, u32[]{:S(2)}) %all-to-all-start.5) | async-done | bytes 589856 | tf_op jit(solution)/shard_map/all_to_all | solution.py:366
  (309 shorter events, 138.1 us)
Async XLA Ops:
  7.2 165.6 %copy-start = (f32[1,197,768]{2,0,1:T(1,128)S(1)}, f32[1,197,768]{2,0,1:T(1,128)}, u32[]{:S(2)}) copy-start(f32[1,197,768]{2,0,1:T(1,128)} %param.19) | copy-start | bytes 1815556
  7.2 166.7 %all-gather.6.cloned.1.call-start = ((), (), s32[]{:S(2)}) async-start(), calls=%async_computation.6 | async-start | bytes 1597440 | tf_op jit(solution)/shard_map/all_gather | solution.py:210
  8.7 370.8 %all-reduce.8.cloned.1.call-start = ((), (), s32[]{:S(2)}) async-start(), calls=%async_computation.7 | async-start | bytes 614400 | tf_op jit(solution)/shard_map/psum | solution.py:223
  189.6 208.6 %all-gather.8.cloned.1.call-start = ((), (), s32[]{:S(2)}) async-start(), calls=%async_computation.8 | async-start | bytes 2396160 | tf_op jit(solution)/shard_map/all_gather | solution.py:212
  190.3 298.1 %all-gather.10.cloned.1.call-start = ((), (), s32[]{:S(2)}) async-start(), calls=%async_computation.9 | async-start | bytes 2396160 | tf_op jit(solution)/shard_map/all_gather | solution.py:213
  191.1 380.3 %all-reduce.10.cloned.1.call-start = ((), (), s32[]{:S(2)}) async-start(), calls=%async_computation.10 | async-start | bytes 614400 | tf_op jit(solution)/shard_map/psum | solution.py:264
  193.2 182.2 %copy-start.4 = (f32[1,197,768]{2,1,0:T(8,128)}, f32[1,197,768]{2,1,0:T(8,128)S(1)}, u32[]{:S(2)}) copy-start(f32[1,197,768]{2,1,0:T(8,128)S(1)} %copy.258) | copy-start | bytes 1815556
  379.5 114.5 %copy-start.49 = (s32[1024]{0:T(1024)}, s32[1024]{0:T(1024)S(1)}, u32[]{:S(2)}) copy-start(s32[1024]{0:T(1024)S(1)} %pad_clamp_fusion.3) | copy-start | bytes 12292
  400.5 87.9 %copy-start.7 = (f32[3,197,384]{2,1,0:T(8,128)}, f32[3,197,384]{2,1,0:T(8,128)S(1)}, u32[]{:S(2)}) copy-start(f32[3,197,384]{2,1,0:T(8,128)S(1)} %fusion.92) | copy-start | bytes 2723332
  528.6 42.7 %copy-start.48 = (f32[197]{0:T(256)S(1)}, f32[197]{0:T(256)}, u32[]{:S(2)}) copy-start(f32[197]{0:T(256)} %copy-done.47) | copy-start | bytes 2368
  531.4 43.5 %copy-start.16 = (bf16[1,768,192]{1,2,0:T(8,128)(2,1)S(1)}, bf16[1,768,192]{1,2,0:T(8,128)(2,1)}, u32[]{:S(2)}) copy-start(bf16[1,768,192]{1,2,0:T(8,128)(2,1)} %copy-done.15) | copy-start | bytes 884740
  585.7 51.3 %all-to-all-start.1 = ((bf16[4,768,192]{2,0,1:T(4,128)(2,1)}), bf16[4,768,192]{2,0,1:T(4,128)(2,1)}, u32[]{:S(2)}, u32[]{:S(2)}) async-start(bf16[4,768,192]{2,0,1:T(4,128)(2,1)} %copy.201), calls=%async_computation.1 | async-start | bytes 3145728 | tf_op jit(solution)/shard_map/all_to_all | solution.py:306
  603.9 44.0 %copy-start.53 = (f32[3,197]{1,0:T(4,128)S(1)}, f32[3,197]{1,0:T(4,128)}, u32[]{:S(2)}) copy-start(f32[3,197]{1,0:T(4,128)} %mul.431) | copy-start | bytes 7096
  637.1 64.2 %all-to-all-start.2 = ((bf16[3,768,384]{2,0,1:T(4,128)(2,1)}), bf16[3,768,384]{2,0,1:T(4,128)(2,1)}, u32[]{:S(2)}, u32[]{:S(2)}) async-start(bf16[3,768,384]{2,0,1:T(4,128)(2,1)} %copy.202), calls=%async_computation.2 | async-start | bytes 4718592 | tf_op jit(solution)/shard_map/all_to_all | solution.py:309
  653.5 58.6 %copy-start.64 = (s32[64]{0:T(128)S(1)}, s32[64]{0:T(128)}, u32[]{:S(2)}) copy-start(s32[64]{0:T(128)} %constant.208) | copy-start | bytes 772
  653.5 58.6 %copy-start.14 = (bf16[1,768,192]{1,2,0:T(8,128)(2,1)S(1)}, bf16[1,768,192]{1,2,0:T(8,128)(2,1)}, u32[]{:S(2)}) copy-start(bf16[1,768,192]{1,2,0:T(8,128)(2,1)} %copy-done.13) | copy-start | bytes 884740
  701.3 63.6 %all-to-all-start.3 = ((bf16[3,768,384]{2,0,1:T(4,128)(2,1)}), bf16[3,768,384]{2,0,1:T(4,128)(2,1)}, u32[]{:S(2)}, u32[]{:S(2)}) async-start(bf16[3,768,384]{2,0,1:T(4,128)(2,1)} %copy.204), calls=%async_computation.3 | async-start | bytes 4718592 | tf_op jit(solution)/shard_map/all_to_all | solution.py:312
  727.1 49.5 %copy-start.39 = (f32[3,12,384]{2,1,0:T(8,128)}, f32[3,12,384]{2,1,0:T(8,128)S(1)}, u32[]{:S(2)}) copy-start(f32[3,12,384]{2,1,0:T(8,128)S(1)} %reduce_sum.238) | copy-start | bytes 165892
  778.8 61.1 %all-to-all-start.4 = ((bf16[64,12,384]{2,1,0:T(8,128)(2,1)}), bf16[64,12,384]{2,1,0:T(8,128)(2,1)S(1)}, u32[]{:S(2)}, u32[]{:S(2)}) async-start(bf16[64,12,384]{2,1,0:T(8,128)(2,1)} %gather_fusion.5), calls=%async_computation.4 | async-start | bytes 1572864 | tf_op jit(solution)/shard_map/all_to_all | solution.py:356
  789.1 47.7 %copy-start.52 = (f32[197]{0:T(256)S(1)}, f32[197]{0:T(256)}, u32[]{:S(2)}) copy-start(f32[197]{0:T(256)} %copy-done.51) | copy-start | bytes 2368
  789.2 47.6 %all-reduce.12.cloned.1.call-start = ((), (), s32[]{:S(2)}) async-start(), calls=%async_computation.11 | async-start | bytes 1228800 | tf_op jit(solution)/shard_map/psum | solution.py:240
  839.9 28.2 %all-to-all-start = ((bf16[1,768,5]{2,0,1:T(2,128)(2,1)}), bf16[1,768,5]{2,0,1:T(2,128)(2,1)}, u32[]{:S(2)}, u32[]{:S(2)}) async-start(bf16[1,768,5]{2,0,1:T(2,128)(2,1)} %copy.199), calls=%async_computation | async-start | bytes 786432 | tf_op jit(solution)/shard_map/all_to_all | solution.py:315
  860.4 21.1 %copy-start.17 = (f32[1,197,768]{2,1,0:T(8,128)S(1)}, f32[1,197,768]{2,1,0:T(8,128)}, u32[]{:S(2)}) copy-start(f32[1,197,768]{2,1,0:T(8,128)} %add_bitcast_fusion) | copy-start | bytes 1815556
  868.1 30.4 %all-to-all-start.5 = ((bf16[64,2,2304]{2,1,0:T(2,128)(2,1)}), bf16[64,2,2304]{2,1,0:T(2,128)(2,1)}, u32[]{:S(2)}, u32[]{:S(2)}) async-start(bf16[64,2,2304]{2,1,0:T(2,128)(2,1)} %reshape.673), calls=%async_computation.5 | async-start | bytes 1179648 | tf_op jit(solution)/shard_map/all_to_all | solution.py:366
  (54 other events, 287.7 us)
Sparse Core Ops, SparseCore 0:
  12.3 114.7 all-gather.5
  189.7 55.5 all-reduce.7
  249.6 118.7 all-gather.7
  372.5 115.8 all-gather.9
  531.1 40.1 all-reduce.9
  793.0 43.7 all-reduce.11
where the time goes:
time: 928 us; the launch traced here: 916 us
  blocking collectives  349 us (38%)
  waiting for transfers between devices  300 us (32%)
  local copies, waits for them, and re-layouts  94.1 us (10%)
  starting transfers between devices  71.3 us (8%)
  other arithmetic  48.9 us (5%)
  matrix products  31.2 us (3%)
  between operations  16.6 us (2%)
    all_gather x1, blocking collectives, shards(): lax.all_gather(round_half(router), 'dp', axis=0, tiled=True)  178 us
    all_gather x1, blocking collectives, shards(): lax.all_gather(round_half(norm_gains), 'dp', axis=1, tiled=True)  160 us
    all_gather x1, waiting for transfers between devices, shards(): lax.all_gather(round_half(expert_out), 'dp', axis=1, tiled=True)  87.9 us
    all_to_all x1, waiting for transfers between devices, shards(): lax.all_to_all(grad_in.astype(jnp.bfloat16), 'dp', split_axis=1, concat_a...  47.8 us
    psum x1, waiting for transfers between devices, shards(): lax.psum(moe_part.astype(jnp.bfloat16), 'tensor').astype(jnp.float32)  41.7 us
    psum x1, waiting for transfers between devices, shards(): lax.psum(grad_normed_part.astype(jnp.bfloat16), 'tensor')  40 us
    all_to_all x1, waiting for transfers between devices, shards(): lax.all_to_all(grad_out.astype(jnp.bfloat16), 'dp', split_axis=1, concat_...  37.7 us
    all_to_all x1, waiting for transfers between devices, shards(): lax.all_to_all(grad_attn.astype(jnp.bfloat16), 'dp', split_axis=1, concat...  33.2 us
  transfers between devices with their start and end apart: 12, of which 7 were waited for; matrix products, arithmetic and copies ran while one was open for 10% of the time, Pallas kernels for 0%

commit v1 on v0

--- a/solution.py
+++ b/solution.py
@@ -83,23 +83,6 @@
     return 0.5 * (1.0 + lax.erf(pre_act * ROOT_HALF)) + pre_act * INV_ROOT_TAU * jnp.exp(
         -0.5 * pre_act * pre_act
     )
-
-
-def slot_tables(picked, experts, capacity):
-    flat_picks = picked.reshape(-1)
-    assign_count = flat_picks.shape[0]
-    one_hot = (flat_picks[:, None] == jnp.arange(experts, dtype=jnp.int32)[None, :]).astype(
-        jnp.int32
-    )
-    before = jnp.cumsum(one_hot, axis=0) - one_hot
-    slot_place = jnp.sum(before * one_hot, axis=1)
-    target = flat_picks * capacity + slot_place
-    slot_owner = (
-        jnp.full((experts * capacity,), assign_count, jnp.int32)
-        .at[target]
-        .set(jnp.arange(assign_count, dtype=jnp.int32))
-    )
-    return (target, slot_owner)
 
 
 def score_table(queries, key_rows):
@@ -205,13 +188,17 @@
     image_count, seq_len, model_width = inputs.shape
     dp_count = lax.axis_size("dp")
     row_count = image_count * seq_len
-    gains_half, attn_half, router_half, in_half, out_half = (
-        lax.all_gather(round_half(norm_gains), "dp", axis=1, tiled=True),
-        lax.all_gather(round_half(attn_mats), "dp", axis=1, tiled=True),
-        lax.all_gather(round_half(router), "dp", axis=0, tiled=True),
-        lax.all_gather(round_half(expert_in), "dp", axis=1, tiled=True),
-        lax.all_gather(round_half(expert_out), "dp", axis=1, tiled=True),
-    )
+    small_plane = jnp.zeros((1, norm_gains.shape[1], attn_mats.shape[2]), jnp.bfloat16)
+    small_plane = small_plane.at[0, :, :2].set(round_half(norm_gains).T)
+    small_plane = small_plane.at[0, :, 2 : 2 + EF].set(round_half(router))
+    packed = lax.all_gather(
+        jnp.concatenate([round_half(attn_mats), small_plane], axis=0), "dp", axis=1, tiled=True
+    )
+    attn_half = packed[:4]
+    gains_half = packed[4, :, :2].T
+    router_half = packed[4, :, 2 : 2 + EF]
+    in_half = lax.all_gather(round_half(expert_in), "dp", axis=1, tiled=True)
+    out_half = lax.all_gather(round_half(expert_out), "dp", axis=1, tiled=True)
     gain_one = to_single(gains_half[0])
     gain_two = to_single(gains_half[1])
     row_in = inputs.reshape(row_count, model_width)
@@ -224,51 +211,39 @@
     middle = row_in + attn_full
     normal_two, inv_two, normed_two = norm_forward(middle, gain_two)
     picked = routes.reshape(row_count, 2)
-    target, slot_owner = slot_tables(picked, EF, CAP)
+    one_hot = (picked[:, :, None] == jnp.arange(EF, dtype=jnp.int32)[None, None, :]).astype(
+        jnp.float32
+    )
     logits = jnp.dot(normed_two, router_half, preferred_element_type=jnp.float32)
-    chosen = jnp.take_along_axis(logits, picked, axis=1)
+    chosen = jnp.sum(logits[:, None, :] * one_hot, axis=2)
     gate_vals = jax.nn.sigmoid(chosen - chosen[:, ::-1])
-    padded = jnp.concatenate([normed_two, jnp.zeros((1, model_width), jnp.bfloat16)], axis=0)
-    dispatched = padded[slot_owner // 2].reshape(EF, CAP, model_width)
-    pre_act = jnp.einsum("ecd,edf->ecf", dispatched, in_half, preferred_element_type=jnp.float32)
+    gate_table = jnp.sum(gate_vals[:, :, None] * one_hot, axis=1)
+    grad_rows = cotangent.reshape(row_count, model_width)
+    pre_act = jnp.einsum("td,edf->etf", normed_two, in_half, preferred_element_type=jnp.float32)
     hidden = round_half(gelu_value(pre_act))
-    expert_rows = jnp.einsum("ecf,edf->ecd", hidden, out_half, preferred_element_type=jnp.float32)
-    per_choice = expert_rows.reshape(EF * CAP, model_width)[target].reshape(
-        row_count, 2, model_width
-    )
-    moe_part = jnp.sum(gate_vals[:, :, None] * per_choice, axis=1)
+    expert_rows = jnp.einsum("etf,edf->etd", hidden, out_half, preferred_element_type=jnp.float32)
+    moe_part = jnp.sum(gate_table.T[:, :, None] * expert_rows, axis=0)
     moe_full = lax.psum(moe_part.astype(jnp.bfloat16), "tensor").astype(jnp.float32)
     output_rows = middle + moe_full
-    grad_rows = cotangent.reshape(row_count, model_width)
-    grad_choice_part = jnp.sum(grad_rows[:, None, :] * per_choice, axis=2)
-    gate_flat = jnp.concatenate([gate_vals.reshape(-1), jnp.zeros((1,), jnp.float32)])
-    grad_pad = jnp.concatenate([grad_rows, jnp.zeros((1, model_width), jnp.float32)], axis=0)
-    grad_expert = round_half(gate_flat[slot_owner][:, None] * grad_pad[slot_owner // 2]).reshape(
-        EF, CAP, model_width
-    )
+    grad_each = jnp.sum(grad_rows[None] * expert_rows, axis=2).T
+    grad_choice_part = jnp.sum(grad_each[:, None, :] * one_hot, axis=2)
+    grad_expert = round_half(gate_table.T[:, :, None] * grad_rows[None])
     grad_hidden = jnp.einsum(
-        "ecd,edf->ecf", grad_expert, out_half, preferred_element_type=jnp.float32
+        "etd,edf->etf", grad_expert, out_half, preferred_element_type=jnp.float32
     )
     grad_pre = round_half(grad_hidden * gelu_slope(pre_act))
-    grad_dispatch = jnp.einsum(
-        "ecf,edf->ecd", grad_pre, in_half, preferred_element_type=jnp.float32
-    )
-    grad_normed_part = jnp.sum(
-        grad_dispatch.reshape(EF * CAP, model_width)[target].reshape(row_count, 2, model_width),
-        axis=1,
-    )
-    grad_in = jnp.einsum("ecd,ecf->edf", dispatched, grad_pre, preferred_element_type=jnp.float32)
-    grad_out = jnp.einsum("ecd,ecf->edf", grad_expert, hidden, preferred_element_type=jnp.float32)
-    grad_choice, grad_normed_moe = (
-        lax.psum(grad_choice_part.astype(jnp.bfloat16), "tensor").astype(jnp.float32),
-        lax.psum(grad_normed_part.astype(jnp.bfloat16), "tensor").astype(jnp.float32),
-    )
+    grad_normed_part = jnp.einsum(
+        "etf,edf->td", grad_pre, in_half, preferred_element_type=jnp.float32
+    )
+    grad_in = jnp.einsum("td,etf->edf", normed_two, grad_pre, preferred_element_type=jnp.float32)
+    grad_out = jnp.einsum("etd,etf->edf", grad_expert, hidden, preferred_element_type=jnp.float32)
+    joined = lax.psum(
+        jnp.concatenate([grad_normed_part, grad_choice_part], axis=1).astype(jnp.bfloat16), "tensor"
+    ).astype(jnp.float32)
+    grad_normed_moe, grad_choice = joined[:, :model_width], joined[:, model_width:]
     gate_prod = gate_vals[:, 0] * gate_vals[:, 1]
     grad_first = (grad_choice[:, 0] - grad_choice[:, 1]) * gate_prod
     grad_picked = jnp.stack([grad_first, -grad_first], axis=1)
-    one_hot = (picked[:, :, None] == jnp.arange(EF, dtype=jnp.int32)[None, None, :]).astype(
-        jnp.float32
-    )
     grad_logits = round_half(jnp.sum(grad_picked[:, :, None] * one_hot, axis=1))
     grad_router = contract_rows(normed_two, grad_logits)
     grad_normed_two = grad_normed_moe + contract_cols(grad_logits, router_half)

time: 928 us -> 861 us (0.928)
  blocking collectives: 349 us -> 0 us
  waiting for transfers between devices: 300 us -> 599 us
  local copies, waits for them, and re-layouts: 94.1 us -> 75.5 us
    all_gather x2 -> x0, blocking collectives: 338 us -> none  [the longest x1 178 us: shards(): lax.all_gather(round_half(router), 'dp', axis=0, tiled=True)]
    all_gather x3, waiting for transfers between devices: 87.9 us -> 356 us  [the longest x1 121 us: shards(): in_half = lax.all_gather(round_half(expert_in), 'dp', axis=1, tiled=True)]
    psum x1, waiting for transfers between devices: 0.02 us -> 36.9 us  [shards(): lax.psum(attn_part.astype(jnp.bfloat16), 'tensor').astype(jnp.float32)]
    gather x10 -> x0, local copies, waits for them, and re-layouts: 23.1 us -> none  [the longest x4 6.39 us: shards(): chosen = jnp.take_along_axis(logits, picked, axis=1)]
    psum x1 -> x0, blocking collectives: 11.6 us -> none  [shards(): lax.psum(grad_choice_part.astype(jnp.bfloat16), 'tensor')]
    reshape x7 -> x1, local copies, waits for them, and re-layouts: 10.7 us -> 0.04 us  [shards(): grad_rows = cotangent.reshape(row_count, model_width)]
    unnamed x149 -> x134, local copies, waits for them, and re-layouts: 18.9 us -> 23.2 us
  transfers between devices with their start and end apart: 12 -> 12, of which waited for: 7 -> 10; matrix products, arithmetic and copies ran while one was open for 10% -> 9% of each run, Pallas kernels for 0% -> 0%
where the time goes in v1:
time: 861 us; the launch traced here: 850 us
  waiting for transfers between devices  599 us (70%)
  local copies, waits for them, and re-layouts  75.5 us (9%)
  starting transfers between devices  71.1 us (8%)
  other arithmetic  45.9 us (5%)
  matrix products  33.5 us (4%)
  between operations  16 us (2%)
  loops' own time  8.68 us (1%)
    all_gather x1, waiting for transfers between devices, shards(): in_half = lax.all_gather(round_half(expert_in), 'dp', axis=1, tiled=True)  121 us
    all_gather x1, waiting for transfers between devices, shards(): lax.all_gather(jnp.concatenate([round_half(attn_mats), small_plane], axis...  118 us
    all_gather x1, waiting for transfers between devices, shards(): out_half = lax.all_gather(round_half(expert_out), 'dp', axis=1, tiled=True)  117 us
    all_to_all x1, waiting for transfers between devices, shards(): lax.all_to_all(grad_in.astype(jnp.bfloat16), 'dp', split_axis=1, concat_a...  48.2 us
    psum x1, waiting for transfers between devices, shards(): lax.psum(moe_part.astype(jnp.bfloat16), 'tensor').astype(jnp.float32)  41.6 us
    psum x1, waiting for transfers between devices, shards(): lax.psum(jnp.concatenate([grad_normed_part, grad_choice_part], axis=1).as...  39.4 us
    psum x1, waiting for transfers between devices, shards(): lax.psum(attn_part.astype(jnp.bfloat16), 'tensor').astype(jnp.float32)  36.9 us
    all_to_all x1, waiting for transfers between devices, shards(): lax.all_to_all(grad_out.astype(jnp.bfloat16), 'dp', split_axis=1, concat_...  34.3 us
  transfers between devices with their start and end apart: 12, of which 10 were waited for; matrix products, arithmetic and copies ran while one was open for 9% of the time, Pallas kernels for 0%

profile of v1, /device:TPU:94, one launch (start us, length us, event | category | flops | bytes accessed | tf_op | source)
XLA Modules:
  0.0 849.5 jit_solution(13263834224516836586)
XLA Ops:
  19.4 117.8 %all-gather.4.cloned.1.call-done = bf16[5,768,192]{2,0,1:T(8,128)(2,1)} async-done(((bf16[5,12,192]{2,0,1:T(8,128)(2,1)}), bf16[5,768,192]{2,0,1:T(8,128)(2,1)}) %all-gather.4.cloned.1.call-update) | async-done | bytes 1474576 | tf_op jit(solution)/shard_map/all_gather | solution.py:194
  139.3 9.2 %fusion.173 = (bf16[1,768,192]{2,0,1:T(2,128)(2,1)}, bf16[1,768,192]{2,0,1:T(2,128)(2,1)}, bf16[1,768,192]{2,0,1:T(2,128)(2,1)S(1)}, bf16[1,768,192]{2,0,1:T(2,128)(2,1)S(1)}) fusion(bf16[5,768,192]{2,0,1:T(8,128)(2,1)} %all-gather.4.cloned.1.call-done), kind=kLoop, calls=%fused_computation.301 | loop fusion | bytes 2359296 | tf_op jit(solution)/shard_map/slice | solution.py:209
  165.3 36.9 %all-reduce.6.cloned.1.call-done = bf16[197,768]{0,1:T(8,128)(2,1)} async-done(((bf16[197,768]{0,1:T(8,128)(2,1)}), bf16[197,768]{0,1:T(8,128)(2,1)}) %all-reduce.6.cloned.1.call-update) | async-done | bytes 302608 | tf_op jit(solution)/shard_map/psum | solution.py:210
  204.0 120.8 %all-gather.6.cloned.1.call-done = bf16[3,768,384]{2,0,1:T(4,128)(2,1)} async-done(((bf16[3,12,384]{2,0,1:T(4,128)(2,1)}), bf16[3,768,384]{2,0,1:T(4,128)(2,1)}) %all-gather.6.cloned.1.call-update) | async-done | bytes 1769488 | tf_op jit(solution)/shard_map/all_gather | solution.py:200
  328.1 117.3 %all-gather.8.cloned.1.call-done = bf16[3,768,384]{2,0,1:T(4,128)(2,1)} async-done(((bf16[3,12,384]{2,0,1:T(4,128)(2,1)}), bf16[3,768,384]{2,0,1:T(4,128)(2,1)}) %all-gather.8.cloned.1.call-update) | async-done | bytes 1769488 | tf_op jit(solution)/shard_map/all_gather | solution.py:201
  445.4 4.0 multiply_reduce_fusion.2
  454.0 39.4 %all-reduce.8.cloned.1.call-done = bf16[197,770]{0,1:T(8,128)(2,1)} async-done(((bf16[197,770]{0,1:T(8,128)(2,1)}), bf16[197,770]{0,1:T(8,128)(2,1)}) %all-reduce.8.cloned.1.call-update) | async-done | bytes 303396 | tf_op jit(solution)/shard_map/psum | solution.py:240
  512.1 13.1 %all-to-all-start.1 = ((bf16[4,768,192]{2,0,1:T(4,128)(2,1)}), bf16[4,768,192]{2,0,1:T(4,128)(2,1)}, u32[]{:S(2)}, u32[]{:S(2)}) async-start(bf16[4,768,192]{2,0,1:T(4,128)(2,1)} %copy.251), calls=%async_computation.1 | async-start | bytes 3145728 | tf_op jit(solution)/shard_map/all_to_all | solution.py:281
  527.2 5.2 copy.253
  532.4 31.1 %all-to-all-done.1 = bf16[4,768,192]{2,0,1:T(4,128)(2,1)} async-done(((bf16[4,768,192]{2,0,1:T(4,128)(2,1)}), bf16[4,768,192]{2,0,1:T(4,128)(2,1)}, u32[]{:S(2)}, u32[]{:S(2)}) %all-to-all-start.1) | async-done | bytes 1179680 | tf_op jit(solution)/shard_map/all_to_all | solution.py:281
  563.5 11.0 %all-to-all-start.2 = ((bf16[3,768,384]{2,0,1:T(4,128)(2,1)}), bf16[3,768,384]{2,0,1:T(4,128)(2,1)}, u32[]{:S(2)}, u32[]{:S(2)}) async-start(bf16[3,768,384]{2,0,1:T(4,128)(2,1)} %copy.253), calls=%async_computation.2 | async-start | bytes 4718592 | tf_op jit(solution)/shard_map/all_to_all | solution.py:284
  579.6 48.2 %all-to-all-done.2 = bf16[3,768,384]{2,0,1:T(4,128)(2,1)} async-done(((bf16[3,768,384]{2,0,1:T(4,128)(2,1)}), bf16[3,768,384]{2,0,1:T(4,128)(2,1)}, u32[]{:S(2)}, u32[]{:S(2)}) %all-to-all-start.2) | async-done | bytes 1769504 | tf_op jit(solution)/shard_map/all_to_all | solution.py:284
  627.8 10.6 %all-to-all-start.3 = ((bf16[3,768,384]{2,0,1:T(4,128)(2,1)}), bf16[3,768,384]{2,0,1:T(4,128)(2,1)}, u32[]{:S(2)}, u32[]{:S(2)}) async-start(bf16[3,768,384]{2,0,1:T(4,128)(2,1)} %copy.255), calls=%async_computation.3 | async-start | bytes 4718592 | tf_op jit(solution)/shard_map/all_to_all | solution.py:287
  649.7 4.7 reshape.538
  657.0 34.3 %all-to-all-done.3 = bf16[3,768,384]{2,0,1:T(4,128)(2,1)} async-done(((bf16[3,768,384]{2,0,1:T(4,128)(2,1)}), bf16[3,768,384]{2,0,1:T(4,128)(2,1)}, u32[]{:S(2)}, u32[]{:S(2)}) %all-to-all-start.3) | async-done | bytes 1769504 | tf_op jit(solution)/shard_map/all_to_all | solution.py:287
  695.0 4.7 reshape.539
  704.8 10.1 %all-to-all-start.4 = ((bf16[64,12,384]{2,1,0:T(8,128)(2,1)}), bf16[64,12,384]{2,1,0:T(8,128)(2,1)S(1)}, u32[]{:S(2)}, u32[]{:S(2)}) async-start(bf16[64,12,384]{2,1,0:T(8,128)(2,1)} %gather_fusion), calls=%async_computation.4 | async-start | bytes 1572864 | tf_op jit(solution)/shard_map/all_to_all | solution.py:331
  722.5 41.6 %all-reduce.10.cloned.1.call-done = (bf16[197,768]{0,1:T(8,128)(2,1)}, bf16[197,768]{0,1:T(8,128)(2,1)}) async-done(((bf16[197,768]{0,1:T(8,128)(2,1)}, bf16[197,768]{0,1:T(8,128)(2,1)}), (bf16[197,768]{0,1:T(8,128)(2,1)}, bf16[197,768]{0,1:T(8,128)(2,1)})) %all-reduce.10.cloned.1.call-update) | async-done | bytes 605200 | tf_op jit(solution)/shard_map/psum | solution.py:226
  767.9 13.0 %all-to-all-start = ((bf16[1,768,5]{2,0,1:T(2,128)(2,1)}), bf16[1,768,5]{2,0,1:T(2,128)(2,1)}, u32[]{:S(2)}, u32[]{:S(2)}) async-start(bf16[1,768,5]{2,0,1:T(2,128)(2,1)} %copy.249), calls=%async_computation | async-start | bytes 786432 | tf_op jit(solution)/shard_map/all_to_all | solution.py:290
  781.9 8.7 %conditional.1 = (bf16[768,384]{0,1:T(8,128)(2,1)S(1)}) conditional(s32[]{:T(128)} %bitcast.63, bf16[64,12,384]{2,1,0:T(8,128)(2,1)S(1)} %all-to-all-done.4, bf16[64,12,384]{2,1,0:T(8,128)(2,1)S(1)} %all-to-all-done.4, () %tuple.25), branch_computations={%region_28.31_spmd, %region_31.0_spmd, %region_33.34_spmd} | conditional | flops 1706655744 | bytes 14450752 | solution.py:338
  795.4 5.1 reduce.33
  803.1 12.9 %all-to-all-start.5 = ((bf16[64,2,2304]{2,1,0:T(2,128)(2,1)}), bf16[64,2,2304]{2,1,0:T(2,128)(2,1)}, u32[]{:S(2)}, u32[]{:S(2)}) async-start(bf16[64,2,2304]{2,1,0:T(2,128)(2,1)} %reshape.565), calls=%async_computation.5 | async-start | bytes 1179648 | tf_op jit(solution)/shard_map/all_to_all | solution.py:341
  821.4 11.3 %all-to-all-done.5 = bf16[64,2,2304]{2,1,0:T(2,128)(2,1)} async-done(((bf16[64,2,2304]{2,1,0:T(2,128)(2,1)}), bf16[64,2,2304]{2,1,0:T(2,128)(2,1)}, u32[]{:S(2)}, u32[]{:S(2)}) %all-to-all-start.5) | async-done | bytes 589856 | tf_op jit(solution)/shard_map/all_to_all | solution.py:341
  832.8 3.8 reshape.566
  (260 shorter events, 118.7 us)
Async XLA Ops:
  7.2 129.9 %all-gather.4.cloned.1.call-start = ((), (), s32[]{:S(2)}) async-start(), calls=%async_computation.6 | async-start | bytes 3194880 | tf_op jit(solution)/shard_map/all_gather | solution.py:194
  15.6 186.6 %all-reduce.6.cloned.1.call-start = ((), (), s32[]{:S(2)}) async-start(), calls=%async_computation.7 | async-start | bytes 786432 | tf_op jit(solution)/shard_map/psum | solution.py:210
  160.9 163.9 %all-gather.6.cloned.1.call-start = ((), (), s32[]{:S(2)}) async-start(), calls=%async_computation.8 | async-start | bytes 2396160 | tf_op jit(solution)/shard_map/all_gather | solution.py:200
  161.6 283.8 %all-gather.8.cloned.1.call-start = ((), (), s32[]{:S(2)}) async-start(), calls=%async_computation.9 | async-start | bytes 2396160 | tf_op jit(solution)/shard_map/all_gather | solution.py:201
  162.4 331.1 %all-reduce.8.cloned.1.call-start = ((), (), s32[]{:S(2)}) async-start(), calls=%async_computation.10 | async-start | bytes 794624 | tf_op jit(solution)/shard_map/psum | solution.py:240
  162.7 286.8 %copy-start.10 = (f32[1,197,768]{2,1,0:T(8,128)}, f32[1,197,768]{2,1,0:T(8,128)S(1)}, u32[]{:S(2)}) copy-start(f32[1,197,768]{2,1,0:T(8,128)S(1)} %copy.306) | copy-start | bytes 1815556
  165.3 38.6 %copy-start.41 = (s32[1,197,2]{1,2,0:T(2,128)S(1)}, s32[1,197,2]{1,2,0:T(2,128)}, u32[]{:S(2)}) copy-start(s32[1,197,2]{1,2,0:T(2,128)} %param.35) | copy-start | bytes 4732
  203.5 291.2 %copy-start.47 = (f32[197]{0:T(256)}, f32[197]{0:T(256)S(1)}, u32[]{:S(2)}) copy-start(f32[197]{0:T(256)S(1)} %add_rsqrt_fusion) | copy-start | bytes 2368
  204.0 245.4 %copy-start.48 = (f32[197,3]{0,1:T(4,128)}, f32[197,3]{0,1:T(4,128)S(1)}, u32[]{:S(2)}) copy-start(f32[197,3]{0,1:T(4,128)S(1)} %select_reduce_fusion.2) | copy-start | bytes 7096
  512.1 51.4 %all-to-all-start.1 = ((bf16[4,768,192]{2,0,1:T(4,128)(2,1)}), bf16[4,768,192]{2,0,1:T(4,128)(2,1)}, u32[]{:S(2)}, u32[]{:S(2)}) async-start(bf16[4,768,192]{2,0,1:T(4,128)(2,1)} %copy.251), calls=%async_computation.1 | async-start | bytes 3145728 | tf_op jit(solution)/shard_map/all_to_all | solution.py:281
  532.4 42.1 %copy-start.11 = (f32[1,197,768]{2,1,0:T(8,128)S(1)}, f32[1,197,768]{2,1,0:T(8,128)}, u32[]{:S(2)}) copy-start(f32[1,197,768]{2,1,0:T(8,128)} %copy-done.10) | copy-start | bytes 1815556
  532.4 42.1 %copy-start.49 = (f32[197,3]{0,1:T(4,128)S(1)}, f32[197,3]{0,1:T(4,128)}, u32[]{:S(2)}) copy-start(f32[197,3]{0,1:T(4,128)} %copy-done.48) | copy-start | bytes 7096
  563.5 64.3 %all-to-all-start.2 = ((bf16[3,768,384]{2,0,1:T(4,128)(2,1)}), bf16[3,768,384]{2,0,1:T(4,128)(2,1)}, u32[]{:S(2)}, u32[]{:S(2)}) async-start(bf16[3,768,384]{2,0,1:T(4,128)(2,1)} %copy.253), calls=%async_computation.2 | async-start | bytes 4718592 | tf_op jit(solution)/shard_map/all_to_all | solution.py:284
  579.6 58.9 %copy-start.57 = (s32[64]{0:T(128)S(1)}, s32[64]{0:T(128)}, u32[]{:S(2)}) copy-start(s32[64]{0:T(128)} %constant.199) | copy-start | bytes 772
  579.6 58.9 %copy-start.27 = (bf16[197,768]{1,0:T(8,128)(2,1)S(1)}, bf16[197,768]{1,0:T(8,128)(2,1)}, u32[]{:S(2)}) copy-start(bf16[197,768]{1,0:T(8,128)(2,1)} %get-tuple-element.173) | copy-start | bytes 907780
  627.8 63.6 %all-to-all-start.3 = ((bf16[3,768,384]{2,0,1:T(4,128)(2,1)}), bf16[3,768,384]{2,0,1:T(4,128)(2,1)}, u32[]{:S(2)}, u32[]{:S(2)}) async-start(bf16[3,768,384]{2,0,1:T(4,128)(2,1)} %copy.255), calls=%async_computation.3 | async-start | bytes 4718592 | tf_op jit(solution)/shard_map/all_to_all | solution.py:287
  657.0 45.4 %copy-start.32 = (f32[3,12,384]{2,1,0:T(8,128)}, f32[3,12,384]{2,1,0:T(8,128)S(1)}, u32[]{:S(2)}) copy-start(f32[3,12,384]{2,1,0:T(8,128)S(1)} %reduce_sum.245) | copy-start | bytes 165892
  704.8 63.1 %all-to-all-start.4 = ((bf16[64,12,384]{2,1,0:T(8,128)(2,1)}), bf16[64,12,384]{2,1,0:T(8,128)(2,1)S(1)}, u32[]{:S(2)}, u32[]{:S(2)}) async-start(bf16[64,12,384]{2,1,0:T(8,128)(2,1)} %gather_fusion), calls=%async_computation.4 | async-start | bytes 1572864 | tf_op jit(solution)/shard_map/all_to_all | solution.py:331
  714.9 49.1 %copy-start.38 = (f32[768]{0:T(1024)S(1)}, f32[768]{0:T(1024)}, u32[]{:S(2)}) copy-start(f32[768]{0:T(1024)} %get-tuple-element.181) | copy-start | bytes 9220
  714.9 49.1 %copy-start.43 = (f32[197]{0:T(256)S(1)}, f32[197]{0:T(256)}, u32[]{:S(2)}) copy-start(f32[197]{0:T(256)} %copy-done.42) | copy-start | bytes 2368
  714.9 49.1 %copy-start.45 = (f32[197]{0:T(256)S(1)}, f32[197]{0:T(256)}, u32[]{:S(2)}) copy-start(f32[197]{0:T(256)} %add_rsqrt_fusion.1) | copy-start | bytes 2368
  714.9 49.1 %all-reduce.10.cloned.1.call-start = ((), (), s32[]{:S(2)}) async-start(), calls=%async_computation.11 | async-start | bytes 1572864 | tf_op jit(solution)/shard_map/psum | solution.py:226
  767.9 35.2 %all-to-all-start = ((bf16[1,768,5]{2,0,1:T(2,128)(2,1)}), bf16[1,768,5]{2,0,1:T(2,128)(2,1)}, u32[]{:S(2)}, u32[]{:S(2)}) async-start(bf16[1,768,5]{2,0,1:T(2,128)(2,1)} %copy.249), calls=%async_computation | async-start | bytes 786432 | tf_op jit(solution)/shard_map/all_to_all | solution.py:290
  803.1 29.6 %all-to-all-start.5 = ((bf16[64,2,2304]{2,1,0:T(2,128)(2,1)}), bf16[64,2,2304]{2,1,0:T(2,128)(2,1)}, u32[]{:S(2)}, u32[]{:S(2)}) async-start(bf16[64,2,2304]{2,1,0:T(2,128)(2,1)} %reshape.565), calls=%async_computation.5 | async-start | bytes 1179648 | tf_op jit(solution)/shard_map/all_to_all | solution.py:341
  (48 other events, 296.2 us)
Sparse Core Ops, SparseCore 0:
  15.7 121.3 all-gather.3
  161.0 41.1 all-reduce.5
  207.0 117.7 all-gather.5
  329.5 115.8 all-gather.7
  452.9 40.5 all-reduce.7
  718.8 45.2 all-reduce.9

commit v2 on v1

--- a/solution.py
+++ b/solution.py
@@ -4,6 +4,8 @@
 import jax.numpy as jnp
 import numpy as np
 from jax import lax
+from jax.experimental import pallas as pl
+from jax.experimental.pallas import tpu as pltpu
 from jax.sharding import PartitionSpec as P
 
 HEAD_DIM = 64
@@ -23,10 +25,6 @@
 INV_ROOT_TAU = 0.3989422804014327
 
 
-def for_sending(value):
-    return jax.tree.map(lambda a: a.astype(jnp.bfloat16) if a.dtype == jnp.float32 else a, value)
-
-
 def round_half(operand):
     return operand.astype(jnp.bfloat16)
 
@@ -51,11 +49,621 @@
     )
 
 
-def fold_sources(received, source_count):
-    return jnp.sum(
-        received.reshape((source_count, received.shape[0] // source_count) + received.shape[1:]),
-        axis=0,
-    )
+NZ, NX, NY = 8, 4, 2
+ROW = 12
+LANE = 128
+PACK = 304
+SPLIT = 128
+PLANE = NX * NY
+BLOCKS = 8
+MESH_ID = pl.DeviceIdType.MESH
+GROUPS = ((0, 4), (4, 4), (8, 4), (12, 4), (16, 4), (20, 4), (24, 1))
+
+
+def spread_matrix(block_count, padded):
+    table = np.zeros((block_count * PLANE * ROW, PLANE * padded), np.float32)
+    for block in range(block_count):
+        for member in range(PLANE):
+            for row in range(ROW):
+                table[
+                    block * PLANE * ROW + member * ROW + row, member * padded + block * ROW + row
+                ] = 1.0
+    return jnp.asarray(table, jnp.bfloat16)
+
+
+def place_of(me):
+    return me // PLANE, lax.rem(me // NY, NX), lax.rem(me, NY)
+
+
+def dp_index(z, x, y):
+    return z * PLANE + x * NY + y
+
+
+def wrap(value, count):
+    return lax.rem(value + 2 * count, count)
+
+
+def neighbours(me):
+    z, x, y = place_of(me)
+    return (
+        dp_index(wrap(z + 1, NZ), x, y),
+        dp_index(wrap(z - 1, NZ), x, y),
+        dp_index(z, wrap(x + 1, NX), y),
+        dp_index(z, wrap(x - 1, NX), y),
+        dp_index(z, x, 1 - y),
+    )
+
+
+def greet(targets, count):
+    barrier = pltpu.get_barrier_semaphore()
+    for target in targets:
+        pl.semaphore_signal(barrier, inc=1, device_id={"dp": target}, device_id_type=MESH_ID)
+    pl.semaphore_wait(barrier, count)
+
+
+def send(source, landing, send_sem, recv_sem, target):
+    copy = pltpu.make_async_remote_copy(
+        src_ref=source,
+        dst_ref=landing,
+        send_sem=send_sem,
+        recv_sem=recv_sem,
+        device_id={"dp": target},
+        device_id_type=MESH_ID,
+    )
+    copy.start()
+    return copy
+
+
+class GatherRing:
+    def __init__(self, chunk, position, count, up, down, send_sems, recv_sems, base):
+        self.chunk, self.position, self.count = chunk, position, count
+        self.up, self.down = up, down
+        self.send_sems, self.recv_sems, self.base = send_sems, recv_sems, base
+        self.copies = []
+
+    def start(self, step):
+        half = step == self.count // 2 - 1
+        pair = []
+        for side, (sign, target) in enumerate(((-1, self.up), (1, self.down))):
+            part = self.chunk(wrap(self.position + sign * step, self.count), side if half else None)
+            slot = self.base + 2 * step + side
+            pair.append(send(part, part, self.send_sems.at[slot], self.recv_sems.at[slot], target))
+        self.copies.append(pair)
+
+    def arrive(self, step):
+        for copy in self.copies[step]:
+            copy.wait_recv()
+
+    def finish(self):
+        for pair in self.copies:
+            for copy in pair:
+                copy.wait_send()
+
+
+def gather_kernel(
+    shard, four, one, attn_out, small_out, in_out, out_out, slots, local_sem, send_sems, recv_sems
+):
+    me = lax.axis_index("dp")
+    z, x, y = place_of(me)
+    up_z, down_z, up_x, down_x, other_y = neighbours(me)
+    greet((up_z, down_z, up_x, down_x, other_y), 5)
+    own = slots.at[z, NY * x + y]
+    keep = pltpu.make_async_copy(shard, own, local_sem)
+    keep.start()
+    first = send(shard, own, send_sems.at[0], recv_sems.at[0], other_y)
+    keep.wait()
+    first.wait_recv()
+
+    def part_x_small(index, half):
+        if half is None:
+            return slots.at[z, pl.ds(NY * index, NY), pl.ds(0, SPLIT)]
+        return slots.at[z, NY * index + half, pl.ds(0, SPLIT)]
+
+    def part_z_small(index, half):
+        rest = pl.ds(SPLIT, PACK - SPLIT)
+        if half is None:
+            return slots.at[index, pl.ds(NY * x, NY), rest]
+        return slots.at[index, NY * x + half, rest]
+
+    def part_z_large(index, half):
+        if half is None:
+            return slots.at[index, pl.ds(0, PLANE), pl.ds(0, SPLIT)]
+        return slots.at[index, pl.ds(half * (PLANE // 2), PLANE // 2), pl.ds(0, SPLIT)]
+
+    def part_x_large(index, half):
+        rest = pl.ds(SPLIT, PACK - SPLIT)
+        if half is None:
+            return slots.at[pl.ds(0, NZ), pl.ds(NY * index, NY), rest]
+        return slots.at[pl.ds(half * (NZ // 2), NZ // 2), pl.ds(NY * index, NY), rest]
+
+    ring_ax = GatherRing(part_x_small, x, NX, up_x, down_x, send_sems, recv_sems, 1)
+    ring_bz = GatherRing(part_z_small, z, NZ, up_z, down_z, send_sems, recv_sems, 5)
+    ring_az = GatherRing(part_z_large, z, NZ, up_z, down_z, send_sems, recv_sems, 13)
+    ring_bx = GatherRing(part_x_large, x, NX, up_x, down_x, send_sems, recv_sems, 21)
+    ring_ax.start(0)
+    ring_bz.start(0)
+    ring_ax.arrive(0)
+    ring_ax.start(1)
+    ring_bz.arrive(0)
+    ring_bz.start(1)
+    ring_ax.arrive(1)
+    ring_az.start(0)
+    ring_bz.arrive(1)
+    ring_bz.start(2)
+    ring_bz.arrive(2)
+    ring_bz.start(3)
+    ring_az.arrive(0)
+    ring_az.start(1)
+    ring_bz.arrive(3)
+    ring_bx.start(0)
+    ring_az.arrive(1)
+    ring_az.start(2)
+    ring_az.arrive(2)
+    ring_az.start(3)
+    ring_bx.arrive(0)
+    ring_bx.start(1)
+    ring_az.arrive(3)
+    ring_bx.arrive(1)
+
+    def compact(plane, carry):
+        rows = pl.ds(pl.multiple_of(plane * PLANE * ROW, 32), PLANE * ROW)
+
+        def put(block, value):
+            if block < 6:
+                attn_out[rows, block * LANE : (block + 1) * LANE] = value
+            elif block == 6:
+                small_out[rows, :] = value
+            else:
+                target = in_out if block < 16 else out_out
+                index = (block - 7) % 9
+                column = (index % 3) * LANE
+                target[index // 3, rows, column : column + LANE] = value
+
+        for first_block, block_count in GROUPS:
+            padded = 48 if block_count == 4 else 16
+            picked = slots[plane, :, pl.ds(first_block * ROW, padded), :]
+            moved = jnp.dot(
+                (four if block_count == 4 else one)[...],
+                picked.reshape(PLANE * padded, LANE),
+                preferred_element_type=jnp.float32,
+            ).astype(jnp.bfloat16)
+            for block in range(block_count):
+                put(
+                    first_block + block,
+                    moved[block * PLANE * ROW : (block + 1) * PLANE * ROW, :],
+                )
+        return carry
+
+    lax.fori_loop(0, NZ, compact, 0)
+    first.wait_send()
+    for ring in (ring_ax, ring_bz, ring_az, ring_bx):
+        ring.finish()
+
+
+def vmem_specs(count):
+    return [pl.BlockSpec(memory_space=pltpu.VMEM)] * count
+
+
+def gather_weights(shard):
+    shapes = ((768, 768), (768, LANE), (EF, 768, 384), (EF, 768, 384))
+    return pl.pallas_call(
+        gather_kernel,
+        out_shape=[jax.ShapeDtypeStruct(shape, jnp.bfloat16) for shape in shapes],
+        in_specs=vmem_specs(3),
+        out_specs=vmem_specs(4),
+        scratch_shapes=[
+            pltpu.VMEM((NZ, PLANE, PACK, LANE), jnp.bfloat16),
+            pltpu.SemaphoreType.DMA,
+            pltpu.SemaphoreType.DMA((25,)),
+            pltpu.SemaphoreType.DMA((25,)),
+        ],
+        compiler_params=pltpu.CompilerParams(
+            collective_id=0, has_side_effects=True, vmem_limit_bytes=60_000_000
+        ),
+    )(shard, spread_matrix(4, 48), spread_matrix(1, 16))
+
+
+def pack_rows(attn, small, left, right):
+    flat = jnp.concatenate(
+        [
+            jnp.transpose(attn, (1, 0, 2)).reshape(ROW, 768),
+            jnp.pad(small, ((0, 0), (0, LANE - small.shape[1]))),
+            jnp.transpose(left, (1, 0, 2)).reshape(ROW, 1152),
+            jnp.transpose(right, (1, 0, 2)).reshape(ROW, 1152),
+        ],
+        axis=1,
+    )
+    rows = jnp.transpose(flat.reshape(ROW, 25, LANE), (1, 0, 2)).reshape(25 * ROW, LANE)
+    return jnp.pad(rows, ((0, PACK - 25 * ROW), (0, 0)))
+
+
+def unpack_rows(rows):
+    flat = jnp.transpose(rows[: 25 * ROW].reshape(25, ROW, LANE), (1, 0, 2)).reshape(ROW, 25 * LANE)
+    attn = jnp.transpose(flat[:, :768].reshape(ROW, 4, 192), (1, 0, 2))
+    small = flat[:, 768:773]
+    left = jnp.transpose(flat[:, 896:2048].reshape(ROW, EF, 384), (1, 0, 2))
+    right = jnp.transpose(flat[:, 2048:3200].reshape(ROW, EF, 384), (1, 0, 2))
+    return attn, small, left, right
+
+
+class ReduceRing:
+    def __init__(self, chunk, landing, position, count, up, down, send_sems, recv_sems, base):
+        self.chunk, self.landing = chunk, landing
+        self.position, self.count = position, count
+        self.up, self.down = up, down
+        self.send_sems, self.recv_sems, self.base = send_sems, recv_sems, base
+        self.copies = []
+
+    def start(self, step):
+        away = self.count // 2 - step
+        pair = []
+        for side, (sign, target) in enumerate(((1, self.up), (-1, self.down))):
+            half = side if step == 0 else None
+            part = self.chunk(wrap(self.position + sign * away, self.count), half)
+            slot = self.base + 2 * step + side
+            pair.append(
+                send(
+                    part,
+                    self.landing(side, step, half),
+                    self.send_sems.at[slot],
+                    self.recv_sems.at[slot],
+                    target,
+                )
+            )
+        self.copies.append(pair)
+
+    def arrive(self, step):
+        for copy in self.copies[step]:
+            copy.wait_recv()
+        away = self.count // 2 - 1 - step
+        if away == 0:
+            mine = self.chunk(self.position, None)
+            mine[...] = (
+                mine[...].astype(jnp.float32)
+                + self.landing(0, step, None)[...].astype(jnp.float32)
+                + self.landing(1, step, None)[...].astype(jnp.float32)
+            ).astype(jnp.bfloat16)
+            return
+        for side, sign in ((0, 1), (1, -1)):
+            half = side if step == 0 else None
+            mine = self.chunk(wrap(self.position + sign * away, self.count), half)
+            mine[...] = (
+                mine[...].astype(jnp.float32)
+                + self.landing(side, step, half)[...].astype(jnp.float32)
+            ).astype(jnp.bfloat16)
+
+    def finish(self):
+        for pair in self.copies:
+            for copy in pair:
+                copy.wait_send()
+
+
+def reduce_kernel(
+    attn, small, left, right, four, one, total,
+    slots, land_az, land_bx, land_ax, land_bz, land_y, send_sems, recv_sems,
+):
+    me = lax.axis_index("dp")
+    z, x, y = place_of(me)
+    up_z, down_z, up_x, down_x, other_y = neighbours(me)
+    greet((up_z, down_z, up_x, down_x, other_y), 5)
+
+    def expand(plane, carry):
+        rows = pl.ds(pl.multiple_of(plane * PLANE * ROW, 32), PLANE * ROW)
+
+        def get(block):
+            if block < 6:
+                return attn[rows, block * LANE : (block + 1) * LANE]
+            if block == 6:
+                return small[rows, :]
+            source = left if block < 16 else right
+            index = (block - 7) % 9
+            column = (index % 3) * LANE
+            return source[index // 3, rows, column : column + LANE]
+
+        for first_block, block_count in GROUPS:
+            padded = 48 if block_count == 4 else 16
+            stacked = [get(first_block + block) for block in range(block_count)]
+            moved = jnp.dot(
+                (four if block_count == 4 else one)[...],
+                stacked[0] if block_count == 1 else jnp.concatenate(stacked, axis=0),
+                preferred_element_type=jnp.float32,
+            ).astype(jnp.bfloat16)
+            slots[plane, :, pl.ds(first_block * ROW, padded), :] = moved.reshape(
+                PLANE, padded, LANE
+            )
+        return carry
+
+    lax.fori_loop(0, NZ, expand, 0)
+    rest = pl.ds(SPLIT, PACK - SPLIT)
+    head = pl.ds(0, SPLIT)
+
+    def part_az(index, half):
+        if half is None:
+            return slots.at[index, pl.ds(0, PLANE), head]
+        return slots.at[index, pl.ds(half * (PLANE // 2), PLANE // 2), head]
+
+    def land_of_az(side, step, half):
+        if half is None:
+            return land_az.at[side, step]
+        return land_az.at[side, step, pl.ds(half * (PLANE // 2), PLANE // 2)]
+
+    def part_bx(index, half):
+        if half is None:
+            return slots.at[pl.ds(0, NZ), pl.ds(NY * index, NY), rest]
+        return slots.at[pl.ds(half * (NZ // 2), NZ // 2), pl.ds(NY * index, NY), rest]
+
+    def land_of_bx(side, step, half):
+        if half is None:
+            return land_bx.at[side, step]
+        return land_bx.at[side, step, pl.ds(half * (NZ // 2), NZ // 2)]
+
+    def part_ax(index, half):
+        if half is None:
+            return slots.at[z, pl.ds(NY * index, NY), head]
+        return slots.at[z, pl.ds(NY * index + half, 1), head]
+
+    def land_of_ax(side, step, half):
+        if half is None:
+            return land_ax.at[side, step]
+        return land_ax.at[side, step, pl.ds(half, 1)]
+
+    def part_bz(index, half):
+        if half is None:
+            return slots.at[index, pl.ds(NY * x, NY), rest]
+        return slots.at[index, pl.ds(NY * x + half, 1), rest]
+
+    def land_of_bz(side, step, half):
+        if half is None:
+            return land_bz.at[side, step]
+        return land_bz.at[side, step, pl.ds(half, 1)]
+
+    ring_az = ReduceRing(part_az, land_of_az, z, NZ, up_z, down_z, send_sems, recv_sems, 1)
+    ring_bx = ReduceRing(part_bx, land_of_bx, x, NX, up_x, down_x, send_sems, recv_sems, 9)
+    ring_ax = ReduceRing(part_ax, land_of_ax, x, NX, up_x, down_x, send_sems, recv_sems, 13)
+    ring_bz = ReduceRing(part_bz, land_of_bz, z, NZ, up_z, down_z, send_sems, recv_sems, 17)
+    ring_az.start(0)
+    ring_bx.start(0)
+    ring_az.arrive(0)
+    ring_az.start(1)
+    ring_bx.arrive(0)
+    ring_bx.start(1)
+    ring_az.arrive(1)
+    ring_az.start(2)
+    ring_az.arrive(2)
+    ring_az.start(3)
+    ring_bx.arrive(1)
+    ring_bz.start(0)
+    ring_bz.arrive(0)
+    ring_bz.start(1)
+    ring_az.arrive(3)
+    ring_ax.start(0)
+    ring_bz.arrive(1)
+    ring_bz.start(2)
+    ring_ax.arrive(0)
+    ring_ax.start(1)
+    ring_bz.arrive(2)
+    ring_bz.start(3)
+    ring_ax.arrive(1)
+    ring_bz.arrive(3)
+    last = send(
+        slots.at[z, NY * x + 1 - y], land_y, send_sems.at[0], recv_sems.at[0], other_y
+    )
+    last.wait_recv()
+    total[...] = slots[z, NY * x + y].astype(jnp.float32) + land_y[...].astype(jnp.float32)
+    last.wait_send()
+    for ring in (ring_az, ring_bx, ring_ax, ring_bz):
+        ring.finish()
+
+
+def reduce_grads(attn, small, left, right):
+    return pl.pallas_call(
+        reduce_kernel,
+        out_shape=jax.ShapeDtypeStruct((PACK, LANE), jnp.float32),
+        in_specs=vmem_specs(6),
+        out_specs=pl.BlockSpec(memory_space=pltpu.VMEM),
+        scratch_shapes=[
+            pltpu.VMEM((NZ, PLANE, PACK, LANE), jnp.bfloat16),
+            pltpu.VMEM((2, 4, PLANE, SPLIT, LANE), jnp.bfloat16),
+            pltpu.VMEM((2, 2, NZ, NY, PACK - SPLIT, LANE), jnp.bfloat16),
+            pltpu.VMEM((2, 2, NY, SPLIT, LANE), jnp.bfloat16),
+            pltpu.VMEM((2, 4, NY, PACK - SPLIT, LANE), jnp.bfloat16),
+            pltpu.VMEM((PACK, LANE), jnp.bfloat16),
+            pltpu.SemaphoreType.DMA((25,)),
+            pltpu.SemaphoreType.DMA((25,)),
+        ],
+        compiler_params=pltpu.CompilerParams(
+            collective_id=1, has_side_effects=True, vmem_limit_bytes=60_000_000
+        ),
+    )(attn, small, left, right, spread_matrix(4, 48).T, spread_matrix(1, 16).T)
+
+
+def muon_kernel(
+    look, narrow, wide, mask_ref, result,
+    arrived, matrix, finished, gram, local_sems, send_sems, recv_sem, back_sem, ret_sems,
+):
+    me = lax.axis_index("dp")
+    shift = lax.rem(lax.axis_index("tensor"), 2) * 4
+
+    def owner_of(block):
+        return block * PLANE + shift
+
+    own = lax.rem(me, PLANE) == shift
+    my_block = me // PLANE
+    barrier = pltpu.get_barrier_semaphore()
+    devices = NZ * PLANE
+
+    def hail(target):
+        pl.semaphore_signal(barrier, inc=1, device_id={"dp": target}, device_id_type=MESH_ID)
+
+    for block in range(BLOCKS):
+
+        @pl.when(me != owner_of(block))
+        def _():
+            hail(owner_of(block))
+
+    @pl.when(own)
+    def _():
+        def hail_one(target, carry):
+            @pl.when(target != me)
+            def _():
+                hail(target)
+
+            return carry
+
+        lax.fori_loop(0, devices, hail_one, 0)
+        pl.semaphore_wait(barrier, BLOCKS - 1 + devices - 1)
+
+    @pl.when(jnp.logical_not(own))
+    def _():
+        pl.semaphore_wait(barrier, BLOCKS)
+
+    def outgoing(block):
+        return pltpu.make_async_remote_copy(
+            src_ref=look.at[block],
+            dst_ref=arrived.at[me],
+            send_sem=send_sems.at[block],
+            recv_sem=recv_sem,
+            device_id={"dp": owner_of(block)},
+            device_id_type=MESH_ID,
+        )
+
+    for block in range(BLOCKS):
+
+        @pl.when(me != owner_of(block))
+        def _():
+            outgoing(block).start()
+
+    @pl.when(own)
+    def _():
+        keep = pltpu.make_async_copy(look.at[my_block], arrived.at[me], local_sems.at[0])
+        keep.start()
+        keep.wait()
+        pltpu.make_async_remote_copy(
+            src_ref=arrived.at[pl.ds(0, devices - 1)],
+            dst_ref=arrived.at[pl.ds(0, devices - 1)],
+            send_sem=back_sem,
+            recv_sem=recv_sem,
+            device_id={"dp": me},
+            device_id_type=MESH_ID,
+        ).wait_recv()
+
+        def compact(plane, carry):
+            picked = arrived[pl.ds(plane * PLANE, PLANE)].reshape(PLANE * 16, 384)
+            rows = pl.ds(pl.multiple_of(plane * PLANE * ROW, 32), PLANE * ROW)
+            matrix[rows, :] = jnp.dot(
+                narrow[...], picked, preferred_element_type=jnp.float32
+            ).astype(jnp.bfloat16)
+            return carry
+
+        lax.fori_loop(0, NZ, compact, 0)
+        joined = my_block >= 2
+        mask = jnp.maximum(mask_ref[...], joined.astype(jnp.float32))
+        raw = matrix[...].astype(jnp.float32)
+        per_col = jnp.sum(raw * raw, axis=0, keepdims=True)
+        square_sum = jnp.dot(
+            jnp.broadcast_to(per_col, (8, 384)), mask, preferred_element_type=jnp.float32,
+            precision=lax.Precision.HIGHEST,
+        )[0:1]
+        matrix[...] = (raw * lax.rsqrt(square_sum + EPSILON)).astype(jnp.bfloat16)
+        for _ in range(NS_ITERS):
+            current = matrix[...]
+            gram_mat = (contract_rows(current, current) * mask).astype(jnp.bfloat16)
+            square = jnp.dot(gram_mat, gram_mat, preferred_element_type=jnp.float32)
+            gram[...] = (
+                NEWTON_B * gram_mat.astype(jnp.float32) + NEWTON_C * square
+            ).astype(jnp.bfloat16)
+            matrix[...] = (
+                NEWTON_A * current.astype(jnp.float32)
+                + jnp.dot(current, gram[...], preferred_element_type=jnp.float32)
+            ).astype(jnp.bfloat16)
+
+        def expand(plane, carry):
+            rows = pl.ds(pl.multiple_of(plane * PLANE * ROW, 32), PLANE * ROW)
+            finished[pl.ds(plane * PLANE, PLANE)] = (
+                jnp.dot(wide[...], matrix[rows, :], preferred_element_type=jnp.float32)
+                .astype(jnp.bfloat16)
+                .reshape(PLANE, 16, 384)
+            )
+            return carry
+
+        lax.fori_loop(0, NZ, expand, 0)
+
+        def give(target, carry):
+            @pl.when(target != me)
+            def _():
+                pltpu.make_async_remote_copy(
+                    src_ref=finished.at[target],
+                    dst_ref=result.at[my_block],
+                    send_sem=back_sem,
+                    recv_sem=ret_sems.at[my_block],
+                    device_id={"dp": target},
+                    device_id_type=MESH_ID,
+                ).start()
+
+            return carry
+
+        lax.fori_loop(0, devices, give, 0)
+        stay = pltpu.make_async_copy(finished.at[me], result.at[my_block], local_sems.at[1])
+        stay.start()
+        stay.wait()
+        pltpu.make_async_remote_copy(
+            src_ref=finished.at[pl.ds(0, devices - 1)],
+            dst_ref=finished.at[pl.ds(0, devices - 1)],
+            send_sem=back_sem,
+            recv_sem=recv_sem,
+            device_id={"dp": me},
+            device_id_type=MESH_ID,
+        ).wait_send()
+
+    for block in range(BLOCKS):
+
+        @pl.when(me != owner_of(block))
+        def _():
+            outgoing(block).wait_send()
+            pltpu.make_async_remote_copy(
+                src_ref=result.at[block],
+                dst_ref=result.at[block],
+                send_sem=send_sems.at[block],
+                recv_sem=ret_sems.at[block],
+                device_id={"dp": owner_of(block)},
+                device_id_type=MESH_ID,
+            ).wait_recv()
+
+
+def half_mask():
+    side = np.arange(384) // 192
+    return jnp.asarray(side[:, None] == side[None, :], jnp.float32)
+
+
+def muon_step(look):
+    return pl.pallas_call(
+        muon_kernel,
+        out_shape=jax.ShapeDtypeStruct((BLOCKS, 16, 384), jnp.bfloat16),
+        in_specs=vmem_specs(4),
+        out_specs=pl.BlockSpec(memory_space=pltpu.VMEM),
+        scratch_shapes=[
+            pltpu.VMEM((NZ * PLANE, 16, 384), jnp.bfloat16),
+            pltpu.VMEM((768, 384), jnp.bfloat16),
+            pltpu.VMEM((NZ * PLANE, 16, 384), jnp.bfloat16),
+            pltpu.VMEM((384, 384), jnp.bfloat16),
+            pltpu.SemaphoreType.DMA((2,)),
+            pltpu.SemaphoreType.DMA((BLOCKS,)),
+            pltpu.SemaphoreType.DMA,
+            pltpu.SemaphoreType.DMA,
+            pltpu.SemaphoreType.DMA((BLOCKS,)),
+        ],
+        compiler_params=pltpu.CompilerParams(
+            collective_id=2, has_side_effects=True, vmem_limit_bytes=60_000_000
+        ),
+    )(look, spread_matrix(1, 16), spread_matrix(1, 16).T, half_mask())
+
+
+def pack_blocks(attn, left, right):
+    pairs = jnp.transpose(
+        jnp.transpose(attn, (1, 0, 2)).reshape(ROW, 2, 384), (1, 0, 2)
+    )
+    stacked = jnp.concatenate([pairs, left, right], axis=0)
+    return jnp.pad(stacked, ((0, 0), (0, 16 - ROW), (0, 0)))
 
 
 def norm_forward(row_data, gain_row):
@@ -144,30 +752,6 @@
         grad_keys.reshape(row_total, full_width),
         grad_values.reshape(row_total, full_width),
     )
-
-
-def orthogonalize(matrix):
-    current = settle(matrix * lax.rsqrt(jnp.sum(matrix * matrix) + EPSILON))
-    for iteration in range(NS_ITERS):
-        gram_mat = settle(contract_rows(current, current))
-        square = jnp.dot(gram_mat, gram_mat, preferred_element_type=jnp.float32)
-        poly_mat = round_half(NEWTON_B * to_single(gram_mat) + NEWTON_C * square)
-        current = settle(
-            NEWTON_A * to_single(current)
-            + jnp.dot(current, poly_mat, preferred_element_type=jnp.float32)
-        )
-    return current
-
-
-def orthogonalize_attention(block_mat):
-    rows_all, slot_width = block_mat.shape
-    sub_blocks = jnp.transpose(block_mat.reshape(rows_all, 2, slot_width // 2), (1, 0, 2))
-    solved = jnp.stack([orthogonalize(sub_blocks[which_mat]) for which_mat in range(2)])
-    return jnp.transpose(solved, (1, 0, 2)).reshape(rows_all, slot_width)
-
-
-def empty_block(block_mat):
-    return jnp.zeros(block_mat.shape, jnp.bfloat16)
 
 
 def shards(
@@ -188,17 +772,17 @@
     image_count, seq_len, model_width = inputs.shape
     dp_count = lax.axis_size("dp")
     row_count = image_count * seq_len
-    small_plane = jnp.zeros((1, norm_gains.shape[1], attn_mats.shape[2]), jnp.bfloat16)
-    small_plane = small_plane.at[0, :, :2].set(round_half(norm_gains).T)
-    small_plane = small_plane.at[0, :, 2 : 2 + EF].set(round_half(router))
-    packed = lax.all_gather(
-        jnp.concatenate([round_half(attn_mats), small_plane], axis=0), "dp", axis=1, tiled=True
-    )
-    attn_half = packed[:4]
-    gains_half = packed[4, :, :2].T
-    router_half = packed[4, :, 2 : 2 + EF]
-    in_half = lax.all_gather(round_half(expert_in), "dp", axis=1, tiled=True)
-    out_half = lax.all_gather(round_half(expert_out), "dp", axis=1, tiled=True)
+    attn_all, small_half, in_half, out_half = gather_weights(
+        pack_rows(
+            round_half(attn_mats),
+            jnp.concatenate([round_half(norm_gains).T, round_half(router)], axis=1),
+            round_half(expert_in),
+            round_half(expert_out),
+        )
+    )
+    attn_half = jnp.stack([attn_all[:, 192 * which : 192 * which + 192] for which in range(4)])
+    gains_half = small_half[:, :2].T
+    router_half = small_half[:, 2 : 2 + EF]
     gain_one = to_single(gains_half[0])
     gain_two = to_single(gains_half[1])
     row_in = inputs.reshape(row_count, model_width)
@@ -257,13 +841,14 @@
     grad_queries, grad_keys, grad_values = attention_backward(
         grad_attn_rows, queries, key_rows, value_rows, log_total
     )
-    grad_attn = jnp.stack(
+    grad_attn = jnp.concatenate(
         [
             contract_rows(normed_one, grad_queries),
             contract_rows(normed_one, grad_keys),
             contract_rows(normed_one, grad_values),
             grad_proj_out,
-        ]
+        ],
+        axis=1,
     )
     grad_normed_one_part = (
         contract_cols(grad_queries, attn_half[0])
@@ -277,24 +862,10 @@
     grad_inputs_rows = grad_middle + grad_in_norm
     gains_cols = jnp.stack([grad_gain_one, grad_gain_two], axis=1)
     small_cols = jnp.concatenate([gains_cols, grad_router], axis=1)
-    got_attn, got_in, got_out, got_small = (
-        lax.all_to_all(
-            grad_attn.astype(jnp.bfloat16), "dp", split_axis=1, concat_axis=0, tiled=True
-        ).astype(grad_attn.dtype),
-        lax.all_to_all(
-            grad_in.astype(jnp.bfloat16), "dp", split_axis=1, concat_axis=0, tiled=True
-        ).astype(grad_in.dtype),
-        lax.all_to_all(
-            grad_out.astype(jnp.bfloat16), "dp", split_axis=1, concat_axis=0, tiled=True
-        ).astype(grad_out.dtype),
-        lax.all_to_all(
-            small_cols[None].astype(jnp.bfloat16), "dp", split_axis=1, concat_axis=0, tiled=True
-        ).astype(jnp.float32),
-    )
-    sum_attn = fold_sources(got_attn, dp_count)
-    sum_in = fold_sources(got_in, dp_count)
-    sum_out = fold_sources(got_out, dp_count)
-    sum_small = fold_sources(got_small, dp_count)[0]
+    small_wide = jnp.pad(round_half(small_cols), ((0, 0), (0, LANE - small_cols.shape[1])))
+    sum_attn, sum_small, sum_in, sum_out = unpack_rows(
+        reduce_grads(round_half(grad_attn), small_wide, round_half(grad_in), round_half(grad_out))
+    )
     sum_gains = sum_small[:, :2].T
     sum_router = sum_small[:, 2:]
     small_step = SMALL_RATE / math.sqrt(image_count * dp_count * seq_len)
@@ -308,42 +879,11 @@
     look_attn = sum_attn + MOMENTUM * moment_attn_new
     look_in = sum_in + MOMENTUM * moment_in_new
     look_out = sum_out + MOMENTUM * moment_out_new
-    shard_rows = look_in.shape[1]
-    slot_width = look_in.shape[2]
-    blocks = 2 * EF + 2
-    per_owner = -(-blocks // dp_count)
-    slot_count = dp_count * per_owner
-    slot_list = list(range(blocks))
-    block_list = [
-        slot_list.index(slot_number) if slot_number in slot_list else blocks
-        for slot_number in range(slot_count)
+    updates = to_single(muon_step(pack_blocks(*map(round_half, (look_attn, look_in, look_out)))))[
+        :, :ROW
     ]
-    slot_of_block = np.array(slot_list)
-    block_of_slot = np.array(block_list)
-    kind_of_slot = np.where(block_of_slot < 2, 0, np.where(block_of_slot < blocks, 1, 2))
-    attn_slots = jnp.transpose(
-        jnp.transpose(look_attn, (1, 0, 2)).reshape(shard_rows, 2, slot_width), (1, 0, 2)
-    )
-    stacked = jnp.concatenate(
-        [attn_slots, look_in, look_out, jnp.zeros((1, shard_rows, slot_width), jnp.float32)], axis=0
-    )
-    outgoing = jnp.take(stacked, jnp.asarray(block_of_slot, dtype=jnp.int32), axis=0)
-    arrived = lax.all_to_all(
-        for_sending(outgoing), "dp", split_axis=0, concat_axis=1, tiled=True
-    ).astype(outgoing.dtype)
-    own_index = lax.axis_index("dp")
-    kind_table = jnp.asarray(kind_of_slot, dtype=jnp.int32)
-    kind_now = kind_table[own_index * per_owner + 0]
-    results = [
-        lax.switch(kind_now, [orthogonalize_attention, orthogonalize, empty_block], arrived[0])
-    ]
-    finished = jnp.stack(results)
-    returned = lax.all_to_all(
-        for_sending(finished), "dp", split_axis=1, concat_axis=0, tiled=True
-    ).astype(finished.dtype)
-    updates = to_single(jnp.take(returned, jnp.asarray(slot_of_block, dtype=jnp.int32), axis=0))
     update_attn = jnp.transpose(
-        jnp.transpose(updates[0:2], (1, 0, 2)).reshape(shard_rows, 4, slot_width // 2), (1, 0, 2)
+        jnp.transpose(updates[0:2], (1, 0, 2)).reshape(ROW, 4, 192), (1, 0, 2)
     )
     attn_new = attn_mats - MUON_RATE * update_attn
     in_new = expert_in - MUON_RATE * updates[2 : EF + 2]

time: 861 us -> 367 us (0.43); the launches traced: 850 us -> 366 us
  waiting for transfers between devices: 599 us -> 114 us
  Pallas kernels: 0 us -> 156 us
  starting transfers between devices: 71.1 us -> 0.3 us
  local copies, waits for them, and re-layouts: 75.5 us -> 25.7 us
  other arithmetic: 45.9 us -> 22.1 us
  loops' own time: 8.68 us -> 0 us
    all_gather x3 -> x0, waiting for transfers between devices: 356 us -> none  [the longest x1 121 us: shards(): in_half = lax.all_gather(round_half(expert_in), 'dp', axis=1, tiled=True)]
    pallas_call x0 -> x3, Pallas kernels: none -> 156 us  [the longest x1 61.2 us: reduce_grads(): pl.pallas_call(reduce_kernel, out_shape=jax.ShapeDtypeStruct((PACK, LANE)...]
    all_to_all x6 -> x0, waiting for transfers between devices: 125 us -> none  [the longest x1 48.2 us: shards(): lax.all_to_all(grad_in.astype(jnp.bfloat16), 'dp', split_axis=1, concat_a...]
    all_to_all x6 -> x0, starting transfers between devices: 70.7 us -> none  [the longest x1 13.1 us: shards(): lax.all_to_all(grad_attn.astype(jnp.bfloat16), 'dp', split_axis=1, concat...]
    convert_element_type x5 -> x0, local copies, waits for them, and re-layouts: 17.7 us -> none  [the longest x3 9.61 us: shards(): got_attn, got_in, got_out, got_small = (lax.all_to_all(grad_attn.astype(j...]
    slice x5 -> x3, local copies, waits for them, and re-layouts: 13.9 us -> 0.02 us  [the longest x1 0.01 us: unpack_rows(): right = jnp.transpose(flat[:, 2048:3200].reshape(ROW, EF, 384), (1, 0, 2))]
    unnamed x134 -> x87, local copies, waits for them, and re-layouts: 23.2 us -> 11.6 us
    another operation x1 -> x0, loops' own time: 8.68 us -> none  [shards(): lax.switch(kind_now, [orthogonalize_attention, orthogonalize, empty_block...]
  transfers between devices with their start and end apart: 12 -> 3, of which waited for: 10 -> 3; matrix products, arithmetic and copies ran while one was open for 9% -> 5% of each run, Pallas kernels for 0% -> 0%
where the time goes in v2:
time: 367 us; the launch traced here: 366 us
  Pallas kernels  156 us (43%)
  waiting for transfers between devices  114 us (31%)
  matrix products  33.7 us (9%)
  local copies, waits for them, and re-layouts  25.7 us (7%)
  other arithmetic  22.1 us (6%)
  between operations  14.5 us (4%)
    pallas_call x1, Pallas kernels, reduce_grads(): pl.pallas_call(reduce_kernel, out_shape=jax.ShapeDtypeStruct((PACK, LANE)...  61.2 us
    pallas_call x1, Pallas kernels, gather_weights(): pl.pallas_call(gather_kernel, out_shape=[jax.ShapeDtypeStruct(shape, jnp....  58.1 us
    psum x1, waiting for transfers between devices, shards(): lax.psum(moe_part.astype(jnp.bfloat16), 'tensor').astype(jnp.float32)  40.8 us
    psum x1, waiting for transfers between devices, shards(): lax.psum(attn_part.astype(jnp.bfloat16), 'tensor').astype(jnp.float32)  38.3 us
    pallas_call x1, Pallas kernels, muon_step(): pl.pallas_call(muon_kernel, out_shape=jax.ShapeDtypeStruct((BLOCKS, 16, 3...  36.3 us
    psum x1, waiting for transfers between devices, shards(): lax.psum(jnp.concatenate([grad_normed_part, grad_choice_part], axis=1).as...  34.4 us
    unnamed x87, local copies, waits for them, and re-layouts  11.6 us
  transfers between devices with their start and end apart: 3, of which 3 were waited for; matrix products, arithmetic and copies ran while one was open for 5% of the time, Pallas kernels for 0%

profile of v2, /device:TPU:94, one launch (start us, length us, event | category | flops | bytes accessed | tf_op | source)
XLA Modules:
  0.0 365.5 jit_solution(17543070515696061658)
XLA Ops:
  11.2 58.1 %shard_map.323 = (bf16[768,768]{1,0:T(8,128)(2,1)}, bf16[768,128]{1,0:T(8,128)(2,1)}, bf16[3,768,384]{2,1,0:T(8,128)(2,1)}, bf16[3,768,384]{2,1,0:T(8,128)(2,1)}) custom-call(bf16[304,128]{1,0:T(8,128)(2,1)} %pad.17.shard, bf16[384,384]{1,0:T(8,128)(2,1)} %constant.52.clone.four, bf16[96,128]{1,0:T(8,128)(2,1)} %constant.53.clone.one.narrow), custom_call_target="tpu_custom_call" | custom-call | tf_op jit(solution)/shard_map/pallas_call | solution.py:249
  75.0 2.1 copy.243
  77.9 1.7 multiply_convert_fusion.6
  79.6 38.3 %all-reduce.9.cloned.1.call-done = bf16[197,768]{0,1:T(8,128)(2,1)} async-done(((bf16[197,768]{0,1:T(8,128)(2,1)}), bf16[197,768]{0,1:T(8,128)(2,1)}) %all-reduce.9.cloned.1.call-update) | async-done | bytes 302608 | tf_op jit(solution)/shard_map/psum | solution.py:794
  120.5 1.7 multiply_convert_fusion.3
  122.4 2.6 fusion.1
  127.4 1.7 multiply_reduce_fusion
  130.3 2.9 convert_bitcast_fusion.left
  133.2 1.9 copy.242
  135.1 3.2 convolution_convert_fusion.right
  138.3 34.4 %all-reduce.11.cloned.1.call-done = bf16[197,770]{0,1:T(8,128)(2,1)} async-done(((bf16[197,770]{0,1:T(8,128)(2,1)}), bf16[197,770]{0,1:T(8,128)(2,1)}) %all-reduce.11.cloned.1.call-update) | async-done | bytes 303396 | tf_op jit(solution)/shard_map/psum | solution.py:824
  175.6 1.6 convolution_convert_fusion.9
  179.2 2.3 convolution_convert_fusion.7
  181.6 2.3 convolution_convert_fusion.8
  185.3 2.1 convolution_convert_fusion.5
  191.9 1.9 copy.254
  193.7 1.9 copy.255
  196.7 1.9 copy.256
  198.5 2.8 pad_maximum_fusion.attn
  201.5 40.8 %all-reduce.13.cloned.1.call-done = (bf16[197,768]{0,1:T(8,128)(2,1)}, bf16[197,768]{0,1:T(8,128)(2,1)}) async-done(((bf16[197,768]{0,1:T(8,128)(2,1)}, bf16[197,768]{0,1:T(8,128)(2,1)}), (bf16[197,768]{0,1:T(8,128)(2,1)}, bf16[197,768]{0,1:T(8,128)(2,1)})) %all-reduce.13.cloned.1.call-update) | async-done | bytes 605200 | tf_op jit(solution)/shard_map/psum | solution.py:810
  242.4 2.0 fusion.27
  245.3 61.2 %shard_map.324 = f32[304,128]{1,0:T(8,128)} custom-call(bf16[768,768]{1,0:T(8,128)(2,1)} %pad_maximum_fusion.attn, bf16[768,128]{1,0:T(8,128)(2,1)} %pad.18.small, bf16[3,768,384]{2,1,0:T(8,128)(2,1)} %convert_bitcast_fusion.left, bf16[3,768,384]{2,1,0:T(8,128)(2,1)} %convolution_convert_fusion.right, bf16[384,384]{1,0:T(8,128)(2,1)} %constant.76.four, ...), custom_call_target="tpu_custom_call" | custom-call | tf_op jit(solution)/shard_map/pallas_call | solution.py:459
  310.3 1.6 add_convert_fusion
  312.5 36.3 %shard_map.325 = bf16[8,16,384]{2,1,0:T(8,128)(2,1)} custom-call(bf16[8,16,384]{2,1,0:T(8,128)(2,1)} %fusion.64.look, bf16[96,128]{1,0:T(8,128)(2,1)} %constant.53.clone.one.narrow, bf16[128,96]{1,0:T(8,128)(2,1)} %constant.77.one.wide, f32[384,384]{1,0:T(8,128)} %constant.54.clone.mask_ref), custom_call_target="tpu_custom_call" | custom-call | tf_op jit(solution)/shard_map/pallas_call | solution.py:639
  (182 shorter events, 43.8 us)
Async XLA Ops:
  7.2 2.7 copy-start.15
  7.2 2.8 copy-start.13
  7.2 2.9 copy-start.17
  7.2 3.0 copy-start.26
  7.2 3.0 copy-start.29
  7.3 110.6 %all-reduce.9.cloned.1.call-start = ((), (), s32[]{:S(2)}) async-start(), calls=%async_computation | async-start | bytes 786432 | tf_op jit(solution)/shard_map/psum | solution.py:794
  9.9 232.4 %copy-start.25 = (f32[197]{0:T(256)}, f32[197]{0:T(256)S(1)}, u32[]{:S(2)}) copy-start(f32[197]{0:T(256)S(1)} %add_rsqrt_fusion.1) | copy-start | bytes 2368
  72.7 4.5 %copy-start.28 = (f32[12,3]{0,1:T(4,128)S(1)}, f32[12,3]{0,1:T(4,128)}, u32[]{:S(2)}) copy-start(f32[12,3]{0,1:T(4,128)} %param.29) | copy-start | bytes 436
  73.8 98.8 %all-reduce.11.cloned.1.call-start = ((), (), s32[]{:S(2)}) async-start(), calls=%async_computation.1 | async-start | bytes 794624 | tf_op jit(solution)/shard_map/psum | solution.py:824
  122.4 3.4 copy-start.34
  130.0 112.3 %all-reduce.13.cloned.1.call-start = ((), (), s32[]{:S(2)}) async-start(), calls=%async_computation.2 | async-start | bytes 1572864 | tf_op jit(solution)/shard_map/psum | solution.py:810
  172.6 2.7 copy-start.4
  183.9 3.5 copy-start.1
  183.9 3.5 copy-start.10
  183.9 4.5 %copy-start.3 = (bf16[768,768]{1,0:T(8,128)(2,1)S(1)}, bf16[768,768]{1,0:T(8,128)(2,1)}, u32[]{:S(2)}) copy-start(bf16[768,768]{1,0:T(8,128)(2,1)} %get-tuple-element.22) | copy-start | bytes 3538948
  185.3 3.4 copy-start.7
  306.5 3.0 copy-start.22
  307.6 42.2 %copy-start.14 = (f32[3,12,384]{2,1,0:T(8,128)S(1)}, f32[3,12,384]{2,1,0:T(8,128)}, u32[]{:S(2)}) copy-start(f32[3,12,384]{2,1,0:T(8,128)} %param.26) | copy-start | bytes 165892
  307.6 42.1 %copy-start.16 = (f32[3,12,384]{2,1,0:T(8,128)S(1)}, f32[3,12,384]{2,1,0:T(8,128)}, u32[]{:S(2)}) copy-start(f32[3,12,384]{2,1,0:T(8,128)} %param.25) | copy-start | bytes 165892
  307.8 42.8 %copy-start.18 = (f32[4,12,192]{2,0,1:T(4,128)S(1)}, f32[4,12,192]{2,0,1:T(4,128)}, u32[]{:S(2)}) copy-start(f32[4,12,192]{2,0,1:T(4,128)} %param.23) | copy-start | bytes 110596
  307.8 43.4 %copy-start.23 = (f32[12,3]{1,0:T(8,128)S(1)}, f32[12,3]{1,0:T(8,128)}, u32[]{:S(2)}) copy-start(f32[12,3]{1,0:T(8,128)} %copy.266) | copy-start | bytes 436
  307.8 46.2 %copy-start.6 = (bf16[197,768]{0,1:T(8,128)(2,1)S(1)}, bf16[197,768]{0,1:T(8,128)(2,1)}, u32[]{:S(2)}) copy-start(bf16[197,768]{0,1:T(8,128)(2,1)} %get-tuple-element.155) | copy-start | bytes 907780
  308.0 46.1 %copy-start.19 = (f32[12,4,192]{2,1,0:T(4,128)}, f32[12,4,192]{2,1,0:T(4,128)S(1)}, u32[]{:S(2)}) copy-start(f32[12,4,192]{2,1,0:T(4,128)S(1)} %reshape.304) | copy-start | bytes 110596
  353.4 5.0 %copy-start.27 = (f32[12,2]{0,1:T(2,128)}, f32[12,2]{0,1:T(2,128)S(1)}, u32[]{:S(2)}) copy-start(f32[12,2]{0,1:T(2,128)S(1)} %copy.291) | copy-start | bytes 292
  (14 other events, 23.5 us)
Sparse Core Ops, SparseCore 0:
  74.0 43.8 all-reduce.8
  130.2 42.4 all-reduce.10
  195.8 46.5 all-reduce.12

commit v3 on v2

--- a/solution.py
+++ b/solution.py
@@ -666,92 +666,295 @@
     return jnp.pad(stacked, ((0, 0), (0, 16 - ROW), (0, 0)))
 
 
-def norm_forward(row_data, gain_row):
-    center = row_data - jnp.mean(row_data, axis=-1, keepdims=True)
-    inv_std = lax.rsqrt(jnp.mean(center * center, axis=-1, keepdims=True) + EPSILON)
-    normal = center * inv_std
-    return (normal, inv_std, round_half(normal * gain_row))
-
-
-def norm_backward(grad_result, normal, inv_std, gain_row):
+TOKENS = 197
+PAD = 208
+WIDE = 768
+HALF = 384
+ERF_TOP = (
+    0.00022905065861350646, 0.0034082910107109506, 0.050955695062380861,
+    0.18520832239976145, 1.128379143519084,
+)
+ERF_BOTTOM = (
+    -1.1791602954361697e-7, 0.000023547966471313185, 0.0010179625278914885,
+    0.014070470171167667, 0.11098505178285362, 0.49746925110067538, 1.0,
+)
+
+
+def rows_dot(left_mat, right_mat):
+    return jnp.dot(left_mat, right_mat, preferred_element_type=jnp.float32)
+
+
+def mean_of(value):
+    return jnp.sum(value, axis=-1, keepdims=True) * (1.0 / WIDE)
+
+
+def norm_parts(row_data):
+    center = row_data - mean_of(row_data)
+    inv_std = lax.rsqrt(mean_of(center * center) + EPSILON)
+    return center * inv_std, inv_std
+
+
+def norm_pull(grad_result, normal, inv_std, gain_row):
     scaled = grad_result * gain_row
-    grad_data = inv_std * (
-        scaled
-        - jnp.mean(scaled, axis=-1, keepdims=True)
-        - normal * jnp.mean(scaled * normal, axis=-1, keepdims=True)
-    )
-    return (grad_data, jnp.sum(grad_result * normal, axis=0))
-
-
-def gelu_value(pre_act):
-    return 0.5 * pre_act * (1.0 + lax.erf(pre_act * ROOT_HALF))
-
-
-def gelu_slope(pre_act):
-    return 0.5 * (1.0 + lax.erf(pre_act * ROOT_HALF)) + pre_act * INV_ROOT_TAU * jnp.exp(
-        -0.5 * pre_act * pre_act
-    )
-
-
-def score_table(queries, key_rows):
-    return jnp.einsum("bqhd,bkhd->bhqk", queries, key_rows, preferred_element_type=jnp.float32) * (
-        1.0 / math.sqrt(HEAD_DIM)
-    )
-
-
-def attention_forward(normed, mats_half, image_count, seq_len):
-    head_count = mats_half.shape[2] // HEAD_DIM
-
-    def project(which_mat):
-        return round_half(
-            jnp.dot(normed, mats_half[which_mat], preferred_element_type=jnp.float32)
-        ).reshape(image_count, seq_len, head_count, HEAD_DIM)
-
-    queries = project(0)
-    key_rows = project(1)
-    value_rows = project(2)
-    scores = score_table(queries, key_rows)
-    row_peak = jnp.max(scores, axis=-1, keepdims=True)
-    log_total = row_peak + jnp.log(jnp.sum(jnp.exp(scores - row_peak), axis=-1, keepdims=True))
-    prob_half = round_half(jnp.exp(scores - log_total))
-    attn_rows = round_half(
-        jnp.einsum("bhqk,bkhd->bqhd", prob_half, value_rows, preferred_element_type=jnp.float32)
-    )
-    return (
-        queries,
-        key_rows,
-        value_rows,
-        log_total,
-        attn_rows.reshape(image_count * seq_len, head_count * HEAD_DIM),
-    )
-
-
-def attention_backward(grad_attn_rows, queries, key_rows, value_rows, log_total):
-    image_count, seq_len, head_count, head_size = queries.shape
-    grad_heads = grad_attn_rows.reshape(image_count, seq_len, head_count, head_size)
-    prob_full = jnp.exp(score_table(queries, key_rows) - log_total)
-    prob_half = round_half(prob_full)
-    grad_prob = jnp.einsum(
-        "bqhd,bkhd->bhqk", grad_heads, value_rows, preferred_element_type=jnp.float32
-    )
-    grad_values = round_half(
-        jnp.einsum("bhqk,bqhd->bkhd", prob_half, grad_heads, preferred_element_type=jnp.float32)
-    )
-    spread = jnp.sum(prob_full * grad_prob, axis=-1, keepdims=True)
-    grad_scores = round_half(prob_full * (grad_prob - spread) * (1.0 / math.sqrt(HEAD_DIM)))
-    grad_queries = round_half(
-        jnp.einsum("bhqk,bkhd->bqhd", grad_scores, key_rows, preferred_element_type=jnp.float32)
-    )
-    grad_keys = round_half(
-        jnp.einsum("bhqk,bqhd->bkhd", grad_scores, queries, preferred_element_type=jnp.float32)
-    )
-    row_total = image_count * seq_len
-    full_width = head_count * head_size
-    return (
-        grad_queries.reshape(row_total, full_width),
-        grad_keys.reshape(row_total, full_width),
-        grad_values.reshape(row_total, full_width),
-    )
+    return inv_std * (scaled - mean_of(scaled) - normal * mean_of(scaled * normal))
+
+
+class TensorSum:
+    def __init__(self, part, land_core, land_chip, final, send_sems, recv_sems, base):
+        self.part, self.land_core, self.land_chip, self.final = part, land_core, land_chip, final
+        self.send_sems, self.recv_sems, self.base = send_sems, recv_sems, base
+        mine = lax.axis_index("tensor")
+        self.core = lax.rem(mine, 2)
+        self.other_core = mine + 1 - 2 * self.core
+        self.other_chip = lax.rem(mine + 2, 4)
+        self.copies = []
+
+    def put(self, source, landing, target):
+        slot = self.base + len(self.copies)
+        copy = pltpu.make_async_remote_copy(
+            src_ref=source,
+            dst_ref=landing,
+            send_sem=self.send_sems.at[slot],
+            recv_sem=self.recv_sems.at[slot],
+            device_id={"tensor": target},
+            device_id_type=MESH_ID,
+        )
+        copy.start()
+        self.copies.append(copy)
+
+    def begin(self):
+        self.put(self.part.at[1 - self.core], self.land_core, self.other_core)
+
+    def across(self):
+        self.copies[0].wait_recv()
+        mine = self.part.at[self.core]
+        mine[...] = (
+            mine[...].astype(jnp.float32) + self.land_core[...].astype(jnp.float32)
+        ).astype(jnp.bfloat16)
+        self.put(mine, self.land_chip, self.other_chip)
+
+    def share(self):
+        self.copies[1].wait_recv()
+        mine = self.final.at[self.core]
+        mine[...] = (
+            self.part[self.core].astype(jnp.float32) + self.land_chip[...].astype(jnp.float32)
+        ).astype(jnp.bfloat16)
+        self.put(mine, mine, self.other_core)
+
+    def done(self):
+        self.copies[2].wait_recv()
+
+    def value(self):
+        return jnp.concatenate(
+            [self.final[0][:, :HALF], self.final[1][:, :HALF]], axis=1
+        ).astype(jnp.float32)
+
+    def finish(self):
+        for copy in self.copies:
+            copy.wait_send()
+
+
+def main_kernel(
+    inputs, cotangent, routes, attn_half, small_half, in_half, out_half,
+    output, grad_inputs, grad_attn, grad_small, grad_in, grad_out,
+    rows_in, rows_cot, prob_all, hidden_all, grad_pre_all,
+    part_a, part_b, part_c, part_d, core_a, core_b, core_c, core_d,
+    chip_a, chip_b, chip_c, chip_d, final_a, final_b, final_c, final_d,
+    send_sems, recv_sems,
+):
+    mine = lax.axis_index("tensor")
+    barrier = pltpu.get_barrier_semaphore()
+    for target in (mine + 1 - 2 * lax.rem(mine, 2), lax.rem(mine + 2, 4)):
+        pl.semaphore_signal(barrier, inc=1, device_id={"tensor": target}, device_id_type=MESH_ID)
+    pl.semaphore_wait(barrier, 2)
+
+    sum_attn = TensorSum(part_a, core_a, chip_a, final_a, send_sems, recv_sems, 0)
+    sum_grad = TensorSum(part_b, core_b, chip_b, final_b, send_sems, recv_sems, 3)
+    sum_moe = TensorSum(part_c, core_c, chip_c, final_c, send_sems, recv_sems, 6)
+    sum_first = TensorSum(part_d, core_d, chip_d, final_d, send_sems, recv_sems, 9)
+
+    def fill(part, value):
+        part[0, :, :HALF] = value[:, :HALF].astype(jnp.bfloat16)
+        part[1, :, :HALF] = value[:, HALF:].astype(jnp.bfloat16)
+
+    for source, held in ((inputs, rows_in), (cotangent, rows_cot)):
+        held[PAD - 16 : PAD, :] = jnp.zeros((16, WIDE), jnp.float32)
+        held[0:TOKENS, :] = source[0]
+    gain_rows = jnp.transpose(small_half[...].astype(jnp.float32))
+    gain_one, gain_two = gain_rows[0:1], gain_rows[1:2]
+    row_in = rows_in[...]
+    normal_one, inv_one = norm_parts(row_in)
+    normed_one = round_half(normal_one * gain_one)
+    qkv = round_half(rows_dot(normed_one, attn_half[:, : 3 * 192]))
+    row_id = lax.broadcasted_iota(jnp.int32, (PAD, PAD), 0)
+    col_id = lax.broadcasted_iota(jnp.int32, (PAD, PAD), 1)
+    scale = 1.0 / math.sqrt(HEAD_DIM)
+
+    def head_of(value, which, head):
+        start = which * 192 + head * HEAD_DIM
+        return value[:, start : start + HEAD_DIM]
+
+    head_rows = []
+    for head in range(3):
+        scores = contract_cols(head_of(qkv, 0, head), head_of(qkv, 1, head)) * scale
+        scores = jnp.where(col_id < TOKENS, scores, -1e30)
+        peak = jnp.max(scores, axis=-1, keepdims=True)
+        log_total = peak + jnp.log(jnp.sum(jnp.exp(scores - peak), axis=-1, keepdims=True))
+        prob = jnp.where(row_id < TOKENS, jnp.exp(scores - log_total), 0.0)
+        prob_all[head] = prob
+        head_rows.append(round_half(rows_dot(round_half(prob), head_of(qkv, 2, head))))
+    blank = jnp.zeros((PAD, HEAD_DIM), jnp.bfloat16)
+    attn_rows = jnp.concatenate([blank] + head_rows, axis=1)
+    fill(part_a, contract_cols(attn_rows, attn_half[:, 512:768]))
+    sum_attn.begin()
+    sum_attn.across()
+    sum_attn.share()
+    sum_attn.done()
+    middle = row_in + sum_attn.value()
+    normal_two, inv_two = norm_parts(middle)
+    normed_two = round_half(normal_two * gain_two)
+    logits = rows_dot(normed_two, small_half[...])
+    lane_id = lax.broadcasted_iota(jnp.int32, (TOKENS, LANE), 1) - 2
+    picks = routes[0]
+    gap = jnp.zeros((PAD - TOKENS, LANE), jnp.float32)
+
+    def chosen_mask(which):
+        hit = (lane_id == picks[:, which : which + 1]).astype(jnp.float32)
+        return jnp.concatenate([hit, gap], axis=0)
+
+    hot_first, hot_second = chosen_mask(0), chosen_mask(1)
+    difference = jnp.sum(logits * (hot_first - hot_second), axis=-1, keepdims=True)
+    gate_first = jax.nn.sigmoid(difference)
+    gate_second = jax.nn.sigmoid(-difference)
+    gates = gate_first * hot_first + gate_second * hot_second
+    sign = hot_first - hot_second
+    cot = rows_cot[...]
+    moe_part = jnp.zeros((PAD, WIDE), jnp.float32)
+    choice_part = jnp.zeros((PAD, 1), jnp.float32)
+    grad_part = jnp.zeros((PAD, WIDE), jnp.float32)
+    for expert in range(EF):
+        gate = gates[:, 2 + expert : 3 + expert]
+        pre_act = rows_dot(normed_two, in_half[expert])
+        inner = 1.0 + erf_of(pre_act * ROOT_HALF)
+        hidden = round_half(0.5 * pre_act * inner)
+        slope = 0.5 * inner + pre_act * INV_ROOT_TAU * jnp.exp(-0.5 * pre_act * pre_act)
+        expert_rows = contract_cols(hidden, out_half[expert])
+        moe_part = moe_part + gate * expert_rows
+        choice_part = choice_part + sign[:, 2 + expert : 3 + expert] * jnp.sum(
+            cot * expert_rows, axis=-1, keepdims=True
+        )
+        grad_expert = round_half(gate * cot)
+        grad_pre = round_half(rows_dot(grad_expert, out_half[expert]) * slope)
+        grad_part = grad_part + contract_cols(grad_pre, in_half[expert])
+        hidden_all[expert] = hidden
+        grad_pre_all[expert] = grad_pre
+    fill(part_b, grad_part)
+    extra = lax.broadcasted_iota(jnp.int32, (PAD, LANE), 1) == 0
+    part_b[0, :, HALF:] = jnp.where(extra, choice_part, 0.0).astype(jnp.bfloat16)
+    part_b[1, :, HALF:] = jnp.zeros((PAD, LANE), jnp.bfloat16)
+    sum_grad.begin()
+    fill(part_c, moe_part)
+    sum_grad.across()
+    for expert in range(EF):
+        grad_in[expert] = round_half(contract_rows(normed_two, grad_pre_all[expert]))
+    sum_grad.share()
+    for expert in range(EF):
+        gate = gates[:, 2 + expert : 3 + expert]
+        grad_out[expert] = round_half(contract_rows(round_half(gate * cot), hidden_all[expert]))
+    sum_moe.begin()
+    sum_grad.done()
+    choice = final_b[0, :, HALF : HALF + 1].astype(jnp.float32)
+    grad_first = choice * gate_first * gate_second
+    grad_logits = round_half(grad_first * sign)
+    grad_normed_two = sum_grad.value() + contract_cols(grad_logits, small_half[...])
+    grad_middle = cot + norm_pull(grad_normed_two, normal_two, inv_two, gain_two)
+    grad_gain_two = jnp.sum(grad_normed_two * normal_two, axis=0, keepdims=True)
+    router_part = contract_rows(normed_two, grad_logits)
+    grad_mid_half = round_half(grad_middle)
+    grad_heads = round_half(rows_dot(grad_mid_half, attn_half[:, 512:768]))
+    sum_moe.across()
+    parts = [[], [], []]
+    for head in range(3):
+        grad_head = grad_heads[:, HEAD_DIM * (head + 1) : HEAD_DIM * (head + 2)]
+        prob = prob_all[head]
+        grad_prob = contract_cols(grad_head, head_of(qkv, 2, head))
+        parts[2].append(round_half(contract_rows(round_half(prob), grad_head)))
+        spread = jnp.sum(prob * grad_prob, axis=-1, keepdims=True)
+        grad_scores = round_half(prob * (grad_prob - spread) * scale)
+        parts[0].append(round_half(rows_dot(grad_scores, head_of(qkv, 1, head))))
+        parts[1].append(round_half(contract_rows(grad_scores, head_of(qkv, 0, head))))
+    grad_qkv = jnp.concatenate(parts[0] + parts[1] + parts[2] + [blank] * 3, axis=1)
+    fill(part_d, contract_cols(grad_qkv, attn_half[...]))
+    sum_first.begin()
+    sum_moe.share()
+    sum_first.across()
+    grad_attn[:, :512] = round_half(contract_rows(normed_one, grad_qkv[:, :512]))
+    grad_attn[:, 512:] = round_half(
+        contract_rows(normed_one, grad_qkv[:, 512:])
+        + contract_rows(grad_mid_half, attn_rows)
+    )
+    sum_moe.done()
+    output[0] = (middle + sum_moe.value())[:TOKENS]
+    sum_first.share()
+    sum_first.done()
+    grad_normed_one = sum_first.value()
+    grad_inputs[0] = (grad_middle + norm_pull(grad_normed_one, normal_one, inv_one, gain_one))[
+        :TOKENS
+    ]
+    grad_gain_one = jnp.sum(grad_normed_one * normal_one, axis=0, keepdims=True)
+    gain_id = lax.broadcasted_iota(jnp.int32, (LANE, WIDE), 0)
+    gain_block = jnp.where(
+        gain_id == 0, grad_gain_one, jnp.where(gain_id == 1, grad_gain_two, 0.0)
+    )
+    grad_small[...] = round_half(jnp.transpose(gain_block) + router_part)
+    for summing in (sum_attn, sum_grad, sum_moe, sum_first):
+        summing.finish()
+
+
+def erf_of(value):
+    bounded = jnp.clip(value, -3.832506856900711, 3.832506856900711)
+    square = bounded * bounded
+    top = jnp.full_like(square, ERF_TOP[0])
+    for factor in ERF_TOP[1:]:
+        top = top * square + factor
+    bottom = jnp.full_like(square, ERF_BOTTOM[0])
+    for factor in ERF_BOTTOM[1:]:
+        bottom = bottom * square + factor
+    return bounded * top / bottom
+
+
+def main_step(inputs, cotangent, routes, attn_half, small_half, in_half, out_half):
+    half, single = jnp.bfloat16, jnp.float32
+    narrow, wide = (PAD, HALF), (PAD, HALF + LANE)
+    shapes = [narrow, wide, narrow, narrow]
+    return pl.pallas_call(
+        main_kernel,
+        out_shape=[
+            jax.ShapeDtypeStruct((1, TOKENS, WIDE), single),
+            jax.ShapeDtypeStruct((1, TOKENS, WIDE), single),
+            jax.ShapeDtypeStruct((WIDE, WIDE), half),
+            jax.ShapeDtypeStruct((WIDE, LANE), half),
+            jax.ShapeDtypeStruct((EF, WIDE, HALF), half),
+            jax.ShapeDtypeStruct((EF, WIDE, HALF), half),
+        ],
+        in_specs=vmem_specs(7),
+        out_specs=vmem_specs(6),
+        scratch_shapes=[
+            pltpu.VMEM((PAD, WIDE), single),
+            pltpu.VMEM((PAD, WIDE), single),
+            pltpu.VMEM((3, PAD, PAD), single),
+            pltpu.VMEM((EF, PAD, HALF), half),
+            pltpu.VMEM((EF, PAD, HALF), half),
+        ]
+        + [pltpu.VMEM((2,) + shape, half) for shape in shapes]
+        + [pltpu.VMEM(shape, half) for shape in shapes]
+        + [pltpu.VMEM(shape, half) for shape in shapes]
+        + [pltpu.VMEM((2,) + shape, half) for shape in shapes]
+        + [pltpu.SemaphoreType.DMA((12,)), pltpu.SemaphoreType.DMA((12,))],
+        compiler_params=pltpu.CompilerParams(
+            collective_id=3, has_side_effects=True, vmem_limit_bytes=60_000_000
+        ),
+    )(inputs, cotangent, routes, attn_half, small_half, in_half, out_half)
 
 
 def shards(
@@ -769,9 +972,6 @@
     moment_out,
     routes,
 ):
-    image_count, seq_len, model_width = inputs.shape
-    dp_count = lax.axis_size("dp")
-    row_count = image_count * seq_len
     attn_all, small_half, in_half, out_half = gather_weights(
         pack_rows(
             round_half(attn_mats),
@@ -780,95 +980,15 @@
             round_half(expert_out),
         )
     )
-    attn_half = jnp.stack([attn_all[:, 192 * which : 192 * which + 192] for which in range(4)])
-    gains_half = small_half[:, :2].T
-    router_half = small_half[:, 2 : 2 + EF]
-    gain_one = to_single(gains_half[0])
-    gain_two = to_single(gains_half[1])
-    row_in = inputs.reshape(row_count, model_width)
-    normal_one, inv_one, normed_one = norm_forward(row_in, gain_one)
-    queries, key_rows, value_rows, log_total, attn_rows = attention_forward(
-        normed_one, attn_half, image_count, seq_len
-    )
-    attn_part = contract_cols(attn_rows, attn_half[3])
-    attn_full = lax.psum(attn_part.astype(jnp.bfloat16), "tensor").astype(jnp.float32)
-    middle = row_in + attn_full
-    normal_two, inv_two, normed_two = norm_forward(middle, gain_two)
-    picked = routes.reshape(row_count, 2)
-    one_hot = (picked[:, :, None] == jnp.arange(EF, dtype=jnp.int32)[None, None, :]).astype(
-        jnp.float32
-    )
-    logits = jnp.dot(normed_two, router_half, preferred_element_type=jnp.float32)
-    chosen = jnp.sum(logits[:, None, :] * one_hot, axis=2)
-    gate_vals = jax.nn.sigmoid(chosen - chosen[:, ::-1])
-    gate_table = jnp.sum(gate_vals[:, :, None] * one_hot, axis=1)
-    grad_rows = cotangent.reshape(row_count, model_width)
-    pre_act = jnp.einsum("td,edf->etf", normed_two, in_half, preferred_element_type=jnp.float32)
-    hidden = round_half(gelu_value(pre_act))
-    expert_rows = jnp.einsum("etf,edf->etd", hidden, out_half, preferred_element_type=jnp.float32)
-    moe_part = jnp.sum(gate_table.T[:, :, None] * expert_rows, axis=0)
-    moe_full = lax.psum(moe_part.astype(jnp.bfloat16), "tensor").astype(jnp.float32)
-    output_rows = middle + moe_full
-    grad_each = jnp.sum(grad_rows[None] * expert_rows, axis=2).T
-    grad_choice_part = jnp.sum(grad_each[:, None, :] * one_hot, axis=2)
-    grad_expert = round_half(gate_table.T[:, :, None] * grad_rows[None])
-    grad_hidden = jnp.einsum(
-        "etd,edf->etf", grad_expert, out_half, preferred_element_type=jnp.float32
-    )
-    grad_pre = round_half(grad_hidden * gelu_slope(pre_act))
-    grad_normed_part = jnp.einsum(
-        "etf,edf->td", grad_pre, in_half, preferred_element_type=jnp.float32
-    )
-    grad_in = jnp.einsum("td,etf->edf", normed_two, grad_pre, preferred_element_type=jnp.float32)
-    grad_out = jnp.einsum("etd,etf->edf", grad_expert, hidden, preferred_element_type=jnp.float32)
-    joined = lax.psum(
-        jnp.concatenate([grad_normed_part, grad_choice_part], axis=1).astype(jnp.bfloat16), "tensor"
-    ).astype(jnp.float32)
-    grad_normed_moe, grad_choice = joined[:, :model_width], joined[:, model_width:]
-    gate_prod = gate_vals[:, 0] * gate_vals[:, 1]
-    grad_first = (grad_choice[:, 0] - grad_choice[:, 1]) * gate_prod
-    grad_picked = jnp.stack([grad_first, -grad_first], axis=1)
-    grad_logits = round_half(jnp.sum(grad_picked[:, :, None] * one_hot, axis=1))
-    grad_router = contract_rows(normed_two, grad_logits)
-    grad_normed_two = grad_normed_moe + contract_cols(grad_logits, router_half)
-    grad_mid_norm, grad_gain_two = norm_backward(grad_normed_two, normal_two, inv_two, gain_two)
-    grad_middle = grad_rows + grad_mid_norm
-    grad_mid_half = round_half(grad_middle)
-    grad_attn_rows = round_half(
-        jnp.dot(grad_mid_half, attn_half[3], preferred_element_type=jnp.float32)
-    )
-    grad_proj_out = contract_rows(grad_mid_half, attn_rows)
-    grad_queries, grad_keys, grad_values = attention_backward(
-        grad_attn_rows, queries, key_rows, value_rows, log_total
-    )
-    grad_attn = jnp.concatenate(
-        [
-            contract_rows(normed_one, grad_queries),
-            contract_rows(normed_one, grad_keys),
-            contract_rows(normed_one, grad_values),
-            grad_proj_out,
-        ],
-        axis=1,
-    )
-    grad_normed_one_part = (
-        contract_cols(grad_queries, attn_half[0])
-        + contract_cols(grad_keys, attn_half[1])
-        + contract_cols(grad_values, attn_half[2])
-    )
-    grad_normed_one = lax.psum(grad_normed_one_part.astype(jnp.bfloat16), "tensor").astype(
-        jnp.float32
-    )
-    grad_in_norm, grad_gain_one = norm_backward(grad_normed_one, normal_one, inv_one, gain_one)
-    grad_inputs_rows = grad_middle + grad_in_norm
-    gains_cols = jnp.stack([grad_gain_one, grad_gain_two], axis=1)
-    small_cols = jnp.concatenate([gains_cols, grad_router], axis=1)
-    small_wide = jnp.pad(round_half(small_cols), ((0, 0), (0, LANE - small_cols.shape[1])))
+    output, grad_inputs, grad_attn, grad_small, grad_in, grad_out = main_step(
+        inputs, cotangent, routes, attn_all, small_half, in_half, out_half
+    )
     sum_attn, sum_small, sum_in, sum_out = unpack_rows(
-        reduce_grads(round_half(grad_attn), small_wide, round_half(grad_in), round_half(grad_out))
+        reduce_grads(grad_attn, grad_small, grad_in, grad_out)
     )
     sum_gains = sum_small[:, :2].T
     sum_router = sum_small[:, 2:]
-    small_step = SMALL_RATE / math.sqrt(image_count * dp_count * seq_len)
+    small_step = SMALL_RATE / math.sqrt(lax.axis_size("dp") * TOKENS)
     moment_gains_new = MOMENTUM * moment_gains + sum_gains
     moment_attn_new = MOMENTUM * moment_attn + sum_attn
     moment_router_new = MOMENTUM * moment_router + sum_router
@@ -888,8 +1008,6 @@
     attn_new = attn_mats - MUON_RATE * update_attn
     in_new = expert_in - MUON_RATE * updates[2 : EF + 2]
     out_new = expert_out - MUON_RATE * updates[EF + 2 : 2 * EF + 2]
-    output = output_rows.reshape(image_count, seq_len, model_width)
-    grad_inputs = grad_inputs_rows.reshape(image_count, seq_len, model_width)
     return (
         output,
         grad_inputs,

time: 367 us -> 221 us (0.60)
  waiting for transfers between devices: 114 us -> 0 us
  Pallas kernels: 156 us -> 200 us
  matrix products: 33.7 us -> 0 us
  local copies, waits for them, and re-layouts: 25.7 us -> 10.4 us
  between operations: 14.5 us -> 1.02 us
  other arithmetic: 22.1 us -> 9.01 us
    psum x3 -> x0, waiting for transfers between devices: 113 us -> none  [the longest x1 40.8 us: shards(): lax.psum(moe_part.astype(jnp.bfloat16), 'tensor').astype(jnp.float32)]
    pallas_call x0 -> x1, Pallas kernels: none -> 41 us  [main_step(): pl.pallas_call(main_kernel, out_shape=[jax.ShapeDtypeStruct((1, TOKENS, W...]
    dot_general x27 -> x0, matrix products: 33.7 us -> none  [the longest x5 5.33 us: contract_cols(): lax.dot_general(left_mat, right_mat, (((1,), (1,)), ((), ())), preferred_...]
    another operation x6 -> x0, local copies, waits for them, and re-layouts: 6.79 us -> none
    reduce_sum x10 -> x0, other arithmetic: 4.71 us -> none  [the longest x2 2.23 us: norm_forward(): center = row_data - jnp.mean(row_data, axis=-1, keepdims=True)]
    unnamed x87 -> x52, local copies, waits for them, and re-layouts: 11.6 us -> 8.06 us
  transfers between devices with their start and end apart: 3 -> 0, of which waited for: 3 -> 0; matrix products, arithmetic and copies ran while one was open for 5% -> 0% of each run, Pallas kernels for 0% -> 0%
where the time goes in v3:
time: 221 us
  Pallas kernels  200 us (90%)
  local copies, waits for them, and re-layouts  10.4 us (5%)
  other arithmetic  9.01 us (4%)
    pallas_call x1, Pallas kernels, reduce_grads(): pl.pallas_call(reduce_kernel, out_shape=jax.ShapeDtypeStruct((PACK, LANE)...  61.7 us
    pallas_call x1, Pallas kernels, gather_weights(): pl.pallas_call(gather_kernel, out_shape=[jax.ShapeDtypeStruct(shape, jnp....  58.3 us
    pallas_call x1, Pallas kernels, main_step(): pl.pallas_call(main_kernel, out_shape=[jax.ShapeDtypeStruct((1, TOKENS, W...  41 us
    pallas_call x1, Pallas kernels, muon_step(): pl.pallas_call(muon_kernel, out_shape=jax.ShapeDtypeStruct((BLOCKS, 16, 3...  39.2 us
    unnamed x52, local copies, waits for them, and re-layouts  8.06 us

profile of v3, /device:TPU:94, one launch (start us, length us, event | category | flops | bytes accessed | tf_op | source)
XLA Modules:
  0.0 220.5 jit_solution(10586153227472770176)
XLA Ops:
  0.7 1.0 convert_bitcast_fusion.1
  1.7 0.9 convert_bitcast_fusion
  2.7 0.8 convert_bitcast_fusion.2
  3.6 0.7 convert_element_type.35
  4.3 0.7 convert_bitcast_fusion.3
  5.3 0.6 pad.13.shard
  5.9 58.3 %shard_map.323 = (bf16[768,768]{1,0:T(8,128)(2,1)}, bf16[768,128]{1,0:T(8,128)(2,1)}, bf16[3,768,384]{2,1,0:T(8,128)(2,1)}, bf16[3,768,384]{2,1,0:T(8,128)(2,1)}) custom-call(bf16[304,128]{1,0:T(8,128)(2,1)} %pad.13.shard, bf16[384,384]{1,0:T(8,128)(2,1)} %constant.11.clone.four, bf16[96,128]{1,0:T(8,128)(2,1)} %constant.4.clone.one.narrow), custom_call_target="tpu_custom_call" | custom-call | tf_op jit(solution)/shard_map/pallas_call | solution.py:249
  64.2 0.9 copy.92.inputs
  65.1 0.9 copy.93.cotangent
  66.0 0.8 copy.94.routes
  66.7 41.0 %shard_map.324 = (f32[1,197,768]{2,1,0:T(8,128)}, f32[1,197,768]{2,1,0:T(8,128)}, bf16[768,768]{1,0:T(8,128)(2,1)}, bf16[768,128]{1,0:T(8,128)(2,1)}, bf16[3,768...) custom-call(f32[1,197,768]{2,1,0:T(8,128)} %copy.92.inputs, f32[1,197,768]{2,1,0:T(8,128)} %copy.93.cotangent, ...), custom_call_target="tpu_custom_call" | custom-call | tf_op jit(solution)/shard_map/pallas_call | solution.py:930
  107.7 61.7 %shard_map.325 = f32[304,128]{1,0:T(8,128)} custom-call(bf16[768,768]{1,0:T(8,128)(2,1)} %get-tuple-element.33.attn, bf16[768,128]{1,0:T(8,128)(2,1)} %get-tuple-element.34.small, bf16[3,768,384]{2,1,0:T(8,128)(2,1)} %get-tuple-element.35.left, bf16[3,768,384]{2,1,0:T(8,128)(2,1)} %get-tuple-element.36.right, bf16[384,384]{1,0:T(8,128)(2,1)} %constant.42.four, ...), custom_call_target="tpu_custom_call" | custom-call | tf_op jit(solution)/shard_map/pallas_call | solution.py:459
  169.4 1.0 reshape.75
  170.8 0.7 add_convert_fusion
  171.7 0.6 fusion.13
  172.4 0.7 fusion.9.look
  173.1 39.2 %shard_map.326 = bf16[8,16,384]{2,1,0:T(8,128)(2,1)} custom-call(bf16[8,16,384]{2,1,0:T(8,128)(2,1)} %fusion.9.look, bf16[96,128]{1,0:T(8,128)(2,1)} %constant.4.clone.one.narrow, bf16[128,96]{1,0:T(8,128)(2,1)} %constant.43.one.wide, f32[384,384]{1,0:T(8,128)} %constant.5.clone.mask_ref), custom_call_target="tpu_custom_call" | custom-call | tf_op jit(solution)/shard_map/pallas_call | solution.py:639
  212.3 0.9 convert_element_type.41
  214.0 0.7 fusion.10
  215.0 0.7 copy.105
  215.6 0.7 copy.106
  216.3 0.7 copy.107
  217.6 1.4 copy.103
  219.1 1.4 copy.104
  (67 shorter events, 2.7 us)
Async XLA Ops:
  0.7 63.6 %copy-start.2 = (f32[1,197,768]{2,0,1:T(1,128)S(1)}, f32[1,197,768]{2,0,1:T(1,128)}, u32[]{:S(2)}) copy-start(f32[1,197,768]{2,0,1:T(1,128)} %param.20) | copy-start | bytes 1815556
  0.7 64.4 %copy-start.3 = (f32[1,197,768]{2,0,1:T(1,128)S(1)}, f32[1,197,768]{2,0,1:T(1,128)}, u32[]{:S(2)}) copy-start(f32[1,197,768]{2,0,1:T(1,128)} %param.21) | copy-start | bytes 1815556
  5.1 60.9 %copy-start.13 = (s32[1,197,2]{1,2,0:T(2,128)S(1)}, s32[1,197,2]{1,2,0:T(2,128)}, u32[]{:S(2)}) copy-start(s32[1,197,2]{1,2,0:T(2,128)} %param.32) | copy-start | bytes 4732
  169.4 1.4 copy-start.8
  169.4 1.4 copy-start.9
  169.4 2.2 %copy-start.10 = (f32[4,12,192]{2,0,1:T(4,128)S(1)}, f32[4,12,192]{2,0,1:T(4,128)}, u32[]{:S(2)}) copy-start(f32[4,12,192]{2,0,1:T(4,128)} %param.28) | copy-start | bytes 110596
  170.6 42.7 %copy-start.6 = (f32[4,12,192]{2,0,1:T(4,128)S(1)}, f32[4,12,192]{2,0,1:T(4,128)}, u32[]{:S(2)}) copy-start(f32[4,12,192]{2,0,1:T(4,128)} %param.23) | copy-start | bytes 110596
  170.6 43.4 %copy-start.4 = (f32[3,12,384]{2,1,0:T(8,128)S(1)}, f32[3,12,384]{2,1,0:T(8,128)}, u32[]{:S(2)}) copy-start(f32[3,12,384]{2,1,0:T(8,128)} %param.26) | copy-start | bytes 165892
  170.6 43.4 %copy-start.5 = (f32[3,12,384]{2,1,0:T(8,128)S(1)}, f32[3,12,384]{2,1,0:T(8,128)}, u32[]{:S(2)}) copy-start(f32[3,12,384]{2,1,0:T(8,128)} %param.25) | copy-start | bytes 165892
  170.7 44.0 %copy-start.14 = (f32[12,3]{0,1:T(4,128)S(1)}, f32[12,3]{0,1:T(4,128)}, u32[]{:S(2)}) copy-start(f32[12,3]{0,1:T(4,128)} %param.29) | copy-start | bytes 436
  170.7 44.1 %copy-start.11 = (f32[12,3]{0,1:T(4,128)S(1)}, f32[12,3]{0,1:T(4,128)}, u32[]{:S(2)}) copy-start(f32[12,3]{0,1:T(4,128)} %param.24) | copy-start | bytes 436
  170.8 46.3 %copy-start.15 = (f32[2,12]{1,0:T(2,128)S(1)}, f32[2,12]{1,0:T(2,128)}, u32[]{:S(2)}) copy-start(f32[2,12]{1,0:T(2,128)} %param.22) | copy-start | bytes 292
  170.8 46.3 %copy-start.16 = (f32[2,12]{1,0:T(2,128)S(1)}, f32[2,12]{1,0:T(2,128)}, u32[]{:S(2)}) copy-start(f32[2,12]{1,0:T(2,128)} %param.27) | copy-start | bytes 292
  170.8 46.8 %copy-start.1 = (f32[1,197,768]{2,1,0:T(8,128)S(1)}, f32[1,197,768]{2,1,0:T(8,128)}, u32[]{:S(2)}) copy-start(f32[1,197,768]{2,1,0:T(8,128)} %get-tuple-element.88) | copy-start | bytes 1815556
  171.7 47.4 %copy-start.7 = (f32[12,4,192]{2,1,0:T(4,128)}, f32[12,4,192]{2,1,0:T(4,128)S(1)}, u32[]{:S(2)}) copy-start(f32[12,4,192]{2,1,0:T(4,128)S(1)} %reshape.77) | copy-start | bytes 110596
  172.4 46.6 %copy-start = (f32[1,197,768]{2,1,0:T(8,128)S(1)}, f32[1,197,768]{2,1,0:T(8,128)}, u32[]{:S(2)}) copy-start(f32[1,197,768]{2,1,0:T(8,128)} %get-tuple-element.89) | copy-start | bytes 1815556
  217.0 3.5 %copy-start.12 = (f32[12,2]{0,1:T(2,128)}, f32[12,2]{0,1:T(2,128)S(1)}, u32[]{:S(2)}) copy-start(f32[12,2]{0,1:T(2,128)S(1)} %copy.108) | copy-start | bytes 292

commit v4 on v3

--- a/solution.py
+++ b/solution.py
@@ -53,20 +53,21 @@
 ROW = 12
 LANE = 128
 PACK = 304
-SPLIT = 128
+SPLIT = 144
 PLANE = NX * NY
+QUAD = PLANE // 2
 BLOCKS = 8
 MESH_ID = pl.DeviceIdType.MESH
 GROUPS = ((0, 4), (4, 4), (8, 4), (12, 4), (16, 4), (20, 4), (24, 1))
 
 
 def spread_matrix(block_count, padded):
-    table = np.zeros((block_count * PLANE * ROW, PLANE * padded), np.float32)
+    table = np.zeros((block_count * QUAD * ROW, QUAD * padded), np.float32)
     for block in range(block_count):
-        for member in range(PLANE):
+        for member in range(QUAD):
             for row in range(ROW):
                 table[
-                    block * PLANE * ROW + member * ROW + row, member * padded + block * ROW + row
+                    block * QUAD * ROW + member * ROW + row, member * padded + block * ROW + row
                 ] = 1.0
     return jnp.asarray(table, jnp.bfloat16)
 
@@ -138,6 +139,20 @@
         for pair in self.copies:
             for copy in pair:
                 copy.wait_send()
+
+
+def run_rounds(queue):
+    last = max(begin + ring.count // 2 for ring, begin in queue)
+    for turn in range(last + 1):
+        for ring, begin in queue:
+            step = turn - begin
+            if 1 <= step <= ring.count // 2:
+                ring.arrive(step - 1)
+            if 0 <= step < ring.count // 2:
+                ring.start(step)
+
+
+GATHER_SEMS = 1 + 4 * 20
 
 
 def gather_kernel(
@@ -154,56 +169,47 @@
     keep.wait()
     first.wait_recv()
 
-    def part_x_small(index, half):
-        if half is None:
-            return slots.at[z, pl.ds(NY * index, NY), pl.ds(0, SPLIT)]
-        return slots.at[z, NY * index + half, pl.ds(0, SPLIT)]
-
-    def part_z_small(index, half):
-        rest = pl.ds(SPLIT, PACK - SPLIT)
-        if half is None:
-            return slots.at[index, pl.ds(NY * x, NY), rest]
-        return slots.at[index, NY * x + half, rest]
-
-    def part_z_large(index, half):
-        if half is None:
-            return slots.at[index, pl.ds(0, PLANE), pl.ds(0, SPLIT)]
-        return slots.at[index, pl.ds(half * (PLANE // 2), PLANE // 2), pl.ds(0, SPLIT)]
-
-    def part_x_large(index, half):
-        rest = pl.ds(SPLIT, PACK - SPLIT)
-        if half is None:
-            return slots.at[pl.ds(0, NZ), pl.ds(NY * index, NY), rest]
-        return slots.at[pl.ds(half * (NZ // 2), NZ // 2), pl.ds(NY * index, NY), rest]
-
-    ring_ax = GatherRing(part_x_small, x, NX, up_x, down_x, send_sems, recv_sems, 1)
-    ring_bz = GatherRing(part_z_small, z, NZ, up_z, down_z, send_sems, recv_sems, 5)
-    ring_az = GatherRing(part_z_large, z, NZ, up_z, down_z, send_sems, recv_sems, 13)
-    ring_bx = GatherRing(part_x_large, x, NX, up_x, down_x, send_sems, recv_sems, 21)
-    ring_ax.start(0)
-    ring_bz.start(0)
-    ring_ax.arrive(0)
-    ring_ax.start(1)
-    ring_bz.arrive(0)
-    ring_bz.start(1)
-    ring_ax.arrive(1)
-    ring_az.start(0)
-    ring_bz.arrive(1)
-    ring_bz.start(2)
-    ring_bz.arrive(2)
-    ring_bz.start(3)
-    ring_az.arrive(0)
-    ring_az.start(1)
-    ring_bz.arrive(3)
-    ring_bx.start(0)
-    ring_az.arrive(1)
-    ring_az.start(2)
-    ring_az.arrive(2)
-    ring_az.start(3)
-    ring_bx.arrive(0)
-    ring_bx.start(1)
-    ring_az.arrive(3)
-    ring_bx.arrive(1)
+    head, rest = pl.ds(0, SPLIT), pl.ds(SPLIT, PACK - SPLIT)
+
+    def across_x(plane, rows):
+        def chunk(index, half):
+            if half is None:
+                return slots.at[plane, pl.ds(NY * index, NY), rows]
+            return slots.at[plane, NY * index + half, rows]
+
+        return chunk
+
+    def across_z(column, rows):
+        def chunk(index, half):
+            if half is None:
+                return slots.at[index, pl.ds(NY * column, NY), rows]
+            return slots.at[index, NY * column + half, rows]
+
+        return chunk
+
+    base = iter(range(1, GATHER_SEMS, 4))
+
+    def ring_x(plane, rows):
+        return GatherRing(
+            across_x(plane, rows), x, NX, up_x, down_x, send_sems, recv_sems, next(base)
+        )
+
+    def ring_z(column, rows):
+        first_sem = next(base)
+        next(base)
+        return GatherRing(
+            across_z(column, rows), z, NZ, up_z, down_z, send_sems, recv_sems, first_sem
+        )
+
+    queue = [(ring_x(z, head), 0), (ring_z(x, rest), 0), (ring_z(x, head), 0), (ring_x(z, rest), 0)]
+    for away in (1, NZ - 1):
+        queue.append((ring_x(wrap(z + away, NZ), rest), 1))
+    for away in (1, NX - 1):
+        queue.append((ring_z(wrap(x + away, NX), head), 1))
+    queue.append((ring_z(wrap(x + 2, NX), head), 2))
+    for away in (2, NZ - 2, 3, NZ - 3, 4):
+        queue.append((ring_x(wrap(z + away, NZ), rest), min(away, NZ - away)))
+    run_rounds(queue)
 
     def compact(plane, carry):
         rows = pl.ds(pl.multiple_of(plane * PLANE * ROW, 32), PLANE * ROW)
@@ -222,21 +228,26 @@
         for first_block, block_count in GROUPS:
             padded = 48 if block_count == 4 else 16
             picked = slots[plane, :, pl.ds(first_block * ROW, padded), :]
+            sides = [
+                picked[side * QUAD : (side + 1) * QUAD].reshape(QUAD * padded, LANE)
+                for side in range(2)
+            ]
             moved = jnp.dot(
                 (four if block_count == 4 else one)[...],
-                picked.reshape(PLANE * padded, LANE),
+                jnp.concatenate(sides, axis=1),
                 preferred_element_type=jnp.float32,
             ).astype(jnp.bfloat16)
             for block in range(block_count):
+                part = moved[block * QUAD * ROW : (block + 1) * QUAD * ROW]
                 put(
                     first_block + block,
-                    moved[block * PLANE * ROW : (block + 1) * PLANE * ROW, :],
+                    jnp.concatenate([part[:, :LANE], part[:, LANE:]], axis=0),
                 )
         return carry
 
     lax.fori_loop(0, NZ, compact, 0)
     first.wait_send()
-    for ring in (ring_ax, ring_bz, ring_az, ring_bx):
+    for ring, _ in queue:
         ring.finish()
 
 
@@ -254,8 +265,8 @@
         scratch_shapes=[
             pltpu.VMEM((NZ, PLANE, PACK, LANE), jnp.bfloat16),
             pltpu.SemaphoreType.DMA,
-            pltpu.SemaphoreType.DMA((25,)),
-            pltpu.SemaphoreType.DMA((25,)),
+            pltpu.SemaphoreType.DMA((GATHER_SEMS,)),
+            pltpu.SemaphoreType.DMA((GATHER_SEMS,)),
         ],
         compiler_params=pltpu.CompilerParams(
             collective_id=0, has_side_effects=True, vmem_limit_bytes=60_000_000
@@ -362,96 +373,83 @@
 
         for first_block, block_count in GROUPS:
             padded = 48 if block_count == 4 else 16
-            stacked = [get(first_block + block) for block in range(block_count)]
+            stacked = []
+            for block in range(block_count):
+                part = get(first_block + block)
+                stacked.append(
+                    jnp.concatenate([part[: QUAD * ROW], part[QUAD * ROW :]], axis=1)
+                )
             moved = jnp.dot(
                 (four if block_count == 4 else one)[...],
                 stacked[0] if block_count == 1 else jnp.concatenate(stacked, axis=0),
                 preferred_element_type=jnp.float32,
             ).astype(jnp.bfloat16)
-            slots[plane, :, pl.ds(first_block * ROW, padded), :] = moved.reshape(
-                PLANE, padded, LANE
-            )
+            for side in range(2):
+                slots[
+                    plane, side * QUAD : (side + 1) * QUAD, pl.ds(first_block * ROW, padded), :
+                ] = moved[:, side * LANE : (side + 1) * LANE].reshape(QUAD, padded, LANE)
         return carry
 
     lax.fori_loop(0, NZ, expand, 0)
-    rest = pl.ds(SPLIT, PACK - SPLIT)
-    head = pl.ds(0, SPLIT)
-
-    def part_az(index, half):
-        if half is None:
-            return slots.at[index, pl.ds(0, PLANE), head]
-        return slots.at[index, pl.ds(half * (PLANE // 2), PLANE // 2), head]
-
-    def land_of_az(side, step, half):
-        if half is None:
-            return land_az.at[side, step]
-        return land_az.at[side, step, pl.ds(half * (PLANE // 2), PLANE // 2)]
-
-    def part_bx(index, half):
-        if half is None:
-            return slots.at[pl.ds(0, NZ), pl.ds(NY * index, NY), rest]
-        return slots.at[pl.ds(half * (NZ // 2), NZ // 2), pl.ds(NY * index, NY), rest]
-
-    def land_of_bx(side, step, half):
-        if half is None:
-            return land_bx.at[side, step]
-        return land_bx.at[side, step, pl.ds(half * (NZ // 2), NZ // 2)]
-
-    def part_ax(index, half):
-        if half is None:
-            return slots.at[z, pl.ds(NY * index, NY), head]
-        return slots.at[z, pl.ds(NY * index + half, 1), head]
-
-    def land_of_ax(side, step, half):
-        if half is None:
-            return land_ax.at[side, step]
-        return land_ax.at[side, step, pl.ds(half, 1)]
-
-    def part_bz(index, half):
-        if half is None:
-            return slots.at[index, pl.ds(NY * x, NY), rest]
-        return slots.at[index, pl.ds(NY * x + half, 1), rest]
-
-    def land_of_bz(side, step, half):
-        if half is None:
-            return land_bz.at[side, step]
-        return land_bz.at[side, step, pl.ds(half, 1)]
-
-    ring_az = ReduceRing(part_az, land_of_az, z, NZ, up_z, down_z, send_sems, recv_sems, 1)
-    ring_bx = ReduceRing(part_bx, land_of_bx, x, NX, up_x, down_x, send_sems, recv_sems, 9)
-    ring_ax = ReduceRing(part_ax, land_of_ax, x, NX, up_x, down_x, send_sems, recv_sems, 13)
-    ring_bz = ReduceRing(part_bz, land_of_bz, z, NZ, up_z, down_z, send_sems, recv_sems, 17)
-    ring_az.start(0)
-    ring_bx.start(0)
-    ring_az.arrive(0)
-    ring_az.start(1)
-    ring_bx.arrive(0)
-    ring_bx.start(1)
-    ring_az.arrive(1)
-    ring_az.start(2)
-    ring_az.arrive(2)
-    ring_az.start(3)
-    ring_bx.arrive(1)
-    ring_bz.start(0)
-    ring_bz.arrive(0)
-    ring_bz.start(1)
-    ring_az.arrive(3)
-    ring_ax.start(0)
-    ring_bz.arrive(1)
-    ring_bz.start(2)
-    ring_ax.arrive(0)
-    ring_ax.start(1)
-    ring_bz.arrive(2)
-    ring_bz.start(3)
-    ring_ax.arrive(1)
-    ring_bz.arrive(3)
+    head, rest = pl.ds(0, SPLIT), pl.ds(SPLIT, PACK - SPLIT)
+
+    def across_x(plane, rows):
+        def chunk(index, half):
+            if half is None:
+                return slots.at[plane, pl.ds(NY * index, NY), rows]
+            return slots.at[plane, pl.ds(NY * index + half, 1), rows]
+
+        return chunk
+
+    def across_z(column, rows):
+        def chunk(index, half):
+            if half is None:
+                return slots.at[index, pl.ds(NY * column, NY), rows]
+            return slots.at[index, pl.ds(NY * column + half, 1), rows]
+
+        return chunk
+
+    def landing_in(held, which):
+        def landing(side, step, half):
+            if half is None:
+                return held.at[which, side, step]
+            return held.at[which, side, step, pl.ds(half, 1)]
+
+        return landing
+
+    base = iter(range(1, GATHER_SEMS, 4))
+
+    def ring_x(plane, rows, held, which):
+        return ReduceRing(
+            across_x(plane, rows), landing_in(held, which), x, NX, up_x, down_x,
+            send_sems, recv_sems, next(base),
+        )
+
+    def ring_z(column, rows, held, which):
+        first_sem = next(base)
+        next(base)
+        return ReduceRing(
+            across_z(column, rows), landing_in(held, which), z, NZ, up_z, down_z,
+            send_sems, recv_sems, first_sem,
+        )
+
+    queue = []
+    for which, away in enumerate((4, 3, NZ - 3, 2, NZ - 2, 1, NZ - 1, 0)):
+        queue.append(
+            (ring_x(wrap(z + away, NZ), rest, land_bx, which), 4 - min(away, NZ - away))
+        )
+    for which, (away, begin) in enumerate(((2, 0), (1, 1), (NX - 1, 1), (0, 2))):
+        queue.append((ring_z(wrap(x + away, NX), head, land_az, which), begin))
+    queue.append((ring_x(z, head, land_ax, 0), 4))
+    queue.append((ring_z(x, rest, land_bz, 0), 2))
+    run_rounds(queue)
     last = send(
         slots.at[z, NY * x + 1 - y], land_y, send_sems.at[0], recv_sems.at[0], other_y
     )
     last.wait_recv()
     total[...] = slots[z, NY * x + y].astype(jnp.float32) + land_y[...].astype(jnp.float32)
     last.wait_send()
-    for ring in (ring_az, ring_bx, ring_ax, ring_bz):
+    for ring, _ in queue:
         ring.finish()
 
 
@@ -463,13 +461,13 @@
         out_specs=pl.BlockSpec(memory_space=pltpu.VMEM),
         scratch_shapes=[
             pltpu.VMEM((NZ, PLANE, PACK, LANE), jnp.bfloat16),
-            pltpu.VMEM((2, 4, PLANE, SPLIT, LANE), jnp.bfloat16),
-            pltpu.VMEM((2, 2, NZ, NY, PACK - SPLIT, LANE), jnp.bfloat16),
-            pltpu.VMEM((2, 2, NY, SPLIT, LANE), jnp.bfloat16),
-            pltpu.VMEM((2, 4, NY, PACK - SPLIT, LANE), jnp.bfloat16),
+            pltpu.VMEM((NX, 2, 4, NY, SPLIT, LANE), jnp.bfloat16),
+            pltpu.VMEM((NZ, 2, 2, NY, PACK - SPLIT, LANE), jnp.bfloat16),
+            pltpu.VMEM((1, 2, 2, NY, SPLIT, LANE), jnp.bfloat16),
+            pltpu.VMEM((1, 2, 4, NY, PACK - SPLIT, LANE), jnp.bfloat16),
             pltpu.VMEM((PACK, LANE), jnp.bfloat16),
-            pltpu.SemaphoreType.DMA((25,)),
-            pltpu.SemaphoreType.DMA((25,)),
+            pltpu.SemaphoreType.DMA((GATHER_SEMS,)),
+            pltpu.SemaphoreType.DMA((GATHER_SEMS,)),
         ],
         compiler_params=pltpu.CompilerParams(
             collective_id=1, has_side_effects=True, vmem_limit_bytes=60_000_000
@@ -548,14 +546,14 @@
         ).wait_recv()
 
         def compact(plane, carry):
-            picked = arrived[pl.ds(plane * PLANE, PLANE)].reshape(PLANE * 16, 384)
-            rows = pl.ds(pl.multiple_of(plane * PLANE * ROW, 32), PLANE * ROW)
+            picked = arrived[pl.ds(plane * QUAD, QUAD)].reshape(QUAD * 16, 384)
+            rows = pl.ds(pl.multiple_of(plane * QUAD * ROW, 16), QUAD * ROW)
             matrix[rows, :] = jnp.dot(
                 narrow[...], picked, preferred_element_type=jnp.float32
             ).astype(jnp.bfloat16)
             return carry
 
-        lax.fori_loop(0, NZ, compact, 0)
+        lax.fori_loop(0, 2 * NZ, compact, 0)
         joined = my_block >= 2
         mask = jnp.maximum(mask_ref[...], joined.astype(jnp.float32))
         raw = matrix[...].astype(jnp.float32)
@@ -578,15 +576,15 @@
             ).astype(jnp.bfloat16)
 
         def expand(plane, carry):
-            rows = pl.ds(pl.multiple_of(plane * PLANE * ROW, 32), PLANE * ROW)
-            finished[pl.ds(plane * PLANE, PLANE)] = (
+            rows = pl.ds(pl.multiple_of(plane * QUAD * ROW, 16), QUAD * ROW)
+            finished[pl.ds(plane * QUAD, QUAD)] = (
                 jnp.dot(wide[...], matrix[rows, :], preferred_element_type=jnp.float32)
                 .astype(jnp.bfloat16)
-                .reshape(PLANE, 16, 384)
+                .reshape(QUAD, 16, 384)
             )
             return carry
 
-        lax.fori_loop(0, NZ, expand, 0)
+        lax.fori_loop(0, 2 * NZ, expand, 0)
 
         def give(target, carry):
             @pl.when(target != me)

time: 221 us -> 206 us (0.932)
  Pallas kernels: 200 us -> 185 us
    pallas_call x1, Pallas kernels: 61.7 us -> 52 us  [reduce_grads(): pl.pallas_call(reduce_kernel, out_shape=jax.ShapeDtypeStruct((PACK, LANE)...]
    pallas_call x1, Pallas kernels: 58.3 us -> 51.8 us  [gather_weights(): pl.pallas_call(gather_kernel, out_shape=[jax.ShapeDtypeStruct(shape, jnp....]
where the time goes in v4:
time: 206 us; the launch traced here: 205 us
  Pallas kernels  185 us (90%)
  local copies, waits for them, and re-layouts  10.4 us (5%)
  other arithmetic  9.01 us (4%)
    pallas_call x1, Pallas kernels, reduce_grads(): pl.pallas_call(reduce_kernel, out_shape=jax.ShapeDtypeStruct((PACK, LANE)...  52 us
    pallas_call x1, Pallas kernels, gather_weights(): pl.pallas_call(gather_kernel, out_shape=[jax.ShapeDtypeStruct(shape, jnp....  51.8 us
    pallas_call x1, Pallas kernels, main_step(): pl.pallas_call(main_kernel, out_shape=[jax.ShapeDtypeStruct((1, TOKENS, W...  41.5 us
    pallas_call x1, Pallas kernels, muon_step(): pl.pallas_call(muon_kernel, out_shape=jax.ShapeDtypeStruct((BLOCKS, 16, 3...  39.5 us
    unnamed x52, local copies, waits for them, and re-layouts  8.06 us

profile of v4, /device:TPU:94, one launch (start us, length us, event | category | flops | bytes accessed | tf_op | source)
XLA Modules:
  0.0 205.2 jit_solution(11515140187250333537)
XLA Ops:
  0.7 1.0 convert_bitcast_fusion.1
  1.7 0.9 convert_bitcast_fusion
  2.7 0.8 convert_bitcast_fusion.2
  3.6 0.7 convert_element_type.35
  4.3 0.7 convert_bitcast_fusion.3
  5.3 0.6 pad.13.shard
  5.9 51.8 %shard_map.323 = (bf16[768,768]{1,0:T(8,128)(2,1)}, bf16[768,128]{1,0:T(8,128)(2,1)}, bf16[3,768,384]{2,1,0:T(8,128)(2,1)}, bf16[3,768,384]{2,1,0:T(8,128)(2,1)}) custom-call(bf16[304,128]{1,0:T(8,128)(2,1)} %pad.13.shard, bf16[192,192]{1,0:T(8,128)(2,1)} %constant.11.clone.four, bf16[48,64]{1,0:T(8,128)(2,1)} %constant.4.clone.one.narrow), custom_call_target="tpu_custom_call" | custom-call | tf_op jit(solution)/shard_map/pallas_call | solution.py:260
  57.7 0.9 copy.92.inputs
  58.6 0.9 copy.93.cotangent
  59.4 0.8 copy.94.routes
  60.2 41.5 %shard_map.324 = (f32[1,197,768]{2,1,0:T(8,128)}, f32[1,197,768]{2,1,0:T(8,128)}, bf16[768,768]{1,0:T(8,128)(2,1)}, bf16[768,128]{1,0:T(8,128)(2,1)}, bf16[3,768...) custom-call(f32[1,197,768]{2,1,0:T(8,128)} %copy.92.inputs, f32[1,197,768]{2,1,0:T(8,128)} %copy.93.cotangent, ...), custom_call_target="tpu_custom_call" | custom-call | tf_op jit(solution)/shard_map/pallas_call | solution.py:928
  101.7 52.0 %shard_map.325 = f32[304,128]{1,0:T(8,128)} custom-call(bf16[768,768]{1,0:T(8,128)(2,1)} %get-tuple-element.33.attn, bf16[768,128]{1,0:T(8,128)(2,1)} %get-tuple-element.34.small, bf16[3,768,384]{2,1,0:T(8,128)(2,1)} %get-tuple-element.35.left, bf16[3,768,384]{2,1,0:T(8,128)(2,1)} %get-tuple-element.36.right, bf16[192,192]{1,0:T(8,128)(2,1)} %constant.11.clone.four, ...), custom_call_target="tpu_custom_call" | custom-call | tf_op jit(solution)/shard_map/pallas_call | solution.py:457
  153.8 1.0 reshape.75
  155.2 0.7 add_convert_fusion
  156.1 0.6 fusion.13
  156.8 0.7 fusion.9.look
  157.5 39.5 %shard_map.326 = bf16[8,16,384]{2,1,0:T(8,128)(2,1)} custom-call(bf16[8,16,384]{2,1,0:T(8,128)(2,1)} %fusion.9.look, bf16[48,64]{1,0:T(8,128)(2,1)} %constant.4.clone.one.narrow, bf16[64,48]{1,0:T(8,128)(2,1)} %constant.43.one.wide, f32[384,384]{1,0:T(8,128)} %constant.5.clone.mask_ref), custom_call_target="tpu_custom_call" | custom-call | tf_op jit(solution)/shard_map/pallas_call | solution.py:637
  197.0 0.9 convert_element_type.41
  198.7 0.7 fusion.10
  199.7 0.7 copy.105
  200.3 0.7 copy.106
  201.0 0.7 copy.107
  202.3 1.4 copy.103
  203.8 1.4 copy.104
  (67 shorter events, 2.7 us)
Async XLA Ops:
  0.7 57.0 %copy-start.2 = (f32[1,197,768]{2,0,1:T(1,128)S(1)}, f32[1,197,768]{2,0,1:T(1,128)}, u32[]{:S(2)}) copy-start(f32[1,197,768]{2,0,1:T(1,128)} %param.20) | copy-start | bytes 1815556
  0.7 57.9 %copy-start.3 = (f32[1,197,768]{2,0,1:T(1,128)S(1)}, f32[1,197,768]{2,0,1:T(1,128)}, u32[]{:S(2)}) copy-start(f32[1,197,768]{2,0,1:T(1,128)} %param.21) | copy-start | bytes 1815556
  5.1 54.4 %copy-start.13 = (s32[1,197,2]{1,2,0:T(2,128)S(1)}, s32[1,197,2]{1,2,0:T(2,128)}, u32[]{:S(2)}) copy-start(s32[1,197,2]{1,2,0:T(2,128)} %param.32) | copy-start | bytes 4732
  153.8 1.4 copy-start.8
  153.8 1.4 copy-start.9
  153.8 2.2 %copy-start.10 = (f32[4,12,192]{2,0,1:T(4,128)S(1)}, f32[4,12,192]{2,0,1:T(4,128)}, u32[]{:S(2)}) copy-start(f32[4,12,192]{2,0,1:T(4,128)} %param.28) | copy-start | bytes 110596
  154.9 43.2 %copy-start.6 = (f32[4,12,192]{2,0,1:T(4,128)S(1)}, f32[4,12,192]{2,0,1:T(4,128)}, u32[]{:S(2)}) copy-start(f32[4,12,192]{2,0,1:T(4,128)} %param.23) | copy-start | bytes 110596
  155.0 43.7 %copy-start.4 = (f32[3,12,384]{2,1,0:T(8,128)S(1)}, f32[3,12,384]{2,1,0:T(8,128)}, u32[]{:S(2)}) copy-start(f32[3,12,384]{2,1,0:T(8,128)} %param.26) | copy-start | bytes 165892
  155.0 43.7 %copy-start.5 = (f32[3,12,384]{2,1,0:T(8,128)S(1)}, f32[3,12,384]{2,1,0:T(8,128)}, u32[]{:S(2)}) copy-start(f32[3,12,384]{2,1,0:T(8,128)} %param.25) | copy-start | bytes 165892
  155.1 44.3 %copy-start.14 = (f32[12,3]{0,1:T(4,128)S(1)}, f32[12,3]{0,1:T(4,128)}, u32[]{:S(2)}) copy-start(f32[12,3]{0,1:T(4,128)} %param.29) | copy-start | bytes 436
  155.1 44.4 %copy-start.11 = (f32[12,3]{0,1:T(4,128)S(1)}, f32[12,3]{0,1:T(4,128)}, u32[]{:S(2)}) copy-start(f32[12,3]{0,1:T(4,128)} %param.24) | copy-start | bytes 436
  155.1 46.6 %copy-start.15 = (f32[2,12]{1,0:T(2,128)S(1)}, f32[2,12]{1,0:T(2,128)}, u32[]{:S(2)}) copy-start(f32[2,12]{1,0:T(2,128)} %param.22) | copy-start | bytes 292
  155.1 46.6 %copy-start.16 = (f32[2,12]{1,0:T(2,128)S(1)}, f32[2,12]{1,0:T(2,128)}, u32[]{:S(2)}) copy-start(f32[2,12]{1,0:T(2,128)} %param.27) | copy-start | bytes 292
  155.1 47.2 %copy-start.1 = (f32[1,197,768]{2,1,0:T(8,128)S(1)}, f32[1,197,768]{2,1,0:T(8,128)}, u32[]{:S(2)}) copy-start(f32[1,197,768]{2,1,0:T(8,128)} %get-tuple-element.88) | copy-start | bytes 1815556
  156.0 47.7 %copy-start.7 = (f32[12,4,192]{2,1,0:T(4,128)}, f32[12,4,192]{2,1,0:T(4,128)S(1)}, u32[]{:S(2)}) copy-start(f32[12,4,192]{2,1,0:T(4,128)S(1)} %reshape.77) | copy-start | bytes 110596
  156.8 47.0 %copy-start = (f32[1,197,768]{2,1,0:T(8,128)S(1)}, f32[1,197,768]{2,1,0:T(8,128)}, u32[]{:S(2)}) copy-start(f32[1,197,768]{2,1,0:T(8,128)} %get-tuple-element.89) | copy-start | bytes 1815556
  201.8 3.5 %copy-start.12 = (f32[12,2]{0,1:T(2,128)}, f32[12,2]{0,1:T(2,128)S(1)}, u32[]{:S(2)}) copy-start(f32[12,2]{0,1:T(2,128)S(1)} %copy.108) | copy-start | bytes 292

commit v5 on v4

v5 whole, which is shorter than its diff:
```python
import math

import jax
import jax.numpy as jnp
import numpy as np
from jax import lax
from jax.experimental import pallas as pl
from jax.experimental.pallas import tpu as pltpu
from jax.sharding import PartitionSpec as P

HEAD_DIM = 64
EF = 3
NS_ITERS = 3
CAP = 197


EPSILON = 1e-06
MOMENTUM = 0.9
MUON_RATE = 0.5
SMALL_RATE = 0.5
NEWTON_A = 3.4445
NEWTON_B = -4.775
NEWTON_C = 2.0315
ROOT_HALF = 0.7071067811865476
INV_ROOT_TAU = 0.3989422804014327


def round_half(operand):
    return operand.astype(jnp.bfloat16)


def settle(operand):
    return lax.optimization_barrier(operand.astype(jnp.bfloat16))


def to_single(operand):
    return operand.astype(jnp.float32)


def contract_rows(left_mat, right_mat):
    return lax.dot_general(
        left_mat, right_mat, (((0,), (0,)), ((), ())), preferred_element_type=jnp.float32
    )


def contract_cols(left_mat, right_mat):
    return lax.dot_general(
        left_mat, right_mat, (((1,), (1,)), ((), ())), preferred_element_type=jnp.float32
    )


NZ, NX, NY = 8, 4, 2
ROW = 12
LANE = 128
PACK = 304
PLANE = NX * NY
QUAD = PLANE // 2
BLOCKS = 8
MESH_ID = pl.DeviceIdType.MESH
GROUPS = ((0, 4), (4, 4), (8, 4), (12, 4), (16, 4), (20, 4), (24, 1))


def spread_matrix(block_count, padded):
    table = np.zeros((block_count * QUAD * ROW, QUAD * padded), np.float32)
    for block in range(block_count):
        for member in range(QUAD):
            for row in range(ROW):
                table[
                    block * QUAD * ROW + member * ROW + row, member * padded + block * ROW + row
                ] = 1.0
    return jnp.asarray(table, jnp.bfloat16)


def place_of(me):
    return me // PLANE, lax.rem(me // NY, NX), lax.rem(me, NY)


def dp_index(z, x, y):
    return z * PLANE + x * NY + y


def wrap(value, count):
    return lax.rem(value + 2 * count, count)


def neighbours(me):
    z, x, y = place_of(me)
    return (
        dp_index(wrap(z + 1, NZ), x, y),
        dp_index(wrap(z - 1, NZ), x, y),
        dp_index(z, wrap(x + 1, NX), y),
        dp_index(z, wrap(x - 1, NX), y),
        dp_index(z, x, 1 - y),
    )


def send(source, landing, send_sem, recv_sem, target):
    copy = pltpu.make_async_remote_copy(
        src_ref=source,
        dst_ref=landing,
        send_sem=send_sem,
        recv_sem=recv_sem,
        device_id={"dp": target},
        device_id_type=MESH_ID,
    )
    copy.start()
    return copy


class GatherRing:
    def __init__(self, chunk, position, count, up, down, send_sems, recv_sems, base):
        self.chunk, self.position, self.count = chunk, position, count
        self.up, self.down = up, down
        self.send_sems, self.recv_sems, self.base = send_sems, recv_sems, base
        self.copies = []

    def start(self, step):
        half = step == self.count // 2 - 1
        pair = []
        for side, (sign, target) in enumerate(((-1, self.up), (1, self.down))):
            part = self.chunk(wrap(self.position + sign * step, self.count), side if half else None)
            slot = self.base + 2 * step + side
            pair.append(send(part, part, self.send_sems.at[slot], self.recv_sems.at[slot], target))
        self.copies.append(pair)

    def arrive(self, step):
        for copy in self.copies[step]:
            copy.wait_recv()

    def finish(self):
        for pair in self.copies:
            for copy in pair:
                copy.wait_send()


def vmem_specs(count):
    return [pl.BlockSpec(memory_space=pltpu.VMEM)] * count


def unpack_rows(rows):
    flat = jnp.transpose(rows[: 25 * ROW].reshape(25, ROW, LANE), (1, 0, 2)).reshape(ROW, 25 * LANE)
    attn = jnp.transpose(flat[:, :768].reshape(ROW, 4, 192), (1, 0, 2))
    small = flat[:, 768:773]
    left = jnp.transpose(flat[:, 896:2048].reshape(ROW, EF, 384), (1, 0, 2))
    right = jnp.transpose(flat[:, 2048:3200].reshape(ROW, EF, 384), (1, 0, 2))
    return attn, small, left, right


class ReduceRing:
    def __init__(self, chunk, landing, position, count, up, down, send_sems, recv_sems, base):
        self.chunk, self.landing = chunk, landing
        self.position, self.count = position, count
        self.up, self.down = up, down
        self.send_sems, self.recv_sems, self.base = send_sems, recv_sems, base
        self.copies = []

    def start(self, step):
        away = self.count // 2 - step
        pair = []
        for side, (sign, target) in enumerate(((1, self.up), (-1, self.down))):
            half = side if step == 0 else None
            part = self.chunk(wrap(self.position + sign * away, self.count), half)
            slot = self.base + 2 * step + side
            pair.append(
                send(
                    part,
                    self.landing(side, step, half),
                    self.send_sems.at[slot],
                    self.recv_sems.at[slot],
                    target,
                )
            )
        self.copies.append(pair)

    def arrive(self, step):
        for copy in self.copies[step]:
            copy.wait_recv()
        away = self.count // 2 - 1 - step
        if away == 0:
            mine = self.chunk(self.position, None)
            mine[...] = (
                mine[...].astype(jnp.float32)
                + self.landing(0, step, None)[...].astype(jnp.float32)
                + self.landing(1, step, None)[...].astype(jnp.float32)
            ).astype(jnp.bfloat16)
            return
        for side, sign in ((0, 1), (1, -1)):
            half = side if step == 0 else None
            mine = self.chunk(wrap(self.position + sign * away, self.count), half)
            mine[...] = (
                mine[...].astype(jnp.float32)
                + self.landing(side, step, half)[...].astype(jnp.float32)
            ).astype(jnp.bfloat16)

    def finish(self):
        for pair in self.copies:
            for copy in pair:
                copy.wait_send()


TOKENS = 197
PAD = 208
WIDE = 768
HALF = 384
ERF_TOP = (
    0.00022905065861350646, 0.0034082910107109506, 0.050955695062380861,
    0.18520832239976145, 1.128379143519084,
)
ERF_BOTTOM = (
    -1.1791602954361697e-7, 0.000023547966471313185, 0.0010179625278914885,
    0.014070470171167667, 0.11098505178285362, 0.49746925110067538, 1.0,
)


def rows_dot(left_mat, right_mat):
    return jnp.dot(left_mat, right_mat, preferred_element_type=jnp.float32)


def mean_of(value):
    return jnp.sum(value, axis=-1, keepdims=True) * (1.0 / WIDE)


def norm_parts(row_data):
    center = row_data - mean_of(row_data)
    inv_std = lax.rsqrt(mean_of(center * center) + EPSILON)
    return center * inv_std, inv_std


def norm_pull(grad_result, normal, inv_std, gain_row):
    scaled = grad_result * gain_row
    return inv_std * (scaled - mean_of(scaled) - normal * mean_of(scaled * normal))


class TensorSum:
    def __init__(self, part, land_core, land_chip, final, send_sems, recv_sems, base):
        self.part, self.land_core, self.land_chip, self.final = part, land_core, land_chip, final
        self.send_sems, self.recv_sems, self.base = send_sems, recv_sems, base
        mine = lax.axis_index("tensor")
        self.core = lax.rem(mine, 2)
        self.other_core = mine + 1 - 2 * self.core
        self.other_chip = lax.rem(mine + 2, 4)
        self.copies = []

    def put(self, source, landing, target):
        slot = self.base + len(self.copies)
        copy = pltpu.make_async_remote_copy(
            src_ref=source,
            dst_ref=landing,
            send_sem=self.send_sems.at[slot],
            recv_sem=self.recv_sems.at[slot],
            device_id={"tensor": target},
            device_id_type=MESH_ID,
        )
        copy.start()
        self.copies.append(copy)

    def begin(self):
        self.put(self.part.at[1 - self.core], self.land_core, self.other_core)

    def across(self):
        self.copies[0].wait_recv()
        mine = self.part.at[self.core]
        mine[...] = (
            mine[...].astype(jnp.float32) + self.land_core[...].astype(jnp.float32)
        ).astype(jnp.bfloat16)
        self.put(mine, self.land_chip, self.other_chip)

    def share(self):
        self.copies[1].wait_recv()
        mine = self.final.at[self.core]
        mine[...] = (
            self.part[self.core].astype(jnp.float32) + self.land_chip[...].astype(jnp.float32)
        ).astype(jnp.bfloat16)
        self.put(mine, mine, self.other_core)

    def done(self):
        self.copies[2].wait_recv()

    def value(self):
        return jnp.concatenate(
            [self.final[0][:, :HALF], self.final[1][:, :HALF]], axis=1
        ).astype(jnp.float32)

    def finish(self):
        for copy in self.copies:
            copy.wait_send()


def erf_of(value):
    bounded = jnp.clip(value, -3.832506856900711, 3.832506856900711)
    square = bounded * bounded
    top = jnp.full_like(square, ERF_TOP[0])
    for factor in ERF_TOP[1:]:
        top = top * square + factor
    bottom = jnp.full_like(square, ERF_BOTTOM[0])
    for factor in ERF_BOTTOM[1:]:
        bottom = bottom * square + factor
    return bounded * top / bottom


class Rounds:
    def __init__(self, queue):
        self.queue, self.turn = queue, 0
        self.turns = 1 + max(begin + ring.count // 2 for ring, begin in queue)

    def advance(self):
        for ring, begin in self.queue:
            step = self.turn - begin
            if 1 <= step <= ring.count // 2:
                ring.arrive(step - 1)
            if 0 <= step < ring.count // 2:
                ring.start(step)
        self.turn += 1

    def finish(self):
        for ring, _ in self.queue:
            ring.finish()


SETS = ((0, 48, 48, GROUPS[:2]), (96, 96, 112, GROUPS[2:]))
RING_SEMS = 2 * 77


def mega_kernel(
    inputs, cotangent, routes, gains, router, attn_mats, mats_in, mats_out,
    moment_attn, moment_in, moment_out, four, one, four_back, one_back, mask_ref,
    output, grad_inputs, total, result,
    packed, slots, attn_half, small_half, in_half, out_half,
    rows_in, rows_cot, prob_all, hidden_all, grad_pre_all,
    grad_attn, grad_small, grad_in, grad_out, sums,
    land_az_p, land_bx_p, land_ax_p, land_bz_p, land_y_p,
    land_az_e, land_bx_e, land_ax_e, land_bz_e, land_y_e,
    part_a, part_b, part_c, part_d, core_a, core_b, core_c, core_d,
    chip_a, chip_b, chip_c, chip_d, final_a, final_b, final_c, final_d,
    small_land, look, arrived, matrix, finished, gram,
    gather_send, gather_recv, reduce_send, reduce_recv, send_sems, recv_sems,
    small_send, small_recv, local_sems, muon_send, muon_recv, back_sem, ret_sems,
):
    me = lax.axis_index("dp")
    mine = lax.axis_index("tensor")
    z, x, y = place_of(me)
    up_z, down_z, up_x, down_x, other_y = neighbours(me)
    barrier = pltpu.get_barrier_semaphore()
    for target in (up_z, down_z, up_x, down_x, other_y):
        pl.semaphore_signal(barrier, inc=1, device_id={"dp": target}, device_id_type=MESH_ID)
    for away in (1, 2, 3):
        pl.semaphore_signal(
            barrier, inc=1, device_id={"tensor": lax.rem(mine + away, 4)}, device_id_type=MESH_ID
        )

    diagonal = lax.broadcasted_iota(jnp.int32, (ROW, ROW), 0) == lax.broadcasted_iota(
        jnp.int32, (ROW, ROW), 1
    )
    lanes = lax.broadcasted_iota(jnp.int32, (ROW, LANE), 1)

    def upright(row):
        return jnp.sum(jnp.where(diagonal, row, 0.0), axis=1, keepdims=True)

    def flat_attn(ref):
        return jnp.concatenate([ref[:, which, :] for which in range(4)], axis=1)

    def block_rows(block):
        return slice(block * ROW, (block + 1) * ROW)

    flat = flat_attn(attn_mats)
    for block in range(6):
        packed[block_rows(block), :] = flat[:, block * LANE : (block + 1) * LANE]
    small = jnp.zeros((ROW, LANE), jnp.float32)
    for lane, (source, row) in enumerate(((gains, 0), (gains, 1), (router, 0), (router, 1), (router, 2))):
        small = small + jnp.where(lanes == lane, upright(source[row : row + 1, :]), 0.0)
    packed[block_rows(6), :] = small
    for index in range(9):
        column = (index % 3) * LANE
        packed[block_rows(7 + index), :] = mats_in[index // 3, :, column : column + LANE]
        packed[block_rows(16 + index), :] = mats_out[index // 3, :, column : column + LANE]
    packed[25 * ROW : PACK, :] = jnp.zeros((PACK - 25 * ROW, LANE), jnp.float32)
    slots[z, NY * x + y] = round_half(packed[...])
    pl.semaphore_wait(barrier, 8)

    def across_x(plane, rows, wide):
        def chunk(index, half):
            if half is None:
                return slots.at[plane, pl.ds(NY * index, NY), rows]
            return slots.at[plane, pl.ds(NY * index + half, 1), rows]

        return chunk

    def across_z(column, rows, wide):
        def chunk(index, half):
            if half is None:
                return slots.at[index, pl.ds(NY * column, NY), rows]
            return slots.at[index, pl.ds(NY * column + half, 1), rows]

        return chunk

    def sem_bases(first):
        while True:
            yield first
            first += 4

    def gather_rounds(which):
        low, rows_a, rows_b, _ = SETS[which]
        head, rest = pl.ds(low, rows_a), pl.ds(low + rows_a, rows_b)
        base = sem_bases(77 * which + 1)

        def ring_x(plane, rows):
            return GatherRing(
                across_x(plane, rows, None), x, NX, up_x, down_x, gather_send, gather_recv,
                next(base),
            )

        def ring_z(column, rows):
            first_sem = next(base)
            next(base)
            return GatherRing(
                across_z(column, rows, None), z, NZ, up_z, down_z, gather_send, gather_recv,
                first_sem,
            )

        queue = [
            (ring_x(z, head), 0), (ring_z(x, rest), 0), (ring_z(x, head), 0), (ring_x(z, rest), 0)
        ]
        for away in (1, NZ - 1):
            queue.append((ring_x(wrap(z + away, NZ), rest), 1))
        for away in (1, NX - 1):
            queue.append((ring_z(wrap(x + away, NX), head), 1))
        queue.append((ring_z(wrap(x + 2, NX), head), 2))
        for away in (2, NZ - 2, 3, NZ - 3, 4):
            queue.append((ring_x(wrap(z + away, NZ), rest), min(away, NZ - away)))
        return Rounds(queue)

    def gather_first(which):
        low, rows_a, rows_b, _ = SETS[which]
        own = slots.at[z, NY * x + y, pl.ds(low, rows_a + rows_b)]
        return send(own, own, gather_send.at[77 * which], gather_recv.at[77 * which], other_y)

    lands = (
        (land_az_p, land_bx_p, land_ax_p, land_bz_p, land_y_p),
        (land_az_e, land_bx_e, land_ax_e, land_bz_e, land_y_e),
    )

    def landing_in(held, which):
        def landing(side, step, half):
            if half is None:
                return held.at[which, side, step]
            return held.at[which, side, step, pl.ds(half, 1)]

        return landing

    def reduce_rounds(which):
        low, rows_a, rows_b, _ = SETS[which]
        land_az, land_bx, land_ax, land_bz, _ = lands[which]
        head, rest = pl.ds(low, rows_a), pl.ds(low + rows_a, rows_b)
        base = sem_bases(77 * which + 1)

        def ring_x(plane, rows, held, index):
            return ReduceRing(
                across_x(plane, rows, None), landing_in(held, index), x, NX, up_x, down_x,
                reduce_send, reduce_recv, next(base),
            )

        def ring_z(column, rows, held, index):
            first_sem = next(base)
            next(base)
            return ReduceRing(
                across_z(column, rows, None), landing_in(held, index), z, NZ, up_z, down_z,
                reduce_send, reduce_recv, first_sem,
            )

        queue = []
        for index, away in enumerate((4, 3, NZ - 3, 2, NZ - 2, 1, NZ - 1, 0)):
            queue.append(
                (ring_x(wrap(z + away, NZ), rest, land_bx, index), 4 - min(away, NZ - away))
            )
        for index, (away, begin) in enumerate(((2, 0), (1, 1), (NX - 1, 1), (0, 2))):
            queue.append((ring_z(wrap(x + away, NX), head, land_az, index), begin))
        queue.append((ring_x(z, head, land_ax, 0), 4))
        queue.append((ring_z(x, rest, land_bz, 0), 2))
        return Rounds(queue)

    def reduce_last(which):
        low, rows_a, rows_b, _ = SETS[which]
        return send(
            slots.at[z, NY * x + 1 - y, pl.ds(low, rows_a + rows_b)], lands[which][4],
            reduce_send.at[77 * which], reduce_recv.at[77 * which], other_y,
        )

    def reduce_close(which, copy):
        low, rows_a, rows_b, _ = SETS[which]
        rows = slice(low, low + rows_a + rows_b)
        copy.wait_recv()
        sums[rows, :] = slots[z, NY * x + y, rows].astype(jnp.float32) + lands[which][4][
            ...
        ].astype(jnp.float32)

    def place(refs, block):
        attn_ref, small_ref, in_ref, out_ref = refs
        if block < 6:
            return attn_ref, None, block * LANE
        if block == 6:
            return small_ref, None, 0
        index = (block - 7) % 9
        return (in_ref if block < 16 else out_ref), index // 3, (index % 3) * LANE

    def compact(which):
        refs = (attn_half, small_half, in_half, out_half)

        def body(plane, carry):
            rows = pl.ds(pl.multiple_of(plane * PLANE * ROW, 32), PLANE * ROW)
            for first_block, block_count in SETS[which][3]:
                padded = 48 if block_count == 4 else 16
                picked = slots[plane, :, pl.ds(first_block * ROW, padded), :]
                sides = [
                    picked[side * QUAD : (side + 1) * QUAD].reshape(QUAD * padded, LANE)
                    for side in range(2)
                ]
                moved = rows_dot(
                    (four if block_count == 4 else one)[...], jnp.concatenate(sides, axis=1)
                ).astype(jnp.bfloat16)
                for block in range(block_count):
                    part = moved[block * QUAD * ROW : (block + 1) * QUAD * ROW]
                    value = jnp.concatenate([part[:, :LANE], part[:, LANE:]], axis=0)
                    ref, lead, column = place(refs, first_block + block)
                    if lead is None:
                        ref[rows, column : column + LANE] = value
                    else:
                        ref[lead, rows, column : column + LANE] = value
            return carry

        lax.fori_loop(0, NZ, body, 0)

    def expand(which):
        refs = (grad_attn, grad_small, grad_in, grad_out)

        def body(plane, carry):
            rows = pl.ds(pl.multiple_of(plane * PLANE * ROW, 32), PLANE * ROW)
            for first_block, block_count in SETS[which][3]:
                padded = 48 if block_count == 4 else 16
                stacked = []
                for block in range(block_count):
                    ref, lead, column = place(refs, first_block + block)
                    if lead is None:
                        part = ref[rows, column : column + LANE]
                    else:
                        part = ref[lead, rows, column : column + LANE]
                    stacked.append(
                        jnp.concatenate([part[: QUAD * ROW], part[QUAD * ROW :]], axis=1)
                    )
                moved = rows_dot(
                    (four_back if block_count == 4 else one_back)[...],
                    stacked[0] if block_count == 1 else jnp.concatenate(stacked, axis=0),
                ).astype(jnp.bfloat16)
                for side in range(2):
                    slots[
                        plane, side * QUAD : (side + 1) * QUAD,
                        pl.ds(first_block * ROW, padded), :,
                    ] = moved[:, side * LANE : (side + 1) * LANE].reshape(QUAD, padded, LANE)
            return carry

        lax.fori_loop(0, NZ, body, 0)

    first_p, first_e = gather_first(0), gather_first(1)
    near, far = gather_rounds(0), gather_rounds(1)
    for source, held in ((inputs, rows_in), (cotangent, rows_cot)):
        held[PAD - 16 : PAD, :] = jnp.zeros((16, WIDE), jnp.float32)
        held[0:TOKENS, :] = source[0]
    row_in = rows_in[...]
    normal_one, inv_one = norm_parts(row_in)
    first_p.wait_recv()
    for turn in range(near.turns):
        near.advance()
        if turn == LAG - 1:
            first_e.wait_recv()
        if turn >= LAG:
            far.advance()
    compact(0)

    sum_attn = TensorSum(part_a, core_a, chip_a, final_a, send_sems, recv_sems, 0)
    sum_grad = TensorSum(part_b, core_b, chip_b, final_b, send_sems, recv_sems, 3)
    sum_moe = TensorSum(part_c, core_c, chip_c, final_c, send_sems, recv_sems, 6)
    sum_first = TensorSum(part_d, core_d, chip_d, final_d, send_sems, recv_sems, 9)

    def fill(part, value):
        part[0, :, :HALF] = value[:, :HALF].astype(jnp.bfloat16)
        part[1, :, :HALF] = value[:, HALF:].astype(jnp.bfloat16)

    gain_rows = jnp.transpose(small_half[...].astype(jnp.float32))
    gain_one, gain_two = gain_rows[0:1], gain_rows[1:2]
    normed_one = round_half(normal_one * gain_one)
    qkv = round_half(rows_dot(normed_one, attn_half[:, : 3 * 192]))
    if far.turn < far.turns:
        far.advance()
    row_id = lax.broadcasted_iota(jnp.int32, (PAD, PAD), 0)
    col_id = lax.broadcasted_iota(jnp.int32, (PAD, PAD), 1)
    scale = 1.0 / math.sqrt(HEAD_DIM)

    def head_of(value, which, head):
        start = which * 192 + head * HEAD_DIM
        return value[:, start : start + HEAD_DIM]

    head_rows = []
    for head in range(3):
        scores = contract_cols(head_of(qkv, 0, head), head_of(qkv, 1, head)) * scale
        scores = jnp.where(col_id < TOKENS, scores, -1e30)
        peak = jnp.max(scores, axis=-1, keepdims=True)
        log_total = peak + jnp.log(jnp.sum(jnp.exp(scores - peak), axis=-1, keepdims=True))
        prob = jnp.where(row_id < TOKENS, jnp.exp(scores - log_total), 0.0)
        prob_all[head] = prob
        head_rows.append(round_half(rows_dot(round_half(prob), head_of(qkv, 2, head))))
    blank = jnp.zeros((PAD, HEAD_DIM), jnp.bfloat16)
    attn_rows = jnp.concatenate([blank] + head_rows, axis=1)
    fill(part_a, contract_cols(attn_rows, attn_half[:, 512:768]))
    sum_attn.begin()
    if far.turn < far.turns:
        far.advance()
    sum_attn.across()
    if far.turn < far.turns:
        far.advance()
    sum_attn.share()
    while far.turn < far.turns:
        far.advance()
    sum_attn.done()
    middle = row_in + sum_attn.value()
    normal_two, inv_two = norm_parts(middle)
    normed_two = round_half(normal_two * gain_two)
    compact(1)
    logits = rows_dot(normed_two, small_half[...])
    lane_id = lax.broadcasted_iota(jnp.int32, (TOKENS, LANE), 1) - 2
    picks = routes[0]
    gap = jnp.zeros((PAD - TOKENS, LANE), jnp.float32)

    def chosen_mask(which):
        hit = (lane_id == picks[:, which : which + 1]).astype(jnp.float32)
        return jnp.concatenate([hit, gap], axis=0)

    hot_first, hot_second = chosen_mask(0), chosen_mask(1)
    sign = hot_first - hot_second
    difference = jnp.sum(logits * sign, axis=-1, keepdims=True)
    gate_first = jax.nn.sigmoid(difference)
    gate_second = jax.nn.sigmoid(-difference)
    gates = gate_first * hot_first + gate_second * hot_second
    cot = rows_cot[...]
    moe_part = jnp.zeros((PAD, WIDE), jnp.float32)
    choice_part = jnp.zeros((PAD, 1), jnp.float32)
    grad_part = jnp.zeros((PAD, WIDE), jnp.float32)
    for expert in range(EF):
        gate = gates[:, 2 + expert : 3 + expert]
        pre_act = rows_dot(normed_two, in_half[expert])
        inner = 1.0 + erf_of(pre_act * ROOT_HALF)
        hidden = round_half(0.5 * pre_act * inner)
        slope = 0.5 * inner + pre_act * INV_ROOT_TAU * jnp.exp(-0.5 * pre_act * pre_act)
        expert_rows = contract_cols(hidden, out_half[expert])
        moe_part = moe_part + gate * expert_rows
        choice_part = choice_part + sign[:, 2 + expert : 3 + expert] * jnp.sum(
            cot * expert_rows, axis=-1, keepdims=True
        )
        grad_expert = round_half(gate * cot)
        grad_pre = round_half(rows_dot(grad_expert, out_half[expert]) * slope)
        grad_part = grad_part + contract_cols(grad_pre, in_half[expert])
        hidden_all[expert] = hidden
        grad_pre_all[expert] = grad_pre
    fill(part_b, grad_part)
    extra = lax.broadcasted_iota(jnp.int32, (PAD, LANE), 1) == 0
    part_b[0, :, HALF:] = jnp.where(extra, choice_part, 0.0).astype(jnp.bfloat16)
    part_b[1, :, HALF:] = jnp.zeros((PAD, LANE), jnp.bfloat16)
    sum_grad.begin()
    fill(part_c, moe_part)
    near.finish()
    far.finish()
    first_p.wait_send()
    first_e.wait_send()
    for expert in range(EF):
        grad_in[expert] = round_half(contract_rows(normed_two, grad_pre_all[expert]))
    sum_grad.across()
    for expert in range(EF):
        gate = gates[:, 2 + expert : 3 + expert]
        grad_out[expert] = round_half(contract_rows(round_half(gate * cot), hidden_all[expert]))
    sum_grad.share()
    expand(1)
    far = reduce_rounds(1)
    far.advance()
    sum_moe.begin()
    sum_grad.done()
    choice = final_b[0, :, HALF : HALF + 1].astype(jnp.float32)
    grad_first = choice * gate_first * gate_second
    grad_logits = round_half(grad_first * sign)
    grad_normed_two = sum_grad.value() + contract_cols(grad_logits, small_half[...])
    grad_middle = cot + norm_pull(grad_normed_two, normal_two, inv_two, gain_two)
    far.advance()
    grad_gain_two = jnp.sum(grad_normed_two * normal_two, axis=0, keepdims=True)
    router_part = contract_rows(normed_two, grad_logits)
    grad_mid_half = round_half(grad_middle)
    grad_heads = round_half(rows_dot(grad_mid_half, attn_half[:, 512:768]))
    sum_moe.across()
    parts = [[], [], []]
    for head in range(3):
        grad_head = grad_heads[:, HEAD_DIM * (head + 1) : HEAD_DIM * (head + 2)]
        prob = prob_all[head]
        grad_prob = contract_cols(grad_head, head_of(qkv, 2, head))
        parts[2].append(round_half(contract_rows(round_half(prob), grad_head)))
        spread = jnp.sum(prob * grad_prob, axis=-1, keepdims=True)
        grad_scores = round_half(prob * (grad_prob - spread) * scale)
        parts[0].append(round_half(rows_dot(grad_scores, head_of(qkv, 1, head))))
        parts[1].append(round_half(contract_rows(grad_scores, head_of(qkv, 0, head))))
        if head > 0:
            far.advance()
    grad_qkv = jnp.concatenate(parts[0] + parts[1] + parts[2] + [blank] * 3, axis=1)
    first_part = contract_cols(grad_qkv, attn_half[...])
    fill(part_d, first_part)
    grad_attn[:, :512] = round_half(contract_rows(normed_one, grad_qkv[:, :512]))
    grad_attn[:, 512:] = round_half(
        contract_rows(normed_one, grad_qkv[:, 512:]) + contract_rows(grad_mid_half, attn_rows)
    )
    grad_gain_one = jnp.sum(first_part * normal_one, axis=0, keepdims=True)
    gain_id = lax.broadcasted_iota(jnp.int32, (LANE, WIDE), 0)
    gain_block = jnp.where(
        gain_id == 0, grad_gain_one, jnp.where(gain_id == 1, grad_gain_two, 0.0)
    )
    grad_small[...] = round_half(jnp.transpose(gain_block) + router_part)
    expand(0)
    near = reduce_rounds(0)
    near.advance()
    far.advance()
    sum_first.begin()
    near.advance()
    far.advance()
    sum_moe.share()
    near.advance()
    while far.turn < far.turns:
        far.advance()
    last_e = reduce_last(1)
    sum_first.across()
    sum_moe.done()
    output[0] = (middle + sum_moe.value())[:TOKENS]
    near.advance()
    near.advance()
    reduce_close(1, last_e)
    near.advance()
    while near.turn < near.turns:
        near.advance()
    last_p = reduce_last(0)
    sum_first.share()

    look[...] = jnp.zeros((BLOCKS, 16, HALF), jnp.bfloat16)

    def sum_cols(first_block, block_count):
        return jnp.concatenate(
            [sums[block_rows(first_block + block), :] for block in range(block_count)], axis=1
        )

    def look_of(gradient, moment):
        return round_half(gradient + MOMENTUM * (MOMENTUM * moment + gradient))

    for expert in range(EF):
        look[2 + EF + expert, 0:ROW, :] = look_of(sum_cols(16 + 3 * expert, 3), moment_out[expert])
        if expert > 0:
            look[2 + expert, 0:ROW, :] = look_of(sum_cols(7 + 3 * expert, 3), moment_in[expert])
    reduce_close(0, last_p)
    look[2, 0:ROW, :] = look_of(sum_cols(7, 3), moment_in[0])
    ahead = look_of(sum_cols(0, 6), flat_attn(moment_attn))
    look[0, 0:ROW, :] = ahead[:, :HALF]
    look[1, 0:ROW, :] = ahead[:, HALF:]

    shift = lax.rem(mine, 2) * 4
    own = lax.rem(me, PLANE) == shift
    my_block = me // PLANE
    devices = NZ * PLANE

    def owner_of(block):
        return block * PLANE + shift

    def outgoing(block):
        return pltpu.make_async_remote_copy(
            src_ref=look.at[block], dst_ref=arrived.at[me], send_sem=muon_send.at[block],
            recv_sem=muon_recv, device_id={"dp": owner_of(block)}, device_id_type=MESH_ID,
        )

    for block in range(BLOCKS):

        @pl.when(me != owner_of(block))
        def _():
            outgoing(block).start()

    small_land[mine] = sums[72:88, :]
    small_copies = []
    for away in (1, 2, 3):
        copy = pltpu.make_async_remote_copy(
            src_ref=small_land.at[mine], dst_ref=small_land.at[mine],
            send_sem=small_send.at[away], recv_sem=small_recv.at[away],
            device_id={"tensor": lax.rem(mine + away, 4)}, device_id_type=MESH_ID,
        )
        copy.start()
        small_copies.append(copy)
    sum_first.done()
    grad_normed_one = sum_first.value()
    grad_inputs[0] = (grad_middle + norm_pull(grad_normed_one, normal_one, inv_one, gain_one))[
        :TOKENS
    ]
    for copy in small_copies:
        copy.wait_recv()
    joint = small_land[0] + small_land[1] + small_land[2] + small_land[3]
    small_lane = lax.broadcasted_iota(jnp.int32, (16, LANE), 1)
    small_row = lax.broadcasted_iota(jnp.int32, (16, LANE), 0)
    total[...] = sums[...]
    total[72:88, :] = jnp.where((small_lane == 0) & (small_row < ROW), joint, sums[72:88, :])
    for copy in small_copies:
        copy.wait_send()

    @pl.when(own)
    def _():
        keep = pltpu.make_async_copy(look.at[my_block], arrived.at[me], local_sems.at[0])
        keep.start()
        keep.wait()
        pltpu.make_async_remote_copy(
            src_ref=arrived.at[pl.ds(0, devices - 1)], dst_ref=arrived.at[pl.ds(0, devices - 1)],
            send_sem=back_sem, recv_sem=muon_recv, device_id={"dp": me}, device_id_type=MESH_ID,
        ).wait_recv()

        def gathered(quad, carry):
            picked = arrived[pl.ds(quad * QUAD, QUAD)].reshape(QUAD * 16, HALF)
            rows = pl.ds(pl.multiple_of(quad * QUAD * ROW, 16), QUAD * ROW)
            matrix[rows, :] = round_half(rows_dot(one[...], picked))
            return carry

        lax.fori_loop(0, 2 * NZ, gathered, 0)
        joined = my_block >= 2
        mask = jnp.maximum(mask_ref[...], joined.astype(jnp.float32))
        raw = matrix[...].astype(jnp.float32)
        per_col = jnp.sum(raw * raw, axis=0, keepdims=True)
        square_sum = jnp.dot(
            jnp.broadcast_to(per_col, (8, HALF)), mask, preferred_element_type=jnp.float32,
            precision=lax.Precision.HIGHEST,
        )[0:1]
        matrix[...] = round_half(raw * lax.rsqrt(square_sum + EPSILON))
        for _ in range(NS_ITERS):
            current = matrix[...]
            gram_mat = round_half(contract_rows(current, current) * mask)
            square = rows_dot(gram_mat, gram_mat)
            gram[...] = round_half(NEWTON_B * gram_mat.astype(jnp.float32) + NEWTON_C * square)
            matrix[...] = round_half(
                NEWTON_A * current.astype(jnp.float32) + rows_dot(current, gram[...])
            )

        def scattered(quad, carry):
            rows = pl.ds(pl.multiple_of(quad * QUAD * ROW, 16), QUAD * ROW)
            finished[pl.ds(quad * QUAD, QUAD)] = round_half(
                rows_dot(one_back[...], matrix[rows, :])
            ).reshape(QUAD, 16, HALF)
            return carry

        lax.fori_loop(0, 2 * NZ, scattered, 0)

        def give(target, carry):
            @pl.when(target != me)
            def _():
                pltpu.make_async_remote_copy(
                    src_ref=finished.at[target], dst_ref=result.at[my_block], send_sem=back_sem,
                    recv_sem=ret_sems.at[my_block], device_id={"dp": target},
                    device_id_type=MESH_ID,
                ).start()

            return carry

        lax.fori_loop(0, devices, give, 0)
        stay = pltpu.make_async_copy(finished.at[me], result.at[my_block], local_sems.at[1])
        stay.start()
        stay.wait()
        pltpu.make_async_remote_copy(
            src_ref=finished.at[pl.ds(0, devices - 1)], dst_ref=finished.at[pl.ds(0, devices - 1)],
            send_sem=back_sem, recv_sem=muon_recv, device_id={"dp": me}, device_id_type=MESH_ID,
        ).wait_send()

    for block in range(BLOCKS):

        @pl.when(me != owner_of(block))
        def _():
            outgoing(block).wait_send()
            pltpu.make_async_remote_copy(
                src_ref=result.at[block], dst_ref=result.at[block], send_sem=muon_send.at[block],
                recv_sem=ret_sems.at[block], device_id={"dp": owner_of(block)},
                device_id_type=MESH_ID,
            ).wait_recv()

    near.finish()
    far.finish()
    last_p.wait_send()
    last_e.wait_send()
    for summing in (sum_attn, sum_grad, sum_moe, sum_first):
        summing.finish()


LAG = 3


def half_mask():
    side = np.arange(384) // 192
    return jnp.asarray(side[:, None] == side[None, :], jnp.float32)


def whole_step(inputs, cotangent, routes, gains, router, attn, mats_in, mats_out, moments):
    half, single = jnp.bfloat16, jnp.float32
    shapes = [(PAD, HALF), (PAD, HALF + LANE), (PAD, HALF), (PAD, HALF)]
    lands = []
    for _, rows_a, rows_b, _ in SETS:
        lands += [
            pltpu.VMEM((NX, 2, 4, NY, rows_a, LANE), half),
            pltpu.VMEM((NZ, 2, 2, NY, rows_b, LANE), half),
            pltpu.VMEM((1, 2, 2, NY, rows_a, LANE), half),
            pltpu.VMEM((1, 2, 4, NY, rows_b, LANE), half),
            pltpu.VMEM((rows_a + rows_b, LANE), half),
        ]
    weights = [(WIDE, WIDE), (WIDE, LANE), (EF, WIDE, HALF), (EF, WIDE, HALF)]
    dma = pltpu.SemaphoreType.DMA
    four, one = spread_matrix(4, 48), spread_matrix(1, 16)
    return pl.pallas_call(
        mega_kernel,
        out_shape=[
            jax.ShapeDtypeStruct((1, TOKENS, WIDE), single),
            jax.ShapeDtypeStruct((1, TOKENS, WIDE), single),
            jax.ShapeDtypeStruct((PACK, LANE), single),
            jax.ShapeDtypeStruct((BLOCKS, 16, HALF), half),
        ],
        in_specs=vmem_specs(16),
        out_specs=vmem_specs(4),
        scratch_shapes=[
            pltpu.VMEM((PACK, LANE), single),
            pltpu.VMEM((NZ, PLANE, PACK, LANE), half),
        ]
        + [pltpu.VMEM(shape, half) for shape in weights]
        + [
            pltpu.VMEM((PAD, WIDE), single),
            pltpu.VMEM((PAD, WIDE), single),
            pltpu.VMEM((3, PAD, PAD), single),
            pltpu.VMEM((EF, PAD, HALF), half),
            pltpu.VMEM((EF, PAD, HALF), half),
        ]
        + [pltpu.VMEM(shape, half) for shape in weights]
        + [pltpu.VMEM((PACK, LANE), single)]
        + lands
        + [pltpu.VMEM((2,) + shape, half) for shape in shapes]
        + [pltpu.VMEM(shape, half) for shape in shapes]
        + [pltpu.VMEM(shape, half) for shape in shapes]
        + [pltpu.VMEM((2,) + shape, half) for shape in shapes]
        + [
            pltpu.VMEM((4, 16, LANE), single),
            pltpu.VMEM((BLOCKS, 16, HALF), half),
            pltpu.VMEM((NZ * PLANE, 16, HALF), half),
            pltpu.VMEM((WIDE, HALF), half),
            pltpu.VMEM((NZ * PLANE, 16, HALF), half),
            pltpu.VMEM((HALF, HALF), half),
            dma((RING_SEMS,)), dma((RING_SEMS,)), dma((RING_SEMS,)), dma((RING_SEMS,)),
            dma((12,)), dma((12,)), dma((4,)), dma((4,)),
            dma((2,)), dma((BLOCKS,)), dma, dma, dma((BLOCKS,)),
        ],
        compiler_params=pltpu.CompilerParams(
            collective_id=0, has_side_effects=True, vmem_limit_bytes=64_000_000
        ),
    )(
        inputs, cotangent, routes, gains, router, attn, mats_in, mats_out, *moments,
        four, one, four.T, one.T, half_mask(),
    )


def shards(
    inputs,
    cotangent,
    norm_gains,
    attn_mats,
    router,
    expert_in,
    expert_out,
    moment_gains,
    moment_attn,
    moment_router,
    moment_in,
    moment_out,
    routes,
):
    def by_rows(value):
        return jnp.transpose(value, (1, 0, 2))

    output, grad_inputs, total, finished = whole_step(
        inputs, cotangent, routes, norm_gains, router.T, by_rows(attn_mats), expert_in, expert_out,
        (by_rows(moment_attn), moment_in, moment_out),
    )
    sum_attn, sum_small, sum_in, sum_out = unpack_rows(total)
    sum_gains = sum_small[:, :2].T
    sum_router = sum_small[:, 2:]
    small_step = SMALL_RATE / math.sqrt(lax.axis_size("dp") * TOKENS)
    moment_gains_new = MOMENTUM * moment_gains + sum_gains
    moment_attn_new = MOMENTUM * moment_attn + sum_attn
    moment_router_new = MOMENTUM * moment_router + sum_router
    moment_in_new = MOMENTUM * moment_in + sum_in
    moment_out_new = MOMENTUM * moment_out + sum_out
    gains_new = norm_gains - small_step * moment_gains_new
    router_new = router - small_step * moment_router_new
    updates = to_single(finished)[:, :ROW]
    update_attn = jnp.transpose(
        jnp.transpose(updates[0:2], (1, 0, 2)).reshape(ROW, 4, 192), (1, 0, 2)
    )
    attn_new = attn_mats - MUON_RATE * update_attn
    in_new = expert_in - MUON_RATE * updates[2 : EF + 2]
    out_new = expert_out - MUON_RATE * updates[EF + 2 : 2 * EF + 2]
    return (
        output,
        grad_inputs,
        sum_gains,
        sum_attn,
        sum_router,
        sum_in,
        sum_out,
        gains_new,
        attn_new,
        router_new,
        in_new,
        out_new,
        moment_gains_new,
        moment_attn_new,
        moment_router_new,
        moment_in_new,
        moment_out_new,
    )


def solution(mesh):
    return jax.shard_map(
        shards,
        mesh=mesh,
        in_specs=(
            P("dp", None, None),
            P("dp", None, None),
            P(None, "dp"),
            P(None, "dp", "tensor"),
            P("dp", None),
            P(None, "dp", "tensor"),
            P(None, "dp", "tensor"),
            P(None, "dp"),
            P(None, "dp", "tensor"),
            P("dp", None),
            P(None, "dp", "tensor"),
            P(None, "dp", "tensor"),
            P("dp", None, None),
        ),
        out_specs=(
            P("dp", None, None),
            P("dp", None, None),
            P(None, "dp"),
            P(None, "dp", "tensor"),
            P("dp", None),
            P(None, "dp", "tensor"),
            P(None, "dp", "tensor"),
            P(None, "dp"),
            P(None, "dp", "tensor"),
            P("dp", None),
            P(None, "dp", "tensor"),
            P(None, "dp", "tensor"),
            P(None, "dp"),
            P(None, "dp", "tensor"),
            P("dp", None),
            P(None, "dp", "tensor"),
            P(None, "dp", "tensor"),
        ),
        check_vma=False,
    )
```

time: 206 us -> 179 us (0.87)
  Pallas kernels: 185 us -> 159 us
  other arithmetic: 9.01 us -> 2.1 us
  local copies, waits for them, and re-layouts: 10.4 us -> 16.6 us
    pallas_call x4 -> x1, Pallas kernels: 185 us -> 159 us  [whole_step(): pl.pallas_call(mega_kernel, out_shape=[jax.ShapeDtypeStruct((1, TOKENS, W...]
    unnamed x52 -> x51, local copies, waits for them, and re-layouts: 8.06 us -> 15.3 us
    transpose x5 -> x0, other arithmetic: 4.02 us -> none  [the longest x1 0.99 us: pack_rows(): jnp.transpose(left, (1, 0, 2)).reshape(ROW, 1152)]
where the time goes in v5:
time: 179 us; the launch traced here: 178 us
  Pallas kernels  159 us (89%)
  local copies, waits for them, and re-layouts  16.6 us (9%)
  other arithmetic  2.1 us (1%)
    pallas_call x1, Pallas kernels, whole_step(): pl.pallas_call(mega_kernel, out_shape=[jax.ShapeDtypeStruct((1, TOKENS, W...  159 us
    unnamed x51, local copies, waits for them, and re-layouts  15.3 us

profile of v5, /device:TPU:94, one launch (start us, length us, event | category | flops | bytes accessed | tf_op | source)
XLA Modules:
  0.0 178.3 jit_solution(5297769836191356780)
XLA Ops:
  0.7 2.0 %copy.79.inputs = f32[1,197,768]{2,1,0:T(8,128)} copy(f32[1,197,768]{2,0,1:T(1,128)} %param.16) | data formatting | bytes 1210368 | tf_op args[0]
  2.7 0.9 copy.80.cotangent
  3.6 0.8 copy.81.routes
  4.3 158.8 %shard_map.287 = (f32[1,197,768]{2,1,0:T(8,128)}, f32[1,197,768]{2,1,0:T(8,128)}, f32[304,128]{1,0:T(8,128)}, bf16[8,16,384]{2,1,0:T(8,128)(2,1)}) custom-call(f32[1,197,768]{2,1,0:T(8,128)} %copy.79.inputs, f32[1,197,768]{2,1,0:T(8,128)} %copy.80.cotangent, s32[1,197,2]{2,1,0:T(8,128)} %copy.81.routes, f32[2,12]{1,0:T(2,128)} %gains.1, f32[3,12]{1,0:T(4,128)} %bitcast.32, ...), custom_call_target="tpu_custom_call" | custom-call | tf_op jit(solution)/shard_map/pallas_call | solution.py:915
  163.1 0.9 reshape.52
  164.1 0.1 copy.99
  164.4 0.8 copy-done.10
  165.3 0.1 mul.56
  165.4 0.6 copy-done.9
  166.0 0.7 bitcast_subtract_fusion
  166.8 0.8 copy-done.3
  167.7 0.6 copy.96
  168.3 0.9 copy-done.4
  169.2 0.6 copy.97
  169.9 0.6 copy.92
  170.5 0.6 copy.93
  171.4 0.7 copy.91
  172.1 0.7 copy.94
  172.8 0.7 copy.95
  173.5 0.6 copy-done.12
  174.1 0.6 multiply_subtract_fusion.1
  174.7 0.7 fusion
  175.4 1.4 copy.89
  176.8 1.4 copy.90
  (46 shorter events, 0.8 us)
Async XLA Ops:
  0.7 2.0 %copy-start.2 = (f32[1,197,768]{2,0,1:T(1,128)S(1)}, f32[1,197,768]{2,0,1:T(1,128)}, u32[]{:S(2)}) copy-start(f32[1,197,768]{2,0,1:T(1,128)} %param.17) | copy-start | bytes 1815556
  2.7 0.9 copy-start.14
  164.3 0.9 copy-start.10
  164.4 1.0 copy-start.7
  165.2 0.8 copy-start.9
  165.2 0.8 copy-start.8
  166.7 0.9 copy-start.3
  168.3 0.9 copy-start.4
  169.2 6.2 %copy-start.1 = (f32[1,197,768]{2,1,0:T(8,128)S(1)}, f32[1,197,768]{2,1,0:T(8,128)}, u32[]{:S(2)}) copy-start(f32[1,197,768]{2,1,0:T(8,128)} %get-tuple-element.76) | copy-start | bytes 1815556
  169.9 1.3 copy-start.15
  169.9 1.4 copy-start.11
  170.5 4.2 %copy-start.6 = (f32[3,12,384]{2,1,0:T(8,128)S(1)}, f32[3,12,384]{2,1,0:T(8,128)}, u32[]{:S(2)}) copy-start(f32[3,12,384]{2,1,0:T(8,128)} %mats_out.1) | copy-start | bytes 165892
  171.2 3.5 %copy-start.5 = (f32[3,12,384]{2,1,0:T(8,128)S(1)}, f32[3,12,384]{2,1,0:T(8,128)}, u32[]{:S(2)}) copy-start(f32[3,12,384]{2,1,0:T(8,128)} %mats_in.1) | copy-start | bytes 165892
  173.4 0.7 copy-start.12
  173.4 0.7 copy-start.16
  174.1 0.6 copy-start.13
  175.4 1.5 copy-start

commit v6 on v5

--- a/solution.py
+++ b/solution.py
@@ -135,15 +135,6 @@
 
 def vmem_specs(count):
     return [pl.BlockSpec(memory_space=pltpu.VMEM)] * count
-
-
-def unpack_rows(rows):
-    flat = jnp.transpose(rows[: 25 * ROW].reshape(25, ROW, LANE), (1, 0, 2)).reshape(ROW, 25 * LANE)
-    attn = jnp.transpose(flat[:, :768].reshape(ROW, 4, 192), (1, 0, 2))
-    small = flat[:, 768:773]
-    left = jnp.transpose(flat[:, 896:2048].reshape(ROW, EF, 384), (1, 0, 2))
-    right = jnp.transpose(flat[:, 2048:3200].reshape(ROW, EF, 384), (1, 0, 2))
-    return attn, small, left, right
 
 
 class ReduceRing:
@@ -326,7 +317,7 @@
     moment_attn, moment_in, moment_out, four, one, four_back, one_back, mask_ref,
     output, grad_inputs, total, result,
     packed, slots, attn_half, small_half, in_half, out_half,
-    rows_in, rows_cot, prob_all, hidden_all, grad_pre_all,
+    raw_in, raw_cot, rows_in, rows_cot, prob_all, hidden_all, grad_pre_all,
     grad_attn, grad_small, grad_in, grad_out, sums,
     land_az_p, land_bx_p, land_ax_p, land_bz_p, land_y_p,
     land_az_e, land_bx_e, land_ax_e, land_bz_e, land_y_e,
@@ -340,6 +331,11 @@
     mine = lax.axis_index("tensor")
     z, x, y = place_of(me)
     up_z, down_z, up_x, down_x, other_y = neighbours(me)
+    loads = []
+    for index, (source, held) in enumerate(((inputs, raw_in), (cotangent, raw_cot))):
+        copy = pltpu.make_async_copy(source.at[:, 0, :], held, local_sems.at[2 + index])
+        copy.start()
+        loads.append(copy)
     barrier = pltpu.get_barrier_semaphore()
     for target in (up_z, down_z, up_x, down_x, other_y):
         pl.semaphore_signal(barrier, inc=1, device_id={"dp": target}, device_id_type=MESH_ID)
@@ -561,9 +557,10 @@
 
     first_p, first_e = gather_first(0), gather_first(1)
     near, far = gather_rounds(0), gather_rounds(1)
-    for source, held in ((inputs, rows_in), (cotangent, rows_cot)):
+    for copy, raw, held in zip(loads, (raw_in, raw_cot), (rows_in, rows_cot)):
+        copy.wait()
         held[PAD - 16 : PAD, :] = jnp.zeros((16, WIDE), jnp.float32)
-        held[0:TOKENS, :] = source[0]
+        held[0:TOKENS, :] = raw[...]
     row_in = rows_in[...]
     normal_one, inv_one = norm_parts(row_in)
     first_p.wait_recv()
@@ -625,13 +622,14 @@
     normed_two = round_half(normal_two * gain_two)
     compact(1)
     logits = rows_dot(normed_two, small_half[...])
-    lane_id = lax.broadcasted_iota(jnp.int32, (TOKENS, LANE), 1) - 2
-    picks = routes[0]
-    gap = jnp.zeros((PAD - TOKENS, LANE), jnp.float32)
+    expert_id = lax.broadcasted_iota(jnp.int32, (16, TOKENS), 0)
+    lane_id = lax.broadcasted_iota(jnp.int32, (16, LANE), 1) - 2
+    spread = (lane_id == lax.broadcasted_iota(jnp.int32, (16, LANE), 0)).astype(jnp.bfloat16)
+    gap = jnp.zeros((16, PAD - TOKENS), jnp.float32)
 
     def chosen_mask(which):
-        hit = (lane_id == picks[:, which : which + 1]).astype(jnp.float32)
-        return jnp.concatenate([hit, gap], axis=0)
+        hit = (expert_id == routes[which : which + 1, :]).astype(jnp.float32)
+        return contract_rows(round_half(jnp.concatenate([hit, gap], axis=1)), spread)
 
     hot_first, hot_second = chosen_mask(0), chosen_mask(1)
     sign = hot_first - hot_second
@@ -920,7 +918,7 @@
             jax.ShapeDtypeStruct((PACK, LANE), single),
             jax.ShapeDtypeStruct((BLOCKS, 16, HALF), half),
         ],
-        in_specs=vmem_specs(16),
+        in_specs=[pl.BlockSpec(memory_space=pl.ANY)] * 2 + vmem_specs(14),
         out_specs=vmem_specs(4),
         scratch_shapes=[
             pltpu.VMEM((PACK, LANE), single),
@@ -928,6 +926,8 @@
         ]
         + [pltpu.VMEM(shape, half) for shape in weights]
         + [
+            pltpu.VMEM((TOKENS, WIDE), single),
+            pltpu.VMEM((TOKENS, WIDE), single),
             pltpu.VMEM((PAD, WIDE), single),
             pltpu.VMEM((PAD, WIDE), single),
             pltpu.VMEM((3, PAD, PAD), single),
@@ -950,7 +950,7 @@
             pltpu.VMEM((HALF, HALF), half),
             dma((RING_SEMS,)), dma((RING_SEMS,)), dma((RING_SEMS,)), dma((RING_SEMS,)),
             dma((12,)), dma((12,)), dma((4,)), dma((4,)),
-            dma((2,)), dma((BLOCKS,)), dma, dma, dma((BLOCKS,)),
+            dma((4,)), dma((BLOCKS,)), dma, dma, dma((BLOCKS,)),
         ],
         compiler_params=pltpu.CompilerParams(
             collective_id=0, has_side_effects=True, vmem_limit_bytes=64_000_000
@@ -959,6 +959,88 @@
         inputs, cotangent, routes, gains, router, attn, mats_in, mats_out, *moments,
         four, one, four.T, one.T, half_mask(),
     )
+
+
+def finish_kernel(
+    total, result, rows_out, rows_grad, gains, router, attn, mats_in, mats_out,
+    moment_gains, moment_router, moment_attn, moment_in, moment_out,
+    output, grad_inputs, sum_gains, sum_attn, sum_router, sum_in, sum_out,
+    gains_new, attn_new, router_new, in_new, out_new,
+    gains_moved, attn_moved, router_moved, in_moved, out_moved, sems,
+):
+    copies = [
+        pltpu.make_async_copy(source.at[0], landing.at[:, 0, :], sems.at[index])
+        for index, (source, landing) in enumerate(((rows_out, output), (rows_grad, grad_inputs)))
+    ]
+    for copy in copies:
+        copy.start()
+    small_step = SMALL_RATE / math.sqrt(NZ * PLANE * TOKENS)
+
+    def columns(first_block, block_count):
+        return jnp.concatenate(
+            [
+                total[(first_block + block) * ROW : (first_block + block + 1) * ROW, :]
+                for block in range(block_count)
+            ],
+            axis=1,
+        )
+
+    diagonal = lax.broadcasted_iota(jnp.int32, (ROW, ROW), 0) == lax.broadcasted_iota(
+        jnp.int32, (ROW, ROW), 1
+    )
+    small = columns(6, 1)
+    small_sets = (
+        (0, 2, gains, moment_gains, sum_gains, gains_new, gains_moved),
+        (2, EF, router, moment_router, sum_router, router_new, router_moved),
+    )
+    for first_lane, count, param, moment, gradient, new, moved in small_sets:
+        for index in range(count):
+            lane = first_lane + index
+            row = slice(index, index + 1)
+            value = jnp.sum(
+                jnp.where(diagonal, small[:, lane : lane + 1], 0.0), axis=0, keepdims=True
+            )
+            gradient[row, :] = value
+            fresh = MOMENTUM * moment[row, :] + value
+            moved[row, :] = fresh
+            new[row, :] = param[row, :] - small_step * fresh
+    flat = columns(0, 6)
+    step = jnp.concatenate([result[0, 0:ROW, :], result[1, 0:ROW, :]], axis=1).astype(jnp.float32)
+    for which in range(4):
+        wide = slice(which * 192, (which + 1) * 192)
+        sum_attn[:, which, :] = flat[:, wide]
+        attn_moved[:, which, :] = MOMENTUM * moment_attn[:, which, :] + flat[:, wide]
+        attn_new[:, which, :] = attn[:, which, :] - MUON_RATE * step[:, wide]
+    for first_block, first_slot, param, moment, gradient, new, moved in (
+        (7, 2, mats_in, moment_in, sum_in, in_new, in_moved),
+        (16, 2 + EF, mats_out, moment_out, sum_out, out_new, out_moved),
+    ):
+        for expert in range(EF):
+            value = columns(first_block + 3 * expert, 3)
+            gradient[expert] = value
+            moved[expert] = MOMENTUM * moment[expert] + value
+            new[expert] = param[expert] - MUON_RATE * result[
+                first_slot + expert, 0:ROW, :
+            ].astype(jnp.float32)
+    for copy in copies:
+        copy.wait()
+
+
+def finish_step(total, result, rows_out, rows_grad, params, moments):
+    single = jnp.float32
+    rows = jax.ShapeDtypeStruct((TOKENS, 1, WIDE), single)
+    group = [
+        jax.ShapeDtypeStruct(shape, single)
+        for shape in ((2, ROW), (ROW, 4, 192), (EF, ROW), (EF, ROW, HALF), (EF, ROW, HALF))
+    ]
+    anywhere = pl.BlockSpec(memory_space=pl.ANY)
+    return pl.pallas_call(
+        finish_kernel,
+        out_shape=[rows, rows] + group * 3,
+        in_specs=vmem_specs(14),
+        out_specs=[anywhere, anywhere] + vmem_specs(15),
+        scratch_shapes=[pltpu.SemaphoreType.DMA((2,))],
+    )(total, result, rows_out, rows_grad, *params, *moments)
 
 
 def shards(
@@ -979,47 +1061,18 @@
     def by_rows(value):
         return jnp.transpose(value, (1, 0, 2))
 
-    output, grad_inputs, total, finished = whole_step(
-        inputs, cotangent, routes, norm_gains, router.T, by_rows(attn_mats), expert_in, expert_out,
-        (by_rows(moment_attn), moment_in, moment_out),
-    )
-    sum_attn, sum_small, sum_in, sum_out = unpack_rows(total)
-    sum_gains = sum_small[:, :2].T
-    sum_router = sum_small[:, 2:]
-    small_step = SMALL_RATE / math.sqrt(lax.axis_size("dp") * TOKENS)
-    moment_gains_new = MOMENTUM * moment_gains + sum_gains
-    moment_attn_new = MOMENTUM * moment_attn + sum_attn
-    moment_router_new = MOMENTUM * moment_router + sum_router
-    moment_in_new = MOMENTUM * moment_in + sum_in
-    moment_out_new = MOMENTUM * moment_out + sum_out
-    gains_new = norm_gains - small_step * moment_gains_new
-    router_new = router - small_step * moment_router_new
-    updates = to_single(finished)[:, :ROW]
-    update_attn = jnp.transpose(
-        jnp.transpose(updates[0:2], (1, 0, 2)).reshape(ROW, 4, 192), (1, 0, 2)
-    )
-    attn_new = attn_mats - MUON_RATE * update_attn
-    in_new = expert_in - MUON_RATE * updates[2 : EF + 2]
-    out_new = expert_out - MUON_RATE * updates[EF + 2 : 2 * EF + 2]
-    return (
-        output,
-        grad_inputs,
-        sum_gains,
-        sum_attn,
-        sum_router,
-        sum_in,
-        sum_out,
-        gains_new,
-        attn_new,
-        router_new,
-        in_new,
-        out_new,
-        moment_gains_new,
-        moment_attn_new,
-        moment_router_new,
-        moment_in_new,
-        moment_out_new,
-    )
+    params = (norm_gains, router.T, by_rows(attn_mats), expert_in, expert_out)
+    moments = (moment_gains, moment_router.T, by_rows(moment_attn), moment_in, moment_out)
+    rows_out, rows_grad, total, finished = whole_step(
+        by_rows(inputs), by_rows(cotangent), routes[0].T, *params, moments[2:]
+    )
+    rows = finish_step(total, finished, rows_out, rows_grad, params, moments)
+    output, grad_inputs = (by_rows(value) for value in rows[:2])
+    groups = []
+    for first in (2, 7, 12):
+        gains, attn, router_rows, left, right = rows[first : first + 5]
+        groups += [gains, by_rows(attn), router_rows.T, left, right]
+    return (output, grad_inputs, *groups)
 
 
 def solution(mesh):

time: 179 us -> 163 us (0.911)
  local copies, waits for them, and re-layouts: 16.6 us -> 0 us
  Pallas kernels: 159 us -> 162 us
  other arithmetic: 2.1 us -> 0 us
    unnamed x51 -> x0, local copies, waits for them, and re-layouts: 15.3 us -> none
    pallas_call x0 -> x1, Pallas kernels: none -> 3.44 us  [finish_step(): pl.pallas_call(finish_kernel, out_shape=[rows, rows] + group * 3, in_spec...]
    sub x4 -> x0, other arithmetic: 2 us -> none  [the longest x1 0.68 us: shards(): out_new = expert_out - MUON_RATE * updates[EF + 2:2 * EF + 2]]
where the time goes in v6:
time: 163 us
  Pallas kernels  162 us (99%)
    pallas_call x1, Pallas kernels, whole_step(): pl.pallas_call(mega_kernel, out_shape=[jax.ShapeDtypeStruct((1, TOKENS, W...  159 us
    pallas_call x1, Pallas kernels, finish_step(): pl.pallas_call(finish_kernel, out_shape=[rows, rows] + group * 3, in_spec...  3.44 us

profile of v6, /device:TPU:94, one launch (start us, length us, event | category | flops | bytes accessed | tf_op | source)
XLA Modules:
  0.0 163.1 jit_solution(2842207762287654689)
XLA Ops:
  0.7 158.9 %shard_map.287 = (f32[1,197,768]{2,1,0:T(8,128)}, f32[1,197,768]{2,1,0:T(8,128)}, f32[304,128]{1,0:T(8,128)}, bf16[8,16,384]{2,1,0:T(8,128)(2,1)}) custom-call(f32[197,1,768]{2,1,0:T(1,128)} %bitcast.17, f32[197,1,768]{2,1,0:T(1,128)} %bitcast.18, s32[2,197]{1,0:T(2,128)} %bitcast.25, f32[2,12]{1,0:T(2,128)} %gains.3, f32[3,12]{1,0:T(4,128)} %bitcast.23, ...), custom_call_target="tpu_custom_call" | custom-call | tf_op jit(solution)/shard_map/pallas_call | solution.py:913
  159.5 3.4 %shard_map.288 = (f32[197,1,768]{2,1,0:T(1,128)}, f32[197,1,768]{2,1,0:T(1,128)}, f32[2,12]{1,0:T(2,128)}, f32[12,4,192]{2,1,0:T(4,128)}, f32[3,12]{1,0:T(4,128)...) custom-call(f32[304,128]{1,0:T(8,128)} %get-tuple-element.38.total, ...), custom_call_target="tpu_custom_call" | custom-call | tf_op jit(solution)/shard_map/pallas_call | solution.py:1037

commit v7 on v6

--- a/solution.py
+++ b/solution.py
@@ -700,7 +700,7 @@
         grad_scores = round_half(prob * (grad_prob - spread) * scale)
         parts[0].append(round_half(rows_dot(grad_scores, head_of(qkv, 1, head))))
         parts[1].append(round_half(contract_rows(grad_scores, head_of(qkv, 0, head))))
-        if head > 0:
+        if head == 2:
             far.advance()
     grad_qkv = jnp.concatenate(parts[0] + parts[1] + parts[2] + [blank] * 3, axis=1)
     first_part = contract_cols(grad_qkv, attn_half[...])
@@ -718,26 +718,22 @@
     expand(0)
     near = reduce_rounds(0)
     near.advance()
-    far.advance()
     sum_first.begin()
-    near.advance()
-    far.advance()
     sum_moe.share()
-    near.advance()
+    while near.turn < near.turns:
+        near.advance()
+        if far.turn < far.turns:
+            far.advance()
+        if near.turn == 3:
+            sum_first.across()
     while far.turn < far.turns:
         far.advance()
+    last_p = reduce_last(0)
     last_e = reduce_last(1)
-    sum_first.across()
+    sum_first.share()
     sum_moe.done()
     output[0] = (middle + sum_moe.value())[:TOKENS]
-    near.advance()
-    near.advance()
     reduce_close(1, last_e)
-    near.advance()
-    while near.turn < near.turns:
-        near.advance()
-    last_p = reduce_last(0)
-    sum_first.share()
 
     look[...] = jnp.zeros((BLOCKS, 16, HALF), jnp.bfloat16)
 
@@ -753,27 +749,33 @@
         look[2 + EF + expert, 0:ROW, :] = look_of(sum_cols(16 + 3 * expert, 3), moment_out[expert])
         if expert > 0:
             look[2 + expert, 0:ROW, :] = look_of(sum_cols(7 + 3 * expert, 3), moment_in[expert])
+    shift = lax.rem(mine, 2) * 4
+    own = lax.rem(me, PLANE) == shift
+    my_block = me // PLANE
+    devices = NZ * PLANE
+
+    def owner_of(block):
+        return block * PLANE + shift
+
+    def outgoing(block):
+        return pltpu.make_async_remote_copy(
+            src_ref=look.at[block], dst_ref=arrived.at[me], send_sem=muon_send.at[block],
+            recv_sem=muon_recv, device_id={"dp": owner_of(block)}, device_id_type=MESH_ID,
+        )
+
+    for block in range(3, BLOCKS):
+
+        @pl.when(me != owner_of(block))
+        def _():
+            outgoing(block).start()
+
     reduce_close(0, last_p)
     look[2, 0:ROW, :] = look_of(sum_cols(7, 3), moment_in[0])
     ahead = look_of(sum_cols(0, 6), flat_attn(moment_attn))
     look[0, 0:ROW, :] = ahead[:, :HALF]
     look[1, 0:ROW, :] = ahead[:, HALF:]
 
-    shift = lax.rem(mine, 2) * 4
-    own = lax.rem(me, PLANE) == shift
-    my_block = me // PLANE
-    devices = NZ * PLANE
-
-    def owner_of(block):
-        return block * PLANE + shift
-
-    def outgoing(block):
-        return pltpu.make_async_remote_copy(
-            src_ref=look.at[block], dst_ref=arrived.at[me], send_sem=muon_send.at[block],
-            recv_sem=muon_recv, device_id={"dp": owner_of(block)}, device_id_type=MESH_ID,
-        )
-
-    for block in range(BLOCKS):
+    for block in range(3):
 
         @pl.when(me != owner_of(block))
         def _():

time: 163 us -> 158 us (0.969)
  Pallas kernels: 162 us -> 157 us
    pallas_call x1, Pallas kernels: 159 us -> 153 us  [whole_step(): pl.pallas_call(mega_kernel, out_shape=[jax.ShapeDtypeStruct((1, TOKENS, W...]
where the time goes in v7:
time: 158 us
  Pallas kernels  157 us (99%)
    pallas_call x1, Pallas kernels, whole_step(): pl.pallas_call(mega_kernel, out_shape=[jax.ShapeDtypeStruct((1, TOKENS, W...  153 us
    pallas_call x1, Pallas kernels, finish_step(): pl.pallas_call(finish_kernel, out_shape=[rows, rows] + group * 3, in_spec...  3.44 us

profile of v7, /device:TPU:94, one launch (start us, length us, event | category | flops | bytes accessed | tf_op | source)
XLA Modules:
  0.0 157.7 jit_solution(1365166889908627176)
XLA Ops:
  0.7 153.4 %shard_map.287 = (f32[1,197,768]{2,1,0:T(8,128)}, f32[1,197,768]{2,1,0:T(8,128)}, f32[304,128]{1,0:T(8,128)}, bf16[8,16,384]{2,1,0:T(8,128)(2,1)}) custom-call(f32[197,1,768]{2,1,0:T(1,128)} %bitcast.17, f32[197,1,768]{2,1,0:T(1,128)} %bitcast.18, s32[2,197]{1,0:T(2,128)} %bitcast.25, f32[2,12]{1,0:T(2,128)} %gains.3, f32[3,12]{1,0:T(4,128)} %bitcast.23, ...), custom_call_target="tpu_custom_call" | custom-call | tf_op jit(solution)/shard_map/pallas_call | solution.py:915
  154.1 3.4 %shard_map.288 = (f32[197,1,768]{2,1,0:T(1,128)}, f32[197,1,768]{2,1,0:T(1,128)}, f32[2,12]{1,0:T(2,128)}, f32[12,4,192]{2,1,0:T(4,128)}, f32[3,12]{1,0:T(4,128)...) custom-call(f32[304,128]{1,0:T(8,128)} %get-tuple-element.38.total, ...), custom_call_target="tpu_custom_call" | custom-call | tf_op jit(solution)/shard_map/pallas_call | solution.py:1039
